TPU v7x, 32 devices: a whole 2x2x4 slice. The times are simulated.
32 devices in a mesh: tm: 4 (over x, core), space: 8 (over z, y).
Axes of the slice: x: 2, y: 2, z: 4, core: 2. Of those that a mesh axis runs over, the one named last changes fastest.
Arguments:
- states: float32 [8, 3, 32, 128, 128], P('tm', None, 'space'), may hold values from -6 to 6
- sources: float32 [8, 3, 32, 128, 128], P('tm', None, 'space'), may hold values from -6 to 6
- conductivity: float32 [32, 128, 128], P('space'), may hold values from 0.5 to 4
- gap_tile: int32 [8, 1024, 1], P('tm', 'space'), may hold values from 0 to 7; in each aligned block of 128 rows (0 to 127, 128 to 255, ..., all dimensions but the last counted through in order) at most 32 rows name the same one
- gap_row: int32 [8, 1024], P('tm', 'space'), may hold values from 0 to 127
Outputs:
- new_states: float32 [8, 3, 32, 128, 128], P('tm', None, 'space')
Inputs may be any that keep to these rules, and one draw needn't show every extreme that they name: `gap_tile`: in each slice no tile maps more than 32 of its own 128 interface rows to any one tile.
All inputs are finite; a program needn't handle non-finite values.
Results may differ from a plain program's by a relative error of at most 0.0001.
Values sent between devices are 32-bit elements; how exact they have to be, the bound alone decides.
No kernel may reach another device: no remote copies, remote signals or barrier semaphores. Data moves between devices by JAX's collectives and lax.ppermute only.
A program may use at most 128 MiB of HBM per device.

v0:
```python
import jax
import jax.numpy as jnp
from jax import lax
from jax.sharding import PartitionSpec as P

STEPS = 4
SWEEPS = 3
COARSE_SWEEPS = 3


inverse_step = 2.0
gap_gain = 1.0


def padded_2(cells, sides, width):
    for axis, dim in sides:
        count = lax.axis_size(axis)
        ends = count - 1
        head = lax.slice_in_dim(cells, 0, width, axis=dim)
        tail = lax.slice_in_dim(cells, cells.shape[dim] - width, cells.shape[dim], axis=dim)
        cells = jnp.concatenate(
            [
                lax.ppermute(tail, axis, [(i, (i + 1) % count) for i in range(ends)]),
                cells,
                lax.ppermute(head, axis, [((i + 1) % count, i) for i in range(ends)]),
            ],
            axis=dim,
        )
    return cells


def passed_along(value, axis, steps):
    count = lax.axis_size(axis)
    pairs = [(source, (source + steps) % count) for source in range(count)]
    return lax.ppermute(value, axis, pairs)


def passed_along_2(value, axis, steps):
    count = lax.axis_size(axis)
    first, last = (max(0, -steps), min(count, count - steps))
    return lax.ppermute(value, axis, [(source, source + steps) for source in range(first, last)])


def neighbours(field):
    wide = padded_2(field, (("space", 2),), 1)
    padded = jnp.pad(wide, ((0, 0), (0, 0), (0, 0), (1, 1), (1, 1)))
    total = padded[:, :, 2:, 1:-1, 1:-1] + padded[:, :, :-2, 1:-1, 1:-1]
    total = total + padded[:, :, 1:-1, 2:, 1:-1] + padded[:, :, 1:-1, :-2, 1:-1]
    total = total + padded[:, :, 1:-1, 1:-1, 2:] + padded[:, :, 1:-1, 1:-1, :-2]
    return total


def jacobi(field, rhs, diag, sweeps):
    for sweep in range(sweeps):
        field = (rhs + neighbours(field)) / diag
    return field


def shards(states, sources, conductivity, gap_tile, gap_row):
    tiles_count = lax.axis_size("space")
    rows_count = states.shape[3]
    conduct = conductivity[None, None]
    tiles = gap_tile[:, :, 0]
    row_ids = jnp.arange(rows_count, dtype=jnp.int32)
    capacity = max(2, 2 * rows_count // tiles_count)
    tile_hot = (
        tiles[:, :, None] == jnp.arange(tiles_count, dtype=jnp.int32)[None, None, :]
    ).astype(jnp.int32)
    before = jnp.cumsum(tile_hot, axis=1) - tile_hot
    position = jnp.sum(before * tile_hot, axis=2)
    target = jnp.arange(tiles_count * capacity, dtype=jnp.int32)
    select_int = (
        (tiles[:, None, :] == (target // capacity)[None, :, None])
        & (position[:, None, :] == (target % capacity)[None, :, None])
    ).astype(jnp.int32)
    select = select_int.astype(jnp.float32)
    slot_dest = jnp.sum(select_int * (gap_row + 1)[:, None, :], axis=2)
    slot_dest = slot_dest.reshape(slot_dest.shape[0], tiles_count, capacity)
    got_dest = lax.all_to_all(slot_dest, "space", split_axis=1, concat_axis=1, tiled=True)
    got_dest = got_dest.reshape(got_dest.shape[0], tiles_count * capacity)
    receive = (got_dest[:, None, :] == (row_ids + 1)[None, :, None]).astype(jnp.float32)
    rate = inverse_step * conduct

    def coarse(field, first, last):
        coarse_rate = inverse_step * conduct / STEPS
        return jacobi(
            field, coarse_rate * field + sources[first:last], coarse_rate + 6.0, COARSE_SWEEPS
        )

    field = states
    for step in range(STEPS):
        packed = jnp.einsum("sjy,syz->sjz", select, field[:, 0, 0], precision=lax.Precision.HIGHEST)
        packed = packed.reshape(packed.shape[0], tiles_count, capacity, packed.shape[2])
        arrived = lax.all_to_all(packed, "space", split_axis=1, concat_axis=1, tiled=True)
        arrived = arrived.reshape(arrived.shape[0], tiles_count * capacity, arrived.shape[3])
        coupled = jnp.einsum("syj,sjz->syz", receive, arrived, precision=lax.Precision.HIGHEST)
        rhs = rate * field + sources
        rhs = rhs.at[:, 0, 0].add(gap_gain * coupled)
        field = jacobi(field, rhs, rate + 6.0, SWEEPS)
    coarse_old = coarse(states, 0, states.shape[0])
    jumps = field - coarse_old
    fine_before = passed_along(field[-1:], "tm", 1)
    incoming = fine_before
    position_tm = lax.axis_index("tm")
    for rounds in range(lax.axis_size("tm") - 1):
        second = coarse(incoming, 0, 1) + jumps[0:1]
        onward = coarse(second, 1, 2) - coarse_old[1:2]
        arrived_state = passed_along_2(onward, "tm", 1)
        incoming = jnp.where(position_tm == rounds + 1, arrived_state + fine_before, incoming)
    second = coarse(incoming, 0, 1) + jumps[0:1]
    return jnp.concatenate([incoming, second], axis=0)


def solution(mesh):
    placed = (
        P("tm", None, "space", None, None),
        P("tm", None, "space", None, None),
        P("space", None, None),
        P("tm", "space", None),
        P("tm", "space"),
    )
    return jax.shard_map(
        shards,
        mesh=mesh,
        in_specs=placed,
        out_specs=P("tm", None, "space", None, None),
        check_vma=False,
    )
```

profile of v0, /device:TPU:10, one launch (start us, length us, event | category | flops | bytes accessed | tf_op | source)
XLA Modules:
  0.0 783.6 jit_solution(11947535838422965737)
XLA Ops:
  14.9 6.2 all-to-all-start
  26.9 6.2 all-to-all-start.1
  42.5 6.8 add_divide_fusion.1
  55.3 13.3 %collective-permute-done.2 = f32[2,3,1,128,128]{4,3,0,2,1:T(8,128)S(1)} collective-permute-done((f32[2,3,1,128,128]{4,3,0,2,1:T(8,128)S(1)}, f32[2,3,1,128,128]{4,3,0,2,1:T(8,128)S(1)}, u32[]{:S(2)}, u32[]{:S(2)}) %collective-permute-start.2) | collective-permute-done | bytes 393248 | tf_op jit(solution)/shard_map/ppermute | solution.py:25
  78.9 14.9 %collective-permute-done.4 = f32[2,3,1,128,128]{4,3,0,2,1:T(8,128)S(1)} collective-permute-done((f32[2,3,1,128,128]{4,3,0,2,1:T(8,128)S(1)}, f32[2,3,1,128,128]{4,3,0,2,1:T(8,128)S(1)}, u32[]{:S(2)}, u32[]{:S(2)}) %collective-permute-start.4) | collective-permute-done | bytes 393248 | tf_op jit(solution)/shard_map/ppermute | solution.py:25
  100.7 5.0 collective-permute-start.6
  108.9 5.3 all-to-all-start.2
  114.2 11.3 %collective-permute-done.6 = f32[2,3,1,128,128]{4,3,0,2,1:T(8,128)S(1)} collective-permute-done((f32[2,3,1,128,128]{4,3,0,2,1:T(8,128)}, f32[2,3,1,128,128]{4,3,0,2,1:T(8,128)S(1)}, u32[]{:S(2)}, u32[]{:S(2)}) %collective-permute-start.6) | collective-permute-done | bytes 393248 | tf_op jit(solution)/shard_map/ppermute | solution.py:25
  133.1 7.1 fusion.37
  140.3 4.9 collective-permute-start.8
  147.3 14.9 %collective-permute-done.8 = f32[2,3,1,128,128]{4,3,0,2,1:T(8,128)S(1)} collective-permute-done((f32[2,3,1,128,128]{4,3,0,2,1:T(8,128)S(1)}, f32[2,3,1,128,128]{4,3,0,2,1:T(8,128)S(1)}, u32[]{:S(2)}, u32[]{:S(2)}) %collective-permute-start.8) | collective-permute-done | bytes 393248 | tf_op jit(solution)/shard_map/ppermute | solution.py:25
  166.0 5.0 collective-permute-start.10
  173.1 15.0 %collective-permute-done.10 = f32[2,3,1,128,128]{4,3,0,2,1:T(8,128)S(1)} collective-permute-done((f32[2,3,1,128,128]{4,3,0,2,1:T(8,128)S(1)}, f32[2,3,1,128,128]{4,3,0,2,1:T(8,128)S(1)}, u32[]{:S(2)}, u32[]{:S(2)}) %collective-permute-start.10) | collective-permute-done | bytes 393248 | tf_op jit(solution)/shard_map/ppermute | solution.py:25
  198.3 5.0 collective-permute-start.12
  207.3 5.5 all-to-all-start.3
  212.8 10.3 %collective-permute-done.12 = f32[2,3,1,128,128]{4,3,0,2,1:T(8,128)S(1)} collective-permute-done((f32[2,3,1,128,128]{4,3,0,2,1:T(8,128)}, f32[2,3,1,128,128]{4,3,0,2,1:T(8,128)S(1)}, u32[]{:S(2)}, u32[]{:S(2)}) %collective-permute-start.12) | collective-permute-done | bytes 393248 | tf_op jit(solution)/shard_map/ppermute | solution.py:25
  230.6 7.1 fusion.28
  237.8 4.9 collective-permute-start.14
  244.8 14.9 %collective-permute-done.14 = f32[2,3,1,128,128]{4,3,0,2,1:T(8,128)S(1)} collective-permute-done((f32[2,3,1,128,128]{4,3,0,2,1:T(8,128)S(1)}, f32[2,3,1,128,128]{4,3,0,2,1:T(8,128)S(1)}, u32[]{:S(2)}, u32[]{:S(2)}) %collective-permute-start.14) | collective-permute-done | bytes 393248 | tf_op jit(solution)/shard_map/ppermute | solution.py:25
  263.5 5.0 collective-permute-start.16
  270.6 15.0 %collective-permute-done.16 = f32[2,3,1,128,128]{4,3,0,2,1:T(8,128)S(1)} collective-permute-done((f32[2,3,1,128,128]{4,3,0,2,1:T(8,128)S(1)}, f32[2,3,1,128,128]{4,3,0,2,1:T(8,128)S(1)}, u32[]{:S(2)}, u32[]{:S(2)}) %collective-permute-start.16) | collective-permute-done | bytes 393248 | tf_op jit(solution)/shard_map/ppermute | solution.py:25
  295.8 5.0 collective-permute-start.18
  304.8 5.0 all-to-all-start.4
  309.8 10.7 %collective-permute-done.18 = f32[2,3,1,128,128]{4,3,0,2,1:T(8,128)S(1)} collective-permute-done((f32[2,3,1,128,128]{4,3,0,2,1:T(8,128)}, f32[2,3,1,128,128]{4,3,0,2,1:T(8,128)S(1)}, u32[]{:S(2)}, u32[]{:S(2)}) %collective-permute-start.18) | collective-permute-done | bytes 393248 | tf_op jit(solution)/shard_map/ppermute | solution.py:25
  327.2 7.1 fusion.19
  334.4 5.1 collective-permute-start.20
  341.5 14.9 %collective-permute-done.20 = f32[2,3,1,128,128]{4,3,0,2,1:T(8,128)S(1)} collective-permute-done((f32[2,3,1,128,128]{4,3,0,2,1:T(8,128)S(1)}, f32[2,3,1,128,128]{4,3,0,2,1:T(8,128)S(1)}, u32[]{:S(2)}, u32[]{:S(2)}) %collective-permute-start.20) | collective-permute-done | bytes 393248 | tf_op jit(solution)/shard_map/ppermute | solution.py:25
  360.1 5.0 collective-permute-start.22
  373.9 17.4 %collective-permute-done.22 = f32[2,3,1,128,128]{4,3,0,2,1:T(8,128)S(1)} collective-permute-done((f32[2,3,1,128,128]{4,3,0,2,1:T(8,128)S(1)}, f32[2,3,1,128,128]{4,3,0,2,1:T(8,128)S(1)}, u32[]{:S(2)}, u32[]{:S(2)}) %collective-permute-start.22) | collective-permute-done | bytes 393248 | tf_op jit(solution)/shard_map/ppermute | solution.py:25
  419.7 7.4 collective-permute-done.26
  428.6 5.0 collective-permute-start.27
  453.5 4.9 collective-permute-done.30
  469.7 4.9 collective-permute-done.36
  509.7 11.7 %collective-permute-done.41 = f32[1,3,4,128,128]{4,3,0,2,1:T(8,128)} collective-permute-done((f32[1,3,4,128,128]{4,3,0,2,1:T(8,128)}, f32[1,3,4,128,128]{4,3,0,2,1:T(8,128)}, u32[]{:S(2)}, u32[]{:S(2)}) %collective-permute-start.41) | collective-permute-done | bytes 786464 | tf_op jit(solution)/shard_map/ppermute | solution.py:41
  531.7 5.5 collective-permute-done.43
  548.1 4.9 collective-permute-done.45
  563.6 4.9 collective-permute-done.47
  579.0 4.9 collective-permute-done.49
  594.5 4.9 collective-permute-done.51
  608.8 5.3 collective-permute-done.53
  618.4 11.7 %collective-permute-done.54 = f32[1,3,4,128,128]{4,3,0,2,1:T(8,128)} collective-permute-done((f32[1,3,4,128,128]{4,3,0,2,1:T(8,128)}, f32[1,3,4,128,128]{4,3,0,2,1:T(8,128)}, u32[]{:S(2)}, u32[]{:S(2)}) %collective-permute-start.54) | collective-permute-done | bytes 786464 | tf_op jit(solution)/shard_map/ppermute | solution.py:41
  637.2 7.0 collective-permute-done.55
  651.9 7.8 collective-permute-done.57
  715.1 5.2 collective-permute-done.66
  724.6 11.7 %collective-permute-done.67 = f32[1,3,4,128,128]{4,3,0,2,1:T(8,128)} collective-permute-done((f32[1,3,4,128,128]{4,3,0,2,1:T(8,128)}, f32[1,3,4,128,128]{4,3,0,2,1:T(8,128)}, u32[]{:S(2)}, u32[]{:S(2)}) %collective-permute-start.67) | collective-permute-done | bytes 786464 | tf_op jit(solution)/shard_map/ppermute | solution.py:41
  743.7 7.5 collective-permute-done.68
  758.6 7.5 collective-permute-done.70
  775.4 5.0 collective-permute-done.73
  (298 shorter events, 399.8 us)
Async XLA Ops:
  5.3 27.8 %collective-permute-start = (f32[2,3,1,128,128]{4,3,0,2,1:T(8,128)}, f32[2,3,1,128,128]{4,3,0,2,1:T(8,128)S(1)}, u32[]{:S(2)}, u32[]{:S(2)}) collective-permute-start(f32[2,3,1,128,128]{4,3,0,2,1:T(8,128)} %get-tuple-element.95), channel_id=1, source_target_pairs={{1,0},{2,1},{3,2},{4,3},{5,4},{6,5},{7,6},{9,8},{10,9},{11,10},{12... | collective-permute-start | bytes 1179656 | tf_op jit(solution)/shard_map/ppermute | solution.py:25
  8.7 24.4 %collective-permute-start.1 = (f32[2,3,1,128,128]{4,3,0,2,1:T(8,128)}, f32[2,3,1,128,128]{4,3,0,2,1:T(8,128)S(1)}, u32[]{:S(2)}, u32[]{:S(2)}) collective-permute-start(f32[2,3,1,128,128]{4,3,0,2,1:T(8,128)} %get-tuple-element.94), channel_id=1, source_target_pairs={{0,1},{1,2},{2,3},{3,4},{4,5},{5,6},{6,7},{8,9},{9,10},{10,11},{11... | collective-permute-start | bytes 1179656 | tf_op jit(solution)/shard_map/ppermute | solution.py:23
  14.9 12.0 %all-to-all-start = ((s32[2,8,32]{2,0,1:T(2,128)}), s32[2,8,32]{2,0,1:T(2,128)S(1)}, u32[]{:S(2)}, u32[]{:S(2)}) async-start(s32[2,8,32]{2,0,1:T(2,128)} %copy.48), calls=%async_computation | async-start | bytes 16384 | tf_op jit(solution)/shard_map/all_to_all | solution.py:79
  26.9 14.4 %all-to-all-start.1 = ((f32[2,8,32,128]{3,2,0,1:T(8,128)}), f32[2,8,32,128]{3,2,0,1:T(8,128)}, u32[]{:S(2)}, u32[]{:S(2)}) async-start(f32[2,8,32,128]{3,2,0,1:T(8,128)} %copy.51), calls=%async_computation.1 | async-start | bytes 524288 | tf_op jit(solution)/shard_map/all_to_all | solution.py:94
  49.4 19.1 %collective-permute-start.2 = (f32[2,3,1,128,128]{4,3,0,2,1:T(8,128)S(1)}, f32[2,3,1,128,128]{4,3,0,2,1:T(8,128)S(1)}, u32[]{:S(2)}, u32[]{:S(2)}) collective-permute-start(f32[2,3,1,128,128]{4,3,0,2,1:T(8,128)S(1)} %get-tuple-element.93), channel_id=1, source_target_pairs={{1,0},{2,1},{3,2},{4,3},{5,4},{6,5},{7,6},{9,8},{10,9},{11,10},{12... | collective-permute-start | bytes 1179656 | tf_op jit(solution)/shard_map/ppermute | solution.py:25
  53.2 15.4 %collective-permute-start.3 = (f32[2,3,1,128,128]{4,3,0,2,1:T(8,128)S(1)}, f32[2,3,1,128,128]{4,3,0,2,1:T(8,128)S(1)}, u32[]{:S(2)}, u32[]{:S(2)}) collective-permute-start(f32[2,3,1,128,128]{4,3,0,2,1:T(8,128)S(1)} %get-tuple-element.92), channel_id=1, source_target_pairs={{0,1},{1,2},{2,3},{3,4},{4,5},{5,6},{6,7},{8,9},{9,10},{10,11},{11... | collective-permute-start | bytes 1179656 | tf_op jit(solution)/shard_map/ppermute | solution.py:23
  72.1 21.7 %collective-permute-start.4 = (f32[2,3,1,128,128]{4,3,0,2,1:T(8,128)S(1)}, f32[2,3,1,128,128]{4,3,0,2,1:T(8,128)S(1)}, u32[]{:S(2)}, u32[]{:S(2)}) collective-permute-start(f32[2,3,1,128,128]{4,3,0,2,1:T(8,128)S(1)} %get-tuple-element.91), channel_id=1, source_target_pairs={{1,0},{2,1},{3,2},{4,3},{5,4},{6,5},{7,6},{9,8},{10,9},{11,10},{12... | collective-permute-start | bytes 1179656 | tf_op jit(solution)/shard_map/ppermute | solution.py:25
  76.7 17.2 %collective-permute-start.5 = (f32[2,3,1,128,128]{4,3,0,2,1:T(8,128)S(1)}, f32[2,3,1,128,128]{4,3,0,2,1:T(8,128)S(1)}, u32[]{:S(2)}, u32[]{:S(2)}) collective-permute-start(f32[2,3,1,128,128]{4,3,0,2,1:T(8,128)S(1)} %get-tuple-element.90), channel_id=1, source_target_pairs={{0,1},{1,2},{2,3},{3,4},{4,5},{5,6},{6,7},{8,9},{9,10},{10,11},{11... | collective-permute-start | bytes 1179656 | tf_op jit(solution)/shard_map/ppermute | solution.py:23
  100.7 24.8 %collective-permute-start.6 = (f32[2,3,1,128,128]{4,3,0,2,1:T(8,128)}, f32[2,3,1,128,128]{4,3,0,2,1:T(8,128)S(1)}, u32[]{:S(2)}, u32[]{:S(2)}) collective-permute-start(f32[2,3,1,128,128]{4,3,0,2,1:T(8,128)} %get-tuple-element.89), channel_id=1, source_target_pairs={{1,0},{2,1},{3,2},{4,3},{5,4},{6,5},{7,6},{9,8},{10,9},{11,10},{12... | collective-permute-start | bytes 1179656 | tf_op jit(solution)/shard_map/ppermute | solution.py:25
  105.8 19.8 %collective-permute-start.7 = (f32[2,3,1,128,128]{4,3,0,2,1:T(8,128)}, f32[2,3,1,128,128]{4,3,0,2,1:T(8,128)S(1)}, u32[]{:S(2)}, u32[]{:S(2)}) collective-permute-start(f32[2,3,1,128,128]{4,3,0,2,1:T(8,128)} %get-tuple-element.88), channel_id=1, source_target_pairs={{0,1},{1,2},{2,3},{3,4},{4,5},{5,6},{6,7},{8,9},{9,10},{10,11},{11... | collective-permute-start | bytes 1179656 | tf_op jit(solution)/shard_map/ppermute | solution.py:23
  108.9 21.4 %all-to-all-start.2 = ((f32[2,8,32,128]{3,2,0,1:T(8,128)}), f32[2,8,32,128]{3,2,0,1:T(8,128)}, u32[]{:S(2)}, u32[]{:S(2)}) async-start(f32[2,8,32,128]{3,2,0,1:T(8,128)} %copy.59), calls=%async_computation.2 | async-start | bytes 524288 | tf_op jit(solution)/shard_map/all_to_all | solution.py:94
  140.3 21.9 %collective-permute-start.8 = (f32[2,3,1,128,128]{4,3,0,2,1:T(8,128)S(1)}, f32[2,3,1,128,128]{4,3,0,2,1:T(8,128)S(1)}, u32[]{:S(2)}, u32[]{:S(2)}) collective-permute-start(f32[2,3,1,128,128]{4,3,0,2,1:T(8,128)S(1)} %get-tuple-element.87), channel_id=1, source_target_pairs={{1,0},{2,1},{3,2},{4,3},{5,4},{6,5},{7,6},{9,8},{10,9},{11,10},{12... | collective-permute-start | bytes 1179656 | tf_op jit(solution)/shard_map/ppermute | solution.py:25
  145.2 17.1 %collective-permute-start.9 = (f32[2,3,1,128,128]{4,3,0,2,1:T(8,128)S(1)}, f32[2,3,1,128,128]{4,3,0,2,1:T(8,128)S(1)}, u32[]{:S(2)}, u32[]{:S(2)}) collective-permute-start(f32[2,3,1,128,128]{4,3,0,2,1:T(8,128)S(1)} %get-tuple-element.86), channel_id=1, source_target_pairs={{0,1},{1,2},{2,3},{3,4},{4,5},{5,6},{6,7},{8,9},{9,10},{10,11},{11... | collective-permute-start | bytes 1179656 | tf_op jit(solution)/shard_map/ppermute | solution.py:23
  166.0 22.1 %collective-permute-start.10 = (f32[2,3,1,128,128]{4,3,0,2,1:T(8,128)S(1)}, f32[2,3,1,128,128]{4,3,0,2,1:T(8,128)S(1)}, u32[]{:S(2)}, u32[]{:S(2)}) collective-permute-start(f32[2,3,1,128,128]{4,3,0,2,1:T(8,128)S(1)} %get-tuple-element.85), channel_id=1, source_target_pairs={{1,0},{2,1},{3,2},{4,3},{5,4},{6,5},{7,6},{9,8},{10,9},{11,10},{12... | collective-permute-start | bytes 1179656 | tf_op jit(solution)/shard_map/ppermute | solution.py:25
  171.0 17.2 %collective-permute-start.11 = (f32[2,3,1,128,128]{4,3,0,2,1:T(8,128)S(1)}, f32[2,3,1,128,128]{4,3,0,2,1:T(8,128)S(1)}, u32[]{:S(2)}, u32[]{:S(2)}) collective-permute-start(f32[2,3,1,128,128]{4,3,0,2,1:T(8,128)S(1)} %get-tuple-element.84), channel_id=1, source_target_pairs={{0,1},{1,2},{2,3},{3,4},{4,5},{5,6},{6,7},{8,9},{9,10},{10,11},{11... | collective-permute-start | bytes 1179656 | tf_op jit(solution)/shard_map/ppermute | solution.py:23
  198.3 24.8 %collective-permute-start.12 = (f32[2,3,1,128,128]{4,3,0,2,1:T(8,128)}, f32[2,3,1,128,128]{4,3,0,2,1:T(8,128)S(1)}, u32[]{:S(2)}, u32[]{:S(2)}) collective-permute-start(f32[2,3,1,128,128]{4,3,0,2,1:T(8,128)} %get-tuple-element.83), channel_id=1, source_target_pairs={{1,0},{2,1},{3,2},{4,3},{5,4},{6,5},{7,6},{9,8},{10,9},{11,10},{12... | collective-permute-start | bytes 1179656 | tf_op jit(solution)/shard_map/ppermute | solution.py:25
  203.3 19.8 %collective-permute-start.13 = (f32[2,3,1,128,128]{4,3,0,2,1:T(8,128)}, f32[2,3,1,128,128]{4,3,0,2,1:T(8,128)S(1)}, u32[]{:S(2)}, u32[]{:S(2)}) collective-permute-start(f32[2,3,1,128,128]{4,3,0,2,1:T(8,128)} %get-tuple-element.82), channel_id=1, source_target_pairs={{0,1},{1,2},{2,3},{3,4},{4,5},{5,6},{6,7},{8,9},{9,10},{10,11},{11... | collective-permute-start | bytes 1179656 | tf_op jit(solution)/shard_map/ppermute | solution.py:23
  207.3 20.5 %all-to-all-start.3 = ((f32[2,8,32,128]{3,2,0,1:T(8,128)}), f32[2,8,32,128]{3,2,0,1:T(8,128)}, u32[]{:S(2)}, u32[]{:S(2)}) async-start(f32[2,8,32,128]{3,2,0,1:T(8,128)} %copy.62), calls=%async_computation.3 | async-start | bytes 524288 | tf_op jit(solution)/shard_map/all_to_all | solution.py:94
  237.8 21.9 %collective-permute-start.14 = (f32[2,3,1,128,128]{4,3,0,2,1:T(8,128)S(1)}, f32[2,3,1,128,128]{4,3,0,2,1:T(8,128)S(1)}, u32[]{:S(2)}, u32[]{:S(2)}) collective-permute-start(f32[2,3,1,128,128]{4,3,0,2,1:T(8,128)S(1)} %get-tuple-element.81), channel_id=1, source_target_pairs={{1,0},{2,1},{3,2},{4,3},{5,4},{6,5},{7,6},{9,8},{10,9},{11,10},{12... | collective-permute-start | bytes 1179656 | tf_op jit(solution)/shard_map/ppermute | solution.py:25
  242.7 17.1 %collective-permute-start.15 = (f32[2,3,1,128,128]{4,3,0,2,1:T(8,128)S(1)}, f32[2,3,1,128,128]{4,3,0,2,1:T(8,128)S(1)}, u32[]{:S(2)}, u32[]{:S(2)}) collective-permute-start(f32[2,3,1,128,128]{4,3,0,2,1:T(8,128)S(1)} %get-tuple-element.80), channel_id=1, source_target_pairs={{0,1},{1,2},{2,3},{3,4},{4,5},{5,6},{6,7},{8,9},{9,10},{10,11},{11... | collective-permute-start | bytes 1179656 | tf_op jit(solution)/shard_map/ppermute | solution.py:23
  263.5 22.1 %collective-permute-start.16 = (f32[2,3,1,128,128]{4,3,0,2,1:T(8,128)S(1)}, f32[2,3,1,128,128]{4,3,0,2,1:T(8,128)S(1)}, u32[]{:S(2)}, u32[]{:S(2)}) collective-permute-start(f32[2,3,1,128,128]{4,3,0,2,1:T(8,128)S(1)} %get-tuple-element.79), channel_id=1, source_target_pairs={{1,0},{2,1},{3,2},{4,3},{5,4},{6,5},{7,6},{9,8},{10,9},{11,10},{12... | collective-permute-start | bytes 1179656 | tf_op jit(solution)/shard_map/ppermute | solution.py:25
  268.5 17.2 %collective-permute-start.17 = (f32[2,3,1,128,128]{4,3,0,2,1:T(8,128)S(1)}, f32[2,3,1,128,128]{4,3,0,2,1:T(8,128)S(1)}, u32[]{:S(2)}, u32[]{:S(2)}) collective-permute-start(f32[2,3,1,128,128]{4,3,0,2,1:T(8,128)S(1)} %get-tuple-element.78), channel_id=1, source_target_pairs={{0,1},{1,2},{2,3},{3,4},{4,5},{5,6},{6,7},{8,9},{9,10},{10,11},{11... | collective-permute-start | bytes 1179656 | tf_op jit(solution)/shard_map/ppermute | solution.py:23
  295.8 24.8 %collective-permute-start.18 = (f32[2,3,1,128,128]{4,3,0,2,1:T(8,128)}, f32[2,3,1,128,128]{4,3,0,2,1:T(8,128)S(1)}, u32[]{:S(2)}, u32[]{:S(2)}) collective-permute-start(f32[2,3,1,128,128]{4,3,0,2,1:T(8,128)} %get-tuple-element.77), channel_id=1, source_target_pairs={{1,0},{2,1},{3,2},{4,3},{5,4},{6,5},{7,6},{9,8},{10,9},{11,10},{12... | collective-permute-start | bytes 1179656 | tf_op jit(solution)/shard_map/ppermute | solution.py:25
  300.8 19.8 %collective-permute-start.19 = (f32[2,3,1,128,128]{4,3,0,2,1:T(8,128)}, f32[2,3,1,128,128]{4,3,0,2,1:T(8,128)S(1)}, u32[]{:S(2)}, u32[]{:S(2)}) collective-permute-start(f32[2,3,1,128,128]{4,3,0,2,1:T(8,128)} %get-tuple-element.76), channel_id=1, source_target_pairs={{0,1},{1,2},{2,3},{3,4},{4,5},{5,6},{6,7},{8,9},{9,10},{10,11},{11... | collective-permute-start | bytes 1179656 | tf_op jit(solution)/shard_map/ppermute | solution.py:23
  304.8 20.5 %all-to-all-start.4 = ((f32[2,8,32,128]{3,2,0,1:T(8,128)}), f32[2,8,32,128]{3,2,0,1:T(8,128)S(1)}, u32[]{:S(2)}, u32[]{:S(2)}) async-start(f32[2,8,32,128]{3,2,0,1:T(8,128)} %copy.65), calls=%async_computation.4 | async-start | bytes 524288 | tf_op jit(solution)/shard_map/all_to_all | solution.py:94
  334.4 22.1 %collective-permute-start.20 = (f32[2,3,1,128,128]{4,3,0,2,1:T(8,128)S(1)}, f32[2,3,1,128,128]{4,3,0,2,1:T(8,128)S(1)}, u32[]{:S(2)}, u32[]{:S(2)}) collective-permute-start(f32[2,3,1,128,128]{4,3,0,2,1:T(8,128)S(1)} %get-tuple-element.75), channel_id=1, source_target_pairs={{1,0},{2,1},{3,2},{4,3},{5,4},{6,5},{7,6},{9,8},{10,9},{11,10},{12... | collective-permute-start | bytes 1179656 | tf_op jit(solution)/shard_map/ppermute | solution.py:25
  339.5 17.1 %collective-permute-start.21 = (f32[2,3,1,128,128]{4,3,0,2,1:T(8,128)S(1)}, f32[2,3,1,128,128]{4,3,0,2,1:T(8,128)S(1)}, u32[]{:S(2)}, u32[]{:S(2)}) collective-permute-start(f32[2,3,1,128,128]{4,3,0,2,1:T(8,128)S(1)} %get-tuple-element.74), channel_id=1, source_target_pairs={{0,1},{1,2},{2,3},{3,4},{4,5},{5,6},{6,7},{8,9},{9,10},{10,11},{11... | collective-permute-start | bytes 1179656 | tf_op jit(solution)/shard_map/ppermute | solution.py:23
  360.1 31.2 %collective-permute-start.22 = (f32[2,3,1,128,128]{4,3,0,2,1:T(8,128)S(1)}, f32[2,3,1,128,128]{4,3,0,2,1:T(8,128)S(1)}, u32[]{:S(2)}, u32[]{:S(2)}) collective-permute-start(f32[2,3,1,128,128]{4,3,0,2,1:T(8,128)S(1)} %get-tuple-element.73), channel_id=1, source_target_pairs={{1,0},{2,1},{3,2},{4,3},{5,4},{6,5},{7,6},{9,8},{10,9},{11,10},{12... | collective-permute-start | bytes 1179656 | tf_op jit(solution)/shard_map/ppermute | solution.py:25
  365.1 26.2 %collective-permute-start.23 = (f32[2,3,1,128,128]{4,3,0,2,1:T(8,128)S(1)}, f32[2,3,1,128,128]{4,3,0,2,1:T(8,128)S(1)}, u32[]{:S(2)}, u32[]{:S(2)}) collective-permute-start(f32[2,3,1,128,128]{4,3,0,2,1:T(8,128)S(1)} %get-tuple-element.72), channel_id=1, source_target_pairs={{0,1},{1,2},{2,3},{3,4},{4,5},{5,6},{6,7},{8,9},{9,10},{10,11},{11... | collective-permute-start | bytes 1179656 | tf_op jit(solution)/shard_map/ppermute | solution.py:23
  367.1 31.9 %collective-permute-start.31 = (f32[2,3,1,128,128]{4,3,0,2,1:T(8,128)S(1)}, f32[2,3,1,128,128]{4,3,0,2,1:T(8,128)S(1)}, u32[]{:S(2)}, u32[]{:S(2)}) collective-permute-start(f32[2,3,1,128,128]{4,3,0,2,1:T(8,128)S(1)} %get-tuple-element.68), channel_id=1, source_target_pairs={{1,0},{2,1},{3,2},{4,3},{5,4},{6,5},{7,6},{9,8},{10,9},{11,10},{12... | collective-permute-start | bytes 1179656 | tf_op jit(solution)/shard_map/ppermute | solution.py:25
  372.0 27.3 %collective-permute-start.32 = (f32[2,3,1,128,128]{4,3,0,2,1:T(8,128)S(1)}, f32[2,3,1,128,128]{4,3,0,2,1:T(8,128)S(1)}, u32[]{:S(2)}, u32[]{:S(2)}) collective-permute-start(f32[2,3,1,128,128]{4,3,0,2,1:T(8,128)S(1)} %get-tuple-element.67), channel_id=1, source_target_pairs={{0,1},{1,2},{2,3},{3,4},{4,5},{5,6},{6,7},{8,9},{9,10},{10,11},{11... | collective-permute-start | bytes 1179656 | tf_op jit(solution)/shard_map/ppermute | solution.py:23
  394.8 11.5 %collective-permute-start.24 = (f32[1,3,4,128,128]{4,3,0,2,1:T(8,128)S(1)}, f32[1,3,4,128,128]{4,3,0,2,1:T(8,128)S(1)}, u32[]{:S(2)}, u32[]{:S(2)}) collective-permute-start(f32[1,3,4,128,128]{4,3,0,2,1:T(8,128)S(1)} %slice.1534), channel_id=1, source_target_pairs={{0,8},{8,16},{16,24},{24,0},{1,9},{9,17},{17,25},{25,1},{2,10},{10... | collective-permute-start | bytes 2359304 | tf_op jit(solution)/shard_map/ppermute | solution.py:35
  406.3 13.3 %collective-permute-start.25 = (f32[1,3,1,128,128]{4,3,0,2,1:T(8,128)S(1)}, f32[1,3,1,128,128]{4,3,0,2,1:T(8,128)S(1)}, u32[]{:S(2)}, u32[]{:S(2)}) collective-permute-start(f32[1,3,1,128,128]{4,3,0,2,1:T(8,128)S(1)} %get-tuple-element.139), channel_id=1, source_target_pairs={{1,0},{2,1},{3,2},{4,3},{5,4},{6,5},{7,6},{9,8},{10,9},{11,10},{12... | collective-permute-start | bytes 589832 | tf_op jit(solution)/shard_map/ppermute | solution.py:25
  410.9 16.2 %collective-permute-start.26 = (f32[1,3,1,128,128]{4,3,0,2,1:T(8,128)S(1)}, f32[1,3,1,128,128]{4,3,0,2,1:T(8,128)S(1)}, u32[]{:S(2)}, u32[]{:S(2)}) collective-permute-start(f32[1,3,1,128,128]{4,3,0,2,1:T(8,128)S(1)} %get-tuple-element.138), channel_id=1, source_target_pairs={{0,1},{1,2},{2,3},{3,4},{4,5},{5,6},{6,7},{8,9},{9,10},{10,11},{11... | collective-permute-start | bytes 589832 | tf_op jit(solution)/shard_map/ppermute | solution.py:23
  412.9 23.4 %collective-permute-start.33 = (f32[2,3,1,128,128]{4,3,0,2,1:T(8,128)S(1)}, f32[2,3,1,128,128]{4,3,0,2,1:T(8,128)S(1)}, u32[]{:S(2)}, u32[]{:S(2)}) collective-permute-start(f32[2,3,1,128,128]{4,3,0,2,1:T(8,128)S(1)} %get-tuple-element.66), channel_id=1, source_target_pairs={{1,0},{2,1},{3,2},{4,3},{5,4},{6,5},{7,6},{9,8},{10,9},{11,10},{12... | collective-permute-start | bytes 1179656 | tf_op jit(solution)/shard_map/ppermute | solution.py:25
  417.7 22.0 %collective-permute-start.34 = (f32[2,3,1,128,128]{4,3,0,2,1:T(8,128)S(1)}, f32[2,3,1,128,128]{4,3,0,2,1:T(8,128)S(1)}, u32[]{:S(2)}, u32[]{:S(2)}) collective-permute-start(f32[2,3,1,128,128]{4,3,0,2,1:T(8,128)S(1)} %get-tuple-element.65), channel_id=1, source_target_pairs={{0,1},{1,2},{2,3},{3,4},{4,5},{5,6},{6,7},{8,9},{9,10},{10,11},{11... | collective-permute-start | bytes 1179656 | tf_op jit(solution)/shard_map/ppermute | solution.py:23
  428.6 15.0 %collective-permute-start.27 = (f32[1,3,1,128,128]{4,3,0,2,1:T(8,128)S(1)}, f32[1,3,1,128,128]{4,3,0,2,1:T(8,128)S(1)}, u32[]{:S(2)}, u32[]{:S(2)}) collective-permute-start(f32[1,3,1,128,128]{4,3,0,2,1:T(8,128)S(1)} %get-tuple-element.137), channel_id=1, source_target_pairs={{1,0},{2,1},{3,2},{4,3},{5,4},{6,5},{7,6},{9,8},{10,9},{11,10},{12... | collective-permute-start | bytes 589832 | tf_op jit(solution)/shard_map/ppermute | solution.py:25
  433.7 10.0 %collective-permute-start.28 = (f32[1,3,1,128,128]{4,3,0,2,1:T(8,128)S(1)}, f32[1,3,1,128,128]{4,3,0,2,1:T(8,128)S(1)}, u32[]{:S(2)}, u32[]{:S(2)}) collective-permute-start(f32[1,3,1,128,128]{4,3,0,2,1:T(8,128)S(1)} %get-tuple-element.136), channel_id=1, source_target_pairs={{0,1},{1,2},{2,3},{3,4},{4,5},{5,6},{6,7},{8,9},{9,10},{10,11},{11... | collective-permute-start | bytes 589832 | tf_op jit(solution)/shard_map/ppermute | solution.py:23
  507.7 13.6 %collective-permute-start.41 = (f32[1,3,4,128,128]{4,3,0,2,1:T(8,128)}, f32[1,3,4,128,128]{4,3,0,2,1:T(8,128)}, u32[]{:S(2)}, u32[]{:S(2)}) collective-permute-start(f32[1,3,4,128,128]{4,3,0,2,1:T(8,128)} %fusion.100), channel_id=1, source_target_pairs={{0,8},{8,16},{16,24},{1,9},{9,17},{17,25},{2,10},{10,18},{18,26},{... | collective-permute-start | bytes 2359304 | tf_op jit(solution)/shard_map/ppermute | solution.py:41
  527.2 10.0 %collective-permute-start.43 = (f32[1,3,1,128,128]{4,3,0,2,1:T(8,128)S(1)}, f32[1,3,1,128,128]{4,3,0,2,1:T(8,128)S(1)}, u32[]{:S(2)}, u32[]{:S(2)}) collective-permute-start(f32[1,3,1,128,128]{4,3,0,2,1:T(8,128)S(1)} %get-tuple-element.126), channel_id=1, source_target_pairs={{0,1},{1,2},{2,3},{3,4},{4,5},{5,6},{6,7},{8,9},{9,10},{10,11},{11... | collective-permute-start | bytes 589832 | tf_op jit(solution)/shard_map/ppermute | solution.py:23
  616.4 13.6 %collective-permute-start.54 = (f32[1,3,4,128,128]{4,3,0,2,1:T(8,128)}, f32[1,3,4,128,128]{4,3,0,2,1:T(8,128)}, u32[]{:S(2)}, u32[]{:S(2)}) collective-permute-start(f32[1,3,4,128,128]{4,3,0,2,1:T(8,128)} %fusion.80), channel_id=1, source_target_pairs={{0,8},{8,16},{16,24},{1,9},{9,17},{17,25},{2,10},{10,18},{18,26},{... | collective-permute-start | bytes 2359304 | tf_op jit(solution)/shard_map/ppermute | solution.py:41
  631.4 12.9 %collective-permute-start.55 = (f32[1,3,1,128,128]{4,3,0,2,1:T(8,128)S(1)}, f32[1,3,1,128,128]{4,3,0,2,1:T(8,128)S(1)}, u32[]{:S(2)}, u32[]{:S(2)}) collective-permute-start(f32[1,3,1,128,128]{4,3,0,2,1:T(8,128)S(1)} %get-tuple-element.115), channel_id=1, source_target_pairs={{1,0},{2,1},{3,2},{4,3},{5,4},{6,5},{7,6},{9,8},{10,9},{11,10},{12... | collective-permute-start | bytes 589832 | tf_op jit(solution)/shard_map/ppermute | solution.py:25
  633.5 10.8 %collective-permute-start.56 = (f32[1,3,1,128,128]{4,3,0,2,1:T(8,128)S(1)}, f32[1,3,1,128,128]{4,3,0,2,1:T(8,128)S(1)}, u32[]{:S(2)}, u32[]{:S(2)}) collective-permute-start(f32[1,3,1,128,128]{4,3,0,2,1:T(8,128)S(1)} %get-tuple-element.114), channel_id=1, source_target_pairs={{0,1},{1,2},{2,3},{3,4},{4,5},{5,6},{6,7},{8,9},{9,10},{10,11},{11... | collective-permute-start | bytes 589832 | tf_op jit(solution)/shard_map/ppermute | solution.py:23
  645.8 13.9 %collective-permute-start.57 = (f32[1,3,1,128,128]{4,3,0,2,1:T(8,128)S(1)}, f32[1,3,1,128,128]{4,3,0,2,1:T(8,128)S(1)}, u32[]{:S(2)}, u32[]{:S(2)}) collective-permute-start(f32[1,3,1,128,128]{4,3,0,2,1:T(8,128)S(1)} %get-tuple-element.113), channel_id=1, source_target_pairs={{1,0},{2,1},{3,2},{4,3},{5,4},{6,5},{7,6},{9,8},{10,9},{11,10},{12... | collective-permute-start | bytes 589832 | tf_op jit(solution)/shard_map/ppermute | solution.py:25
  722.7 13.6 %collective-permute-start.67 = (f32[1,3,4,128,128]{4,3,0,2,1:T(8,128)}, f32[1,3,4,128,128]{4,3,0,2,1:T(8,128)}, u32[]{:S(2)}, u32[]{:S(2)}) collective-permute-start(f32[1,3,4,128,128]{4,3,0,2,1:T(8,128)} %fusion.60), channel_id=1, source_target_pairs={{0,8},{8,16},{16,24},{1,9},{9,17},{17,25},{2,10},{10,18},{18,26},{... | collective-permute-start | bytes 2359304 | tf_op jit(solution)/shard_map/ppermute | solution.py:41
  737.8 13.4 %collective-permute-start.68 = (f32[1,3,1,128,128]{4,3,0,2,1:T(8,128)S(1)}, f32[1,3,1,128,128]{4,3,0,2,1:T(8,128)S(1)}, u32[]{:S(2)}, u32[]{:S(2)}) collective-permute-start(f32[1,3,1,128,128]{4,3,0,2,1:T(8,128)S(1)} %get-tuple-element.103), channel_id=1, source_target_pairs={{1,0},{2,1},{3,2},{4,3},{5,4},{6,5},{7,6},{9,8},{10,9},{11,10},{12... | collective-permute-start | bytes 589832 | tf_op jit(solution)/shard_map/ppermute | solution.py:25
  739.9 11.3 %collective-permute-start.69 = (f32[1,3,1,128,128]{4,3,0,2,1:T(8,128)S(1)}, f32[1,3,1,128,128]{4,3,0,2,1:T(8,128)S(1)}, u32[]{:S(2)}, u32[]{:S(2)}) collective-permute-start(f32[1,3,1,128,128]{4,3,0,2,1:T(8,128)S(1)} %get-tuple-element.102), channel_id=1, source_target_pairs={{0,1},{1,2},{2,3},{3,4},{4,5},{5,6},{6,7},{8,9},{9,10},{10,11},{11... | collective-permute-start | bytes 589832 | tf_op jit(solution)/shard_map/ppermute | solution.py:23
  752.8 13.4 %collective-permute-start.70 = (f32[1,3,1,128,128]{4,3,0,2,1:T(8,128)S(1)}, f32[1,3,1,128,128]{4,3,0,2,1:T(8,128)S(1)}, u32[]{:S(2)}, u32[]{:S(2)}) collective-permute-start(f32[1,3,1,128,128]{4,3,0,2,1:T(8,128)S(1)} %get-tuple-element.101), channel_id=1, source_target_pairs={{1,0},{2,1},{3,2},{4,3},{5,4},{6,5},{7,6},{9,8},{10,9},{11,10},{12... | collective-permute-start | bytes 589832 | tf_op jit(solution)/shard_map/ppermute | solution.py:25
  (55 other events, 756.1 us)
where the time goes:
time: 794 us; the launch traced here: 784 us
  waiting for transfers between devices  354 us (45%)
  starting transfers between devices  263 us (33%)
  other arithmetic  138 us (17%)
  local copies, waits for them, and re-layouts  16.4 us (2%)
  matrix products  10.4 us (1%)
    ppermute x35, waiting for transfers between devices, padded_2(): lax.ppermute(head, axis, [((i + 1) % count, i) for i in range(ends)])  222 us
    ppermute x35, starting transfers between devices, padded_2(): lax.ppermute(head, axis, [((i + 1) % count, i) for i in range(ends)])  155 us
    ppermute x35, waiting for transfers between devices, padded_2(): lax.ppermute(tail, axis, [(i, (i + 1) % count) for i in range(ends)])  86.2 us
    ppermute x35, starting transfers between devices, padded_2(): lax.ppermute(tail, axis, [(i, (i + 1) % count) for i in range(ends)])  74 us
    concatenate x35, other arithmetic, padded_2(): jnp.concatenate([lax.ppermute(tail, axis, [(i, (i + 1) % count) for i in...  57.4 us
    div x26, other arithmetic, jacobi(): field = (rhs + neighbours(field)) / diag  52.3 us
    ppermute x3, waiting for transfers between devices, passed_along_2(): lax.ppermute(value, axis, [(source, source + steps) for source in range(f...  35.1 us
    all_to_all x4, starting transfers between devices, shards(): lax.all_to_all(packed, 'space', split_axis=1, concat_axis=1, tiled=True)  21.9 us
  transfers between devices with their start and end apart: 79, of which 63 were waited for; matrix products, arithmetic and copies ran while one was open for 5% of the time, Pallas kernels for 0%

commit v1 on v0

v1 whole, which is shorter than its diff:
```python
import functools

import jax
import jax.numpy as jnp
from jax import lax
from jax.experimental import pallas as pl
from jax.experimental.pallas import tpu as pltpu
from jax.sharding import PartitionSpec as P

STEPS = 4
SWEEPS = 3

inverse_step = 2.0
gap_gain = 1.0

AXES = ("tm", "space")
HIGHEST = lax.Precision.HIGHEST
PAD = 8


class Layout:
    def __init__(self, times, tiles):
        self.times, self.tiles = times, tiles
        self.all = [(t // 2, t % 2, s // 2, s % 2) for t in range(times) for s in range(tiles)]

    def number(self, ht, c, hs, y):
        return (2 * ht + c) * self.tiles + 2 * hs + y

    def at(self, block, tile):
        return self.number(block // 2, tile % 2, tile // 2, block % 2)

    def relabel(self):
        return [(self.number(h, c, z, y), self.number(h, y, z, c)) for h, c, z, y in self.all]

    def pairs(self, shift_of, blocks=None):
        found = []
        for block in range(self.times) if blocks is None else blocks:
            for tile in range(self.tiles):
                other = shift_of(tile)
                if 0 <= other < self.tiles:
                    found.append((self.at(block, tile), self.at(block, other)))
        return found

    def chip(self, blocks=None):
        return self.pairs(lambda tile: tile ^ 1, blocks)

    def hop(self, blocks=None):
        return self.pairs(lambda tile: tile + 1 if tile % 2 else tile - 1, blocks)

    def down(self):
        return self.pairs(lambda tile: tile - 1)

    def columns(self):
        return [[self.at(block, tile) for tile in range(self.tiles)] for block in range(self.times)]

    def spread(self, k, roles):
        return [
            (self.at(block, tile), self.at(block ^ k, tile))
            for block in range(self.times)
            if block ^ k < roles
            for tile in range(self.tiles)
        ]

    def home(self, k, roles):
        return [
            (self.at(role, tile), (role ^ k) * self.tiles + tile)
            for role in range(roles)
            for tile in range(self.tiles)
        ]


def send(value, pairs):
    return lax.ppermute(value, AXES, pairs)


def f32(*shape):
    return jax.ShapeDtypeStruct(shape, jnp.float32)


def whole(*shape):
    return pl.BlockSpec(shape, lambda i: (0,) * len(shape))


def each(*shape):
    return pl.BlockSpec((None,) + shape, lambda i: (i,) + (0,) * len(shape))


SCALARS = pl.BlockSpec(memory_space=pltpu.SMEM)


def run(kernel, name, grid, in_specs, out_specs, out_shape, scratch=()):
    return pl.pallas_call(
        kernel,
        grid=(grid,),
        in_specs=in_specs,
        out_specs=out_specs,
        out_shape=out_shape,
        scratch_shapes=list(scratch),
        name=name,
    )


def join(flags, own, chip, hop, put):
    wide, count = chip.shape[0], own.shape[0]
    put(wide, own)

    @pl.when(flags[0] == 0)
    def _():
        put(0, hop)
        put(wide + count, chip)

    @pl.when(flags[0] != 0)
    def _():
        put(0, chip)
        put(wide + count, hop)


def extend_kernel(flags, own, chip, hop, out):
    def put(start, ref):
        out[start : start + ref.shape[0]] = ref[...]

    join(flags, own, chip, hop, put)


def conduct_kernel(flags, own, chip, hop, ext, inv_fine, inv_coarse):
    extend_kernel(flags, own, chip, hop, ext)
    wide, count = chip.shape[0], own.shape[0]
    for plane in range(2 * wide + count):
        inside = 1
        if plane < wide:
            inside = flags[1]
        elif plane >= wide + count:
            inside = flags[2]
        mask = jnp.full(ext.shape[1:], inside, jnp.int32) != 0
        rate = inverse_step * ext[plane]
        inv_fine[plane] = jnp.where(mask, 1.0 / (rate + 6.0), 0.0)
        inv_coarse[plane] = jnp.where(mask, 1.0 / (rate / STEPS + 6.0), 0.0)


def sweep(src, dst, base, inv, low, high, shift=0):
    rows, lanes = base.shape[1:]
    lane = lax.broadcasted_iota(jnp.int32, (rows, lanes), 1)
    left_edge, right_edge = lane == 0, lane == lanes - 1

    def plane(p, carry):
        mid = src[p, PAD : PAD + rows, :]
        total = src[p - 1, PAD : PAD + rows, :] + src[p + 1, PAD : PAD + rows, :]
        total = total + (src[p, PAD - 1 : PAD - 1 + rows, :] + src[p, PAD + 1 : PAD + 1 + rows, :])
        left = jnp.where(left_edge, 0.0, pltpu.roll(mid, 1, 1))
        right = jnp.where(right_edge, 0.0, pltpu.roll(mid, lanes - 1, 1))
        new = base[p - 1] + (total + (left + right)) * inv[p - 1]
        if shift:
            dst[p - shift] = new
        else:
            dst[p, PAD : PAD + rows, :] = new
        return carry

    lax.fori_loop(low, high, plane, 0)


def three(start, work, other, base, inv, out):
    planes = start.shape[0]
    sweep(start, work, base, inv, 1, planes - 1)
    sweep(work, other, base, inv, 2, planes - 2)
    sweep(other, out, base, inv, 3, planes - 3, 3)


def clear_edges(*buffers):
    for buffer in buffers:
        rows = buffer.shape[1] - 2 * PAD
        zero = jnp.zeros((buffer.shape[0], PAD, buffer.shape[2]), jnp.float32)
        buffer[:, 0:PAD, :] = zero
        buffer[:, PAD + rows :, :] = zero


def load_field(flags, own, chip, hop, buffer):
    rows = own.shape[1]

    def put(start, ref):
        buffer[start : start + ref.shape[0], PAD : PAD + rows, :] = ref[...]

    join(flags, own, chip, hop, put)


def emit_halos(flags, out, to_chip, to_hop):
    core = flags[0]
    to_chip[...] = out[pl.ds(1 - core, SWEEPS)]
    to_hop[...] = out[pl.ds(core, SWEEPS)]


def fine_kernel(first, last, coupled, *refs):
    refs = list(refs)
    flags, own, chip, hop, source, ext, inv = refs[:7]
    refs = refs[7:]
    if coupled:
        gap, gap_next, refs = refs[0], refs[1], refs[2:]
    if coupled and not last:
        select, refs = refs[0], refs[1:]
    if first:
        inv_coarse, refs = refs[0], refs[1:]
    if last:
        old, refs = refs[0], refs[1:]
    out, refs = refs[0], refs[1:]
    if not last:
        to_chip, to_hop, refs = refs[0], refs[1], refs[2:]
    if coupled and not last:
        packed, refs = refs[0], refs[1:]
    if first:
        old_out, refs = refs[0], refs[1:]
    one, two, three_, base = refs[:4]
    rows = own.shape[1]
    planes = ext.shape[0]
    wide = (planes - own.shape[0]) // 2

    @pl.when(pl.program_id(0) == 0)
    def _():
        clear_edges(one, two, three_)

    load_field(flags, own, chip, hop, one)

    if first:

        def start_coarse(p, carry):
            v = one[p + 1, PAD : PAD + rows, :]
            base[p] = (inverse_step / STEPS) * ext[p] * v * inv_coarse[p]
            return carry

        lax.fori_loop(0, planes, start_coarse, 0)
        three(one, two, three_, base, inv_coarse, old_out)

    def start(p, carry):
        v = one[p + 1, PAD : PAD + rows, :]
        base[p] = (inverse_step * ext[p] * v + source[p]) * inv[p]
        return carry

    lax.fori_loop(0, planes, start, 0)
    if coupled:
        base[wide] = base[wide] + gap_gain * gap[...] * inv[wide]
        above = wide + own.shape[0]
        base[above] = base[above] + gap_gain * gap_next[...] * inv[above]
    three(one, two, three_, base, inv, out)
    if not last:
        emit_halos(flags, out, to_chip, to_hop)
    if coupled and not last:
        pack_into(select, out, packed)
    if last:
        keep = jnp.where(pl.program_id(0) % flags[5] == flags[4], 0.0, 1.0)
        out[...] = out[...] - keep * old[...]


def pack_into(select, field, packed):
    rows = jnp.dot(select[...], field[0], precision=HIGHEST, preferred_element_type=jnp.float32)
    packed[...] = rows.reshape(packed.shape)


def pack_kernel(select, field, packed):
    pack_into(select, field, packed)


def index_kernel(tiles_count, capacity, tile, row, select, dest):
    rows = tile.shape[-1]
    slots = tiles_count * capacity
    lower = lax.broadcasted_iota(jnp.int32, (rows, rows), 0)
    upper = lax.broadcasted_iota(jnp.int32, (rows, rows), 1)
    earlier = (lower < upper).astype(jnp.float32)
    hot = lax.broadcasted_iota(jnp.int32, (tiles_count, rows), 0) == tile[...]
    hot = hot.astype(jnp.float32)
    before = jnp.dot(hot, earlier, precision=HIGHEST, preferred_element_type=jnp.float32)
    position = jnp.sum(before * hot, axis=0, keepdims=True).astype(jnp.int32)
    slot = tile[...] * capacity + position
    chosen = (lax.broadcasted_iota(jnp.int32, (slots, rows), 0) == slot).astype(jnp.float32)
    select[...] = chosen
    wanted = jnp.broadcast_to((row[...] + 1).astype(jnp.float32), (8, rows))
    found = lax.dot_general(
        wanted,
        chosen,
        (((1,), (1,)), ((), ())),
        precision=HIGHEST,
        preferred_element_type=jnp.float32,
    )
    dest[...] = found[0:1]


def unpack_kernel(got, arrived, gap):
    rows, slots = gap.shape[0], got.shape[1]
    want = (lax.broadcasted_iota(jnp.int32, (rows, slots), 0) + 1).astype(jnp.float32)
    receive = (want == got[...]).astype(jnp.float32)
    values = arrived[...].reshape(slots, gap.shape[1])
    gap[...] = jnp.dot(receive, values, precision=HIGHEST, preferred_element_type=jnp.float32)


def fetch(flags, block, slot, parts, buffer, sem):
    for k, part in enumerate(parts):

        @pl.when(flags[3] ^ k == block)
        def _():
            copy = pltpu.make_async_copy(part.at[slot], buffer, sem)
            copy.start()
            copy.wait()


def begin_kernel(block, slot, parts_count, *refs):
    flags, parts = refs[0], refs[1 : 1 + parts_count]
    out, to_chip, to_hop, sem = refs[1 + parts_count :]
    fetch(flags, block, slot, parts, out, sem)
    emit_halos(flags, out, to_chip, to_hop)


def chain_kernel(block, slot, last, parts_count, *refs):
    flags, own, chip, hop, ext, inv = refs[:6]
    parts, refs = refs[6 : 6 + parts_count], list(refs[6 + parts_count :])
    out, refs = refs[0], refs[1:]
    if not last:
        to_chip, to_hop, refs = refs[0], refs[1], refs[2:]
    one, two, three_, base, jump, sem = refs
    rows = own.shape[1]
    planes = ext.shape[0]
    clear_edges(one, two, three_)
    load_field(flags, own, chip, hop, one)

    def start(p, carry):
        v = one[p + 1, PAD : PAD + rows, :]
        base[p] = (inverse_step / STEPS) * ext[p] * v * inv[p]
        return carry

    lax.fori_loop(0, planes, start, 0)
    fetch(flags, block, slot, parts, jump, sem)
    three(one, two, three_, base, inv, out)
    out[...] = out[...] + jump[...]
    if not last:
        emit_halos(flags, out, to_chip, to_hop)


def shards(states, sources, conductivity, gap_tile, gap_row):
    times, tiles = lax.axis_size("tm"), lax.axis_size("space")
    slices, comps, planes, rows, lanes = states.shape
    lay = Layout(times, tiles)
    capacity = max(2, 2 * rows // tiles)
    time_index, tile_index = lax.axis_index("tm"), lax.axis_index("space")
    core = time_index % 2
    block = 2 * (time_index // 2) + tile_index % 2
    tile = 2 * (tile_index // 2) + core
    last_slot = jnp.where(block == times - 1, slices - 1, -1)
    flags = jnp.stack(
        [
            core,
            (tile > 0).astype(jnp.int32),
            (tile < tiles - 1).astype(jnp.int32),
            block,
            last_slot,
            jnp.full((), slices, jnp.int32),
        ]
    ).astype(jnp.int32)
    relabel = lay.relabel()
    edge = SWEEPS - 1
    ext_planes = planes + 2 * edge
    buf_planes = planes + 2 * SWEEPS
    plane = (rows, lanes)

    def cut(value, start, width, axis):
        return lax.dynamic_slice_in_dim(value, start, width, axis)

    def exchange(value, width, axis):
        top = planes - width
        return (
            send(cut(value, top * (1 - core), width, axis), lay.chip()),
            send(cut(value, top * core, width, axis), lay.hop()),
        )

    tables = send(jnp.stack([gap_tile[:, :, 0], gap_row]), relabel)
    state_0 = send(states[:, 0], relabel)
    source_0 = send(sources[:, 0], relabel)
    conduct = send(conductivity, relabel)
    state_1 = send(jnp.moveaxis(states[:, 1:], 1, 0).reshape(-1, planes, *plane), relabel)
    source_1 = send(jnp.moveaxis(sources[:, 1:], 1, 0).reshape(-1, planes, *plane), relabel)

    select, dest = run(
        functools.partial(index_kernel, tiles, capacity),
        "gap_index",
        slices,
        [each(1, rows), each(1, rows)],
        [each(tiles * capacity, rows), each(1, tiles * capacity)],
        [f32(slices, tiles * capacity, rows), f32(slices, 1, tiles * capacity)],
    )(tables[0][:, None], tables[1][:, None])
    groups = lay.columns()

    def trade(value):
        return lax.all_to_all(value, AXES, 0, 0, axis_index_groups=groups, tiled=True)

    dest = jnp.swapaxes(dest.reshape(slices, tiles, capacity), 0, 1)
    got = jnp.swapaxes(trade(dest), 0, 1).reshape(slices, 1, tiles * capacity)

    cond_chip, cond_hop = exchange(conduct, edge, 0)
    ext, inv_fine, inv_coarse = run(
        conduct_kernel,
        "conduct",
        1,
        [SCALARS, whole(planes, *plane), whole(edge, *plane), whole(edge, *plane)],
        [whole(ext_planes, *plane)] * 3,
        [f32(ext_planes, *plane)] * 3,
    )(flags, conduct, cond_chip, cond_hop)

    def widen(value):
        chip, hop = exchange(value, edge, 1)
        return run(
            extend_kernel,
            "widen",
            value.shape[0],
            [SCALARS, each(planes, *plane), each(edge, *plane), each(edge, *plane)],
            each(ext_planes, *plane),
            f32(value.shape[0], ext_planes, *plane),
        )(flags, value, chip, hop)

    wide_0, wide_1 = widen(source_0), widen(source_1)

    buffers = [pltpu.VMEM((buf_planes, rows + 2 * PAD, lanes), jnp.float32)] * 3 + [
        pltpu.VMEM((ext_planes, *plane), jnp.float32)
    ]
    packed_shape = (tiles, slices, capacity, lanes)
    packed_spec = pl.BlockSpec((tiles, None, capacity, lanes), lambda i: (0, i, 0, 0))

    def fine(step, field, chip, hop, source, gaps=None, old=None):
        first, last = step == 0, step == STEPS - 1
        count = field.shape[0]
        args = [flags, field, chip, hop, source, ext, inv_fine]
        ins = [
            SCALARS,
            each(planes, *plane),
            each(SWEEPS, *plane),
            each(SWEEPS, *plane),
            each(ext_planes, *plane),
            whole(ext_planes, *plane),
            whole(ext_planes, *plane),
        ]
        outs, shapes = [each(planes, *plane)], [f32(count, planes, *plane)]
        if gaps is not None:
            args += list(gaps)
            ins += [each(*plane)] * 2
            if not last:
                args.append(select)
                ins.append(each(tiles * capacity, rows))
        if first:
            args.append(inv_coarse)
            ins.append(whole(ext_planes, *plane))
        if last:
            args.append(old)
            ins.append(each(planes, *plane))
        if not last:
            outs += [each(SWEEPS, *plane)] * 2
            shapes += [f32(count, SWEEPS, *plane)] * 2
            if gaps is not None:
                outs.append(packed_spec)
                shapes.append(f32(*packed_shape))
        if first:
            outs.append(each(planes, *plane))
            shapes.append(f32(count, planes, *plane))
        return run(
            functools.partial(fine_kernel, first, last, gaps is not None),
            f"fine_{step}_{int(gaps is not None)}",
            count,
            ins,
            outs,
            shapes,
            buffers,
        )(*args)

    def coupling(packed):
        arrived = trade(packed)
        gap = run(
            unpack_kernel,
            "unpack",
            slices,
            [each(1, tiles * capacity), packed_spec],
            each(*plane),
            f32(slices, *plane),
        )(got, arrived)
        return gap, send(gap, lay.down())

    packed = run(
        pack_kernel,
        "pack",
        slices,
        [each(tiles * capacity, rows), each(planes, *plane)],
        packed_spec,
        f32(*packed_shape),
    )(select, state_0)
    field_0, (chip_0, hop_0) = state_0, exchange(state_0, SWEEPS, 1)
    field_1, (chip_1, hop_1) = state_1, exchange(state_1, SWEEPS, 1)
    old_0 = old_1 = None
    for step in range(STEPS):
        gaps = coupling(packed)
        result_1 = fine(step, field_1, chip_1, hop_1, wide_1, None, old_1)
        result_0 = fine(step, field_0, chip_0, hop_0, wide_0, gaps, old_0)
        field_0, field_1 = result_0[0], result_1[0]
        if step == 0:
            old_0, old_1 = result_0[4], result_1[3]
        if step < STEPS - 1:
            packed = result_0[3]
            chip_0, hop_0 = send(result_0[1], lay.chip()), send(result_0[2], lay.hop())
            chip_1, hop_1 = send(result_1[1], lay.chip()), send(result_1[2], lay.hop())

    jumps = jnp.concatenate([field_0[None], field_1.reshape(comps - 1, slices, planes, *plane)], 0)

    def component(index):
        return lax.dynamic_index_in_dim(jumps, jnp.minimum(index, comps - 1), 0, keepdims=False)

    parts = [component(block)]
    for k in range(1, times):
        parts.append(send(component(block ^ k), lay.spread(k, comps)))
    anywhere = [pl.BlockSpec(memory_space=pl.ANY)] * times
    halo_specs = [whole(SWEEPS, *plane)] * 2
    halo_shapes = [f32(SWEEPS, *plane)] * 2
    dma = pltpu.SemaphoreType.DMA(())
    roles = range(comps)
    total = times * slices
    new, chip, hop = run(
        functools.partial(begin_kernel, times - 1, slices - 1, times),
        "begin",
        1,
        [SCALARS] + anywhere,
        [whole(planes, *plane)] + halo_specs,
        [f32(planes, *plane)] + halo_shapes,
        [dma],
    )(flags, *parts)
    news = [new]
    for j in range(total - 1):
        chip, hop = send(chip, lay.chip(roles)), send(hop, lay.hop(roles))
        last = j == total - 2
        result = run(
            functools.partial(chain_kernel, j // slices, j % slices, last, times),
            f"chain_{j}",
            1,
            [SCALARS, whole(planes, *plane)] + halo_specs + [whole(ext_planes, *plane)] * 2 + anywhere,
            [whole(planes, *plane)] + ([] if last else halo_specs),
            [f32(planes, *plane)] + ([] if last else halo_shapes),
            buffers + [pltpu.VMEM((planes, *plane), jnp.float32), dma],
        )(flags, new, chip, hop, ext, inv_coarse, *parts)
        new = result[0]
        if not last:
            chip, hop = result[1:]
        news.append(new)

    ready = jnp.stack(news).reshape(times, slices, planes, *plane)
    back = jnp.stack(
        [
            send(lax.dynamic_index_in_dim(ready, block ^ k, 0, keepdims=False), lay.home(k, comps))
            for k in range(times)
        ]
    )
    return jnp.stack(
        [
            lax.dynamic_index_in_dim(back, time_index ^ comp, 0, keepdims=False)
            for comp in range(comps)
        ],
        axis=1,
    )


def solution(mesh):
    placed = (
        P("tm", None, "space", None, None),
        P("tm", None, "space", None, None),
        P("space", None, None),
        P("tm", "space", None),
        P("tm", "space"),
    )
    return jax.shard_map(
        shards,
        mesh=mesh,
        in_specs=placed,
        out_specs=P("tm", None, "space", None, None),
        check_vma=False,
    )
```

time: 794 us -> 448 us (0.56)
  waiting for transfers between devices: 354 us -> 101 us
  Pallas kernels: 0 us -> 150 us
  other arithmetic: 138 us -> 4.68 us
  starting transfers between devices: 263 us -> 153 us
  local copies, waits for them, and re-layouts: 16.4 us -> 31.6 us
  matrix products: 10.4 us -> 0 us
    ppermute x74 -> x53, waiting for transfers between devices: 347 us -> 93.6 us  [send(): return lax.ppermute(value, AXES, pairs)]
    pallas_call x0 -> x25, Pallas kernels: none -> 150 us  [the longest x8 89.1 us: fine(): run(functools.partial(fine_kernel, first, last, gaps is not None), f'fine...]
    ppermute x74 -> x53, starting transfers between devices: 235 us -> 128 us  [send(): return lax.ppermute(value, AXES, pairs)]
    concatenate x36 -> x0, other arithmetic: 57.5 us -> none  [the longest x35 57.4 us: padded_2(): jnp.concatenate([lax.ppermute(tail, axis, [(i, (i + 1) % count) for i in...]
    div x27 -> x0, other arithmetic: 53.4 us -> none  [the longest x26 52.3 us: jacobi(): field = (rhs + neighbours(field)) / diag]
    unnamed x48 -> x85, local copies, waits for them, and re-layouts: 1.25 us -> 18.4 us
    add x8 -> x0, other arithmetic: 14.2 us -> none  [the longest x2 9.37 us: shards(): rhs = rate * field + sources]
    dot_general x8 -> x0, matrix products: 10.4 us -> none  [the longest x4 5.93 us: shards(): jnp.einsum('syj,sjz->syz', receive, arrived, precision=lax.Precision.HIGH...]
  transfers between devices with their start and end apart: 79 -> 58, of which waited for: 63 -> 19; matrix products, arithmetic and copies ran while one was open for 5% -> 4% of each run, Pallas kernels for 0% -> 22%
where the time goes in v1:
time: 448 us; the launch traced here: 442 us
  starting transfers between devices  153 us (34%)
  Pallas kernels  150 us (33%)
  waiting for transfers between devices  101 us (23%)
  local copies, waits for them, and re-layouts  31.6 us (7%)
  other arithmetic  4.68 us (1%)
    ppermute x53, starting transfers between devices, send(): return lax.ppermute(value, AXES, pairs)  128 us
    ppermute x53, waiting for transfers between devices, send(): return lax.ppermute(value, AXES, pairs)  93.6 us
    pallas_call x8, Pallas kernels, fine(): run(functools.partial(fine_kernel, first, last, gaps is not None), f'fine...  89.1 us
    pallas_call x7, Pallas kernels, shards(): run(functools.partial(chain_kernel, j // slices, j % slices, last, times)...  37.9 us
    all_to_all x5, starting transfers between devices, trade(): lax.all_to_all(value, AXES, 0, 0, axis_index_groups=groups, tiled=True)  25.8 us
    unnamed x85, local copies, waits for them, and re-layouts  18.4 us
  transfers between devices with their start and end apart: 58, of which 19 were waited for; matrix products, arithmetic and copies ran while one was open for 4% of the time, Pallas kernels for 22%

profile of v1, /device:TPU:10, one launch (start us, length us, event | category | flops | bytes accessed | tf_op | source)
XLA Modules:
  0.0 441.7 jit_solution(4667769530827201996)
XLA Ops:
  10.6 22.3 %collective-permute-start.7 = (f32[2,128,128]{2,1,0:T(8,128)S(1)}, f32[2,128,128]{2,1,0:T(8,128)S(1)}, u32[]{:S(2)}, u32[]{:S(2)}) collective-permute-start(f32[2,128,128]{2,1,0:T(8,128)S(1)} %get-tuple-element.123), channel_id=1, source_target_pairs={{0,8},{8,0},{2,10},{10,2},{4,12},{12,4},{6,14},{14,6},{1,9},{9,1},... | collective-permute-start | bytes 393224 | tf_op jit(solution)/shard_map/ppermute | solution.py:73
  34.4 6.0 %collective-permute-start.22 = (f32[4,3,128,128]{3,2,1,0:T(8,128)}, f32[4,3,128,128]{3,2,1,0:T(8,128)}, u32[]{:S(2)}, u32[]{:S(2)}) collective-permute-start(f32[4,3,128,128]{3,2,1,0:T(8,128)} %get-tuple-element.116), channel_id=1, source_target_pairs={{8,2},{2,8},{10,4},{4,10},{12,6},{6,12},{9,3},{3,9},{11,5},{5,11},... | collective-permute-start | bytes 2359304 | tf_op jit(solution)/shard_map/ppermute | solution.py:73
  42.2 4.5 %collective-permute-start.8 = (f32[2,128,128]{2,1,0:T(8,128)S(1)}, f32[2,128,128]{2,1,0:T(8,128)S(1)}, u32[]{:S(2)}, u32[]{:S(2)}) collective-permute-start(f32[2,128,128]{2,1,0:T(8,128)S(1)} %get-tuple-element.122), channel_id=1, source_target_pairs={{8,2},{2,8},{10,4},{4,10},{12,6},{6,12},{9,3},{3,9},{11,5},{5,11},... | collective-permute-start | bytes 393224 | tf_op jit(solution)/shard_map/ppermute | solution.py:73
  47.9 3.8 collective-permute-done.8.hop
  53.3 2.6 collective-permute-start.25
  62.0 4.4 %all-to-all-start = ((f32[8,2,32]{2,1,0:T(2,128)}), f32[8,2,32]{2,1,0:T(2,128)S(1)}, u32[]{:S(2)}, u32[]{:S(2)}) async-start(f32[8,2,32]{2,1,0:T(2,128)} %bitcast.73), calls=%async_computation | async-start | bytes 16384 | tf_op jit(solution)/shard_map/all_to_all | solution.py:388
  70.6 4.8 %all-to-all-start.1 = ((f32[8,2,32,128]{3,2,1,0:T(8,128)}), f32[8,2,32,128]{3,2,1,0:T(8,128)S(1)}, u32[]{:S(2)}, u32[]{:S(2)}) async-start(f32[8,2,32,128]{3,2,1,0:T(8,128)} %pack.1), calls=%async_computation.1 | async-start | bytes 524288 | tf_op jit(solution)/shard_map/all_to_all | solution.py:388
  79.3 3.8 widen.3.refs_4_
  83.1 20.0 %fine_0_0.1 = (f32[4,4,128,128]{3,2,1,0:T(8,128)}, f32[4,3,128,128]{3,2,1,0:T(8,128)}, f32[4,3,128,128]{3,2,1,0:T(8,128)}, f32[4,4,128,128]{3,2,1,0:T(8,128)}) custom-call(s32[6]{0:T(128)} %stack.91.flags.refs_0_, f32[4,4,128,128]{3,2,1,0:T(8,128)} %copy-done.3, f32[4,3,128,128]{3,2,1,0:T(8,128)} %collective-permute-done.21.refs_2_, ...), custom_call_target="tpu_custom_call" | custom-call | tf_op jit(solution)/shard_map/fine_0_0/pallas_call | solution.py:457
  109.0 3.5 collective-permute-start.5
  115.9 7.9 %collective-permute-done.5.hop = f32[2,2,128,128]{3,2,1,0:T(8,128)} collective-permute-done((f32[2,2,128,128]{3,2,1,0:T(8,128)}, f32[2,2,128,128]{3,2,1,0:T(8,128)}, u32[]{:S(2)}, u32[]{:S(2)}) %collective-permute-start.5) | collective-permute-done | bytes 262176 | tf_op jit(solution)/shard_map/ppermute | solution.py:73
  129.6 12.1 %fine_0_1.1 = (f32[2,4,128,128]{3,2,1,0:T(8,128)}, f32[2,3,128,128]{3,2,1,0:T(8,128)}, f32[2,3,128,128]{3,2,1,0:T(8,128)}, f32[8,2,32,128]{3,2,1,0:T(8,128)}, f32[2,4,128,128]{3,2,1,0:T(8,128)}) custom-call(s32[6]{0:T(128)} %stack.91.flags.refs_0_, f32[2,4,128,128]{3,2,1,0:T(8,128)} %copy-done.4, f32[2,3,128,128]{3,2,1,0:T(8,128)} %copy-done.26, ...), custom_call_target="tpu_custom_call" | custom-call | tf_op jit(solution)/shard_map/fine_0_1/pallas_call | solution.py:457
  141.6 5.7 %all-to-all-start.2 = ((f32[8,2,32,128]{3,2,1,0:T(8,128)}), f32[8,2,32,128]{3,2,1,0:T(8,128)S(1)}, u32[]{:S(2)}, u32[]{:S(2)}) async-start(f32[8,2,32,128]{3,2,1,0:T(8,128)} %get-tuple-element.62), calls=%async_computation.2 | async-start | bytes 524288 | tf_op jit(solution)/shard_map/all_to_all | solution.py:388
  150.6 11.4 %fine_1_0.1 = (f32[4,4,128,128]{3,2,1,0:T(8,128)}, f32[4,3,128,128]{3,2,1,0:T(8,128)}, f32[4,3,128,128]{3,2,1,0:T(8,128)}) custom-call(s32[6]{0:T(128)} %stack.91.flags.refs_0_, f32[4,4,128,128]{3,2,1,0:T(8,128)} %get-tuple-element.72.refs_1_, f32[4,3,128,128]{3,2,1,0:T(8,128)} %copy-done.15, f32[4,3,128,128]{3,2,1,0:T(8,128)} %copy-done.16, ...), custom_call_target="tpu_custom_call" | custom-call | tf_op jit(solution)/shard_map/fine_1_0/pallas_call | solution.py:457
  168.5 3.4 collective-permute-start.13
  172.0 4.9 %collective-permute-done.13.refs_8_ = f32[2,128,128]{2,1,0:T(8,128)S(1)} collective-permute-done((f32[2,128,128]{2,1,0:T(8,128)}, f32[2,128,128]{2,1,0:T(8,128)S(1)}, u32[]{:S(2)}, u32[]{:S(2)}) %collective-permute-start.13) | collective-permute-done | bytes 131104 | tf_op jit(solution)/shard_map/ppermute | solution.py:73
  177.5 7.7 %fine_1_1.1 = (f32[2,4,128,128]{3,2,1,0:T(8,128)}, f32[2,3,128,128]{3,2,1,0:T(8,128)}, f32[2,3,128,128]{3,2,1,0:T(8,128)}, f32[8,2,32,128]{3,2,1,0:T(8,128)}) custom-call(s32[6]{0:T(128)} %stack.91.flags.refs_0_, f32[2,4,128,128]{3,2,1,0:T(8,128)} %get-tuple-element.59.refs_1_, f32[2,3,128,128]{3,2,1,0:T(8,128)} %copy-done.27, ...), custom_call_target="tpu_custom_call" | custom-call | tf_op jit(solution)/shard_map/fine_1_1/pallas_call | solution.py:457
  185.2 5.4 %all-to-all-start.3 = ((f32[8,2,32,128]{3,2,1,0:T(8,128)}), f32[8,2,32,128]{3,2,1,0:T(8,128)S(1)}, u32[]{:S(2)}, u32[]{:S(2)}) async-start(f32[8,2,32,128]{3,2,1,0:T(8,128)} %get-tuple-element.66), calls=%async_computation.3 | async-start | bytes 524288 | tf_op jit(solution)/shard_map/all_to_all | solution.py:388
  193.9 11.4 %fine_2_0.1 = (f32[4,4,128,128]{3,2,1,0:T(8,128)}, f32[4,3,128,128]{3,2,1,0:T(8,128)}, f32[4,3,128,128]{3,2,1,0:T(8,128)}) custom-call(s32[6]{0:T(128)} %stack.91.flags.refs_0_, f32[4,4,128,128]{3,2,1,0:T(8,128)} %get-tuple-element.75.refs_1_, f32[4,3,128,128]{3,2,1,0:T(8,128)} %copy-done.17, f32[4,3,128,128]{3,2,1,0:T(8,128)} %copy-done.18, ...), custom_call_target="tpu_custom_call" | custom-call | tf_op jit(solution)/shard_map/fine_2_0/pallas_call | solution.py:457
  211.8 3.5 collective-permute-start.16
  215.3 4.9 %collective-permute-done.16.refs_8_ = f32[2,128,128]{2,1,0:T(8,128)S(1)} collective-permute-done((f32[2,128,128]{2,1,0:T(8,128)}, f32[2,128,128]{2,1,0:T(8,128)S(1)}, u32[]{:S(2)}, u32[]{:S(2)}) %collective-permute-start.16) | collective-permute-done | bytes 131104 | tf_op jit(solution)/shard_map/ppermute | solution.py:73
  220.8 7.7 %fine_2_1.1 = (f32[2,4,128,128]{3,2,1,0:T(8,128)}, f32[2,3,128,128]{3,2,1,0:T(8,128)}, f32[2,3,128,128]{3,2,1,0:T(8,128)}, f32[8,2,32,128]{3,2,1,0:T(8,128)}) custom-call(s32[6]{0:T(128)} %stack.91.flags.refs_0_, f32[2,4,128,128]{3,2,1,0:T(8,128)} %get-tuple-element.63.refs_1_, f32[2,3,128,128]{3,2,1,0:T(8,128)} %copy-done.25, ...), custom_call_target="tpu_custom_call" | custom-call | tf_op jit(solution)/shard_map/fine_2_1/pallas_call | solution.py:457
  228.5 5.4 %all-to-all-start.4 = ((f32[8,2,32,128]{3,2,1,0:T(8,128)}), f32[8,2,32,128]{3,2,1,0:T(8,128)S(1)}, u32[]{:S(2)}, u32[]{:S(2)}) async-start(f32[8,2,32,128]{3,2,1,0:T(8,128)} %get-tuple-element.70), calls=%async_computation.4 | async-start | bytes 524288 | tf_op jit(solution)/shard_map/all_to_all | solution.py:388
  236.0 5.7 %all-to-all-done.4.arrived = f32[8,2,32,128]{3,2,1,0:T(8,128)S(1)} async-done(((f32[8,2,32,128]{3,2,1,0:T(8,128)}), f32[8,2,32,128]{3,2,1,0:T(8,128)S(1)}, u32[]{:S(2)}, u32[]{:S(2)}) %all-to-all-start.4) | async-done | bytes 262176 | tf_op jit(solution)/shard_map/all_to_all | solution.py:388
  244.5 3.0 collective-permute-start.19
  247.7 2.7 collective-permute-done.19.refs_8_
  251.1 7.2 %fine_3_1.1 = f32[2,4,128,128]{3,2,1,0:T(8,128)} custom-call(s32[6]{0:T(128)} %stack.91.flags.refs_0_, f32[2,4,128,128]{3,2,1,0:T(8,128)} %get-tuple-element.67.refs_1_, f32[2,3,128,128]{3,2,1,0:T(8,128)} %copy-done.23, f32[2,3,128,128]{3,2,1,0:T(8,128)} %copy-done.24, f32[2,8,128,128]{3,2,1,0:T(8,128)} %widen.2.refs_4_, ...), custom_call_target="tpu_custom_call" | custom-call | tf_op jit(solution)/shard_map/fine_3_1/pallas_call | solution.py:457
  259.4 11.6 %fine_3_0.1 = f32[4,4,128,128]{3,2,1,0:T(8,128)} custom-call(s32[6]{0:T(128)} %stack.91.flags.refs_0_, f32[4,4,128,128]{3,2,1,0:T(8,128)} %get-tuple-element.78.refs_1_, f32[4,3,128,128]{3,2,1,0:T(8,128)} %copy-done.19, f32[4,3,128,128]{3,2,1,0:T(8,128)} %copy-done.20, f32[4,8,128,128]{3,2,1,0:T(8,128)} %widen.3.refs_4_, ...), custom_call_target="tpu_custom_call" | custom-call | tf_op jit(solution)/shard_map/fine_3_0/pallas_call | solution.py:457
  274.8 5.2 %collective-permute-start.33 = (f32[2,4,128,128]{3,2,1,0:T(8,128)S(1)}, f32[2,4,128,128]{3,2,1,0:T(8,128)S(1)}, u32[]{:S(2)}, u32[]{:S(2)}) collective-permute-start(f32[2,4,128,128]{3,2,1,0:T(8,128)S(1)} %get-tuple-element.113), channel_id=1, source_target_pairs={{0,16},{8,24},{2,18},{10,26},{4,20},{12,28},{6,22},{14,30},{16,0},... | collective-permute-start | bytes 1572872 | tf_op jit(solution)/shard_map/ppermute | solution.py:73
  282.0 18.6 %collective-permute-done.32.refs_2_.refs_7_ = f32[2,4,128,128]{3,2,1,0:T(8,128)S(1)} collective-permute-done((f32[2,4,128,128]{3,2,1,0:T(8,128)S(1)}, f32[2,4,128,128]{3,2,1,0:T(8,128)S(1)}, u32[]{:S(2)}, u32[]{:S(2)}) %collective-permute-start.32) | collective-permute-done | bytes 524320 | tf_op jit(solution)/shard_map/ppermute | solution.py:73
  311.2 3.9 collective-permute-done.36.refs_3_
  315.0 5.4 %chain_0.1 = (f32[4,128,128]{2,1,0:T(8,128)}, f32[3,128,128]{2,1,0:T(8,128)}, f32[3,128,128]{2,1,0:T(8,128)}) custom-call(s32[6]{0:T(128)} %stack.91.flags.refs_0_, f32[4,128,128]{2,1,0:T(8,128)} %get-tuple-element.82.refs_1_, f32[3,128,128]{2,1,0:T(8,128)} %collective-permute-done.35.refs_2_, f32[3,128,128]{2,1,0:T(8,128)} %collective-permute-done.36.refs_3_, ...), custom_call_target="tpu_custom_call" | custom-call | tf_op jit(solution)/shard_map/chain_0/pallas_call | solution.py:529
  325.8 4.3 collective-permute-done.38.refs_3_
  330.2 5.4 %chain_1.1 = (f32[4,128,128]{2,1,0:T(8,128)}, f32[3,128,128]{2,1,0:T(8,128)}, f32[3,128,128]{2,1,0:T(8,128)}) custom-call(s32[6]{0:T(128)} %stack.91.flags.refs_0_, f32[4,128,128]{2,1,0:T(8,128)} %get-tuple-element.85.refs_1_, f32[3,128,128]{2,1,0:T(8,128)} %collective-permute-done.37.refs_2_, f32[3,128,128]{2,1,0:T(8,128)} %collective-permute-done.38.refs_3_, ...), custom_call_target="tpu_custom_call" | custom-call | tf_op jit(solution)/shard_map/chain_1/pallas_call | solution.py:529
  340.6 4.4 collective-permute-done.40.refs_3_
  345.0 5.4 %chain_2.1 = (f32[4,128,128]{2,1,0:T(8,128)}, f32[3,128,128]{2,1,0:T(8,128)}, f32[3,128,128]{2,1,0:T(8,128)}) custom-call(s32[6]{0:T(128)} %stack.91.flags.refs_0_, f32[4,128,128]{2,1,0:T(8,128)} %get-tuple-element.88.refs_1_, f32[3,128,128]{2,1,0:T(8,128)} %collective-permute-done.39.refs_2_, f32[3,128,128]{2,1,0:T(8,128)} %collective-permute-done.40.refs_3_, ...), custom_call_target="tpu_custom_call" | custom-call | tf_op jit(solution)/shard_map/chain_2/pallas_call | solution.py:529
  355.6 4.4 collective-permute-done.42.refs_3_
  360.0 5.5 %chain_3.1 = (f32[4,128,128]{2,1,0:T(8,128)}, f32[3,128,128]{2,1,0:T(8,128)}, f32[3,128,128]{2,1,0:T(8,128)}) custom-call(s32[6]{0:T(128)} %stack.91.flags.refs_0_, f32[4,128,128]{2,1,0:T(8,128)} %get-tuple-element.91.refs_1_, f32[3,128,128]{2,1,0:T(8,128)} %collective-permute-done.41.refs_2_, f32[3,128,128]{2,1,0:T(8,128)} %collective-permute-done.42.refs_3_, ...), custom_call_target="tpu_custom_call" | custom-call | tf_op jit(solution)/shard_map/chain_3/pallas_call | solution.py:529
  370.4 4.4 collective-permute-done.44.refs_3_
  374.8 5.4 %chain_4.1 = (f32[4,128,128]{2,1,0:T(8,128)}, f32[3,128,128]{2,1,0:T(8,128)}, f32[3,128,128]{2,1,0:T(8,128)}) custom-call(s32[6]{0:T(128)} %stack.91.flags.refs_0_, f32[4,128,128]{2,1,0:T(8,128)} %get-tuple-element.94.refs_1_, f32[3,128,128]{2,1,0:T(8,128)} %collective-permute-done.43.refs_2_, f32[3,128,128]{2,1,0:T(8,128)} %collective-permute-done.44.refs_3_, ...), custom_call_target="tpu_custom_call" | custom-call | tf_op jit(solution)/shard_map/chain_4/pallas_call | solution.py:529
  385.5 4.4 collective-permute-done.46.refs_3_
  389.9 5.4 %chain_5.1 = (f32[4,128,128]{2,1,0:T(8,128)}, f32[3,128,128]{2,1,0:T(8,128)}, f32[3,128,128]{2,1,0:T(8,128)}) custom-call(s32[6]{0:T(128)} %stack.91.flags.refs_0_, f32[4,128,128]{2,1,0:T(8,128)} %get-tuple-element.97.refs_1_, f32[3,128,128]{2,1,0:T(8,128)} %collective-permute-done.45.refs_2_, f32[3,128,128]{2,1,0:T(8,128)} %collective-permute-done.46.refs_3_, ...), custom_call_target="tpu_custom_call" | custom-call | tf_op jit(solution)/shard_map/chain_5/pallas_call | solution.py:529
  400.2 4.4 collective-permute-done.48.refs_3_
  404.6 5.3 %chain_6.1 = f32[4,128,128]{2,1,0:T(8,128)} custom-call(s32[6]{0:T(128)} %stack.91.flags.refs_0_, f32[4,128,128]{2,1,0:T(8,128)} %get-tuple-element.100.refs_1_, f32[3,128,128]{2,1,0:T(8,128)} %collective-permute-done.47.refs_2_, f32[3,128,128]{2,1,0:T(8,128)} %collective-permute-done.48.refs_3_, f32[8,128,128]{2,1,0:T(8,128)} %get-tuple-element.54.refs_5_.refs_4_, ...), custom_call_target="tpu_custom_call" | custom-call | tf_op jit(solution)/shard_map/chain_6/pallas_call | solution.py:529
  412.1 4.1 collective-permute-start.52
  418.1 3.2 collective-permute-start.50
  422.1 7.6 %collective-permute-done.52 = f32[2,4,128,128]{3,2,1,0:T(8,128)S(1)} collective-permute-done((f32[2,4,128,128]{3,2,1,0:T(8,128)}, f32[2,4,128,128]{3,2,1,0:T(8,128)S(1)}, u32[]{:S(2)}, u32[]{:S(2)}) %collective-permute-start.52) | collective-permute-done | bytes 524320 | tf_op jit(solution)/shard_map/ppermute | solution.py:73
  429.7 10.4 %collective-permute-done.51 = f32[2,4,128,128]{3,2,1,0:T(8,128)S(1)} collective-permute-done((f32[2,4,128,128]{3,2,1,0:T(8,128)}, f32[2,4,128,128]{3,2,1,0:T(8,128)S(1)}, u32[]{:S(2)}, u32[]{:S(2)}) %collective-permute-start.51) | collective-permute-done | bytes 524320 | tf_op jit(solution)/shard_map/ppermute | solution.py:73
  (203 shorter events, 126.1 us)
Async XLA Ops:
  2.5 30.4 %collective-permute-start.20 = (f32[4,4,128,128]{3,2,1,0:T(8,128)}, f32[4,4,128,128]{3,2,1,0:T(8,128)S(1)}, u32[]{:S(2)}, u32[]{:S(2)}) collective-permute-start(f32[4,4,128,128]{3,2,1,0:T(8,128)} %bitcast.16), channel_id=1, source_target_pairs={{0,0},{1,8},{2,2},{3,10},{4,4},{5,12},{6,6},{7,14},{8,1},{9,9},{10... | collective-permute-start | bytes 3145736 | tf_op jit(solution)/shard_map/ppermute | solution.py:73
  5.6 36.6 %collective-permute-start.23 = (f32[4,4,128,128]{3,2,1,0:T(8,128)}, f32[4,4,128,128]{3,2,1,0:T(8,128)S(1)}, u32[]{:S(2)}, u32[]{:S(2)}) collective-permute-start(f32[4,4,128,128]{3,2,1,0:T(8,128)} %bitcast.18), channel_id=1, source_target_pairs={{0,0},{1,8},{2,2},{3,10},{4,4},{5,12},{6,6},{7,14},{8,1},{9,9},{10... | collective-permute-start | bytes 3145736 | tf_op jit(solution)/shard_map/ppermute | solution.py:73
  9.1 44.2 %collective-permute-start.3 = (f32[2,4,128,128]{3,2,1,0:T(8,128)S(1)}, f32[2,4,128,128]{3,2,1,0:T(8,128)S(1)}, u32[]{:S(2)}, u32[]{:S(2)}) collective-permute-start(f32[2,4,128,128]{3,2,1,0:T(8,128)S(1)} %slice_bitcast_fusion.2), channel_id=1, source_target_pairs={{0,0},{1,8},{2,2},{3,10},{4,4},{5,12},{6,6},{7,14},{8,1},{9,9},{10... | collective-permute-start | bytes 1572872 | tf_op jit(solution)/shard_map/ppermute | solution.py:73
  9.8 24.5 %collective-permute-start.9 = (s32[2,2,128]{2,1,0:T(2,128)S(1)}, s32[2,2,128]{2,1,0:T(2,128)S(1)}, u32[]{:S(2)}, u32[]{:S(2)}) collective-permute-start(s32[2,2,128]{2,1,0:T(2,128)S(1)} %pad_add_fusion), channel_id=1, source_target_pairs={{0,0},{1,8},{2,2},{3,10},{4,4},{5,12},{6,6},{7,14},{8,1},{9,9},{10... | collective-permute-start | bytes 6152 | tf_op jit(solution)/shard_map/ppermute | solution.py:73
  10.6 30.9 %collective-permute-start.7 = (f32[2,128,128]{2,1,0:T(8,128)S(1)}, f32[2,128,128]{2,1,0:T(8,128)S(1)}, u32[]{:S(2)}, u32[]{:S(2)}) collective-permute-start(f32[2,128,128]{2,1,0:T(8,128)S(1)} %get-tuple-element.123), channel_id=1, source_target_pairs={{0,8},{8,0},{2,10},{10,2},{4,12},{12,4},{6,14},{14,6},{1,9},{9,1},... | collective-permute-start | bytes 393224 | tf_op jit(solution)/shard_map/ppermute | solution.py:73
  34.3 48.7 %collective-permute-start.21 = (f32[4,3,128,128]{3,2,1,0:T(8,128)}, f32[4,3,128,128]{3,2,1,0:T(8,128)}, u32[]{:S(2)}, u32[]{:S(2)}) collective-permute-start(f32[4,3,128,128]{3,2,1,0:T(8,128)} %get-tuple-element.117), channel_id=1, source_target_pairs={{0,8},{8,0},{2,10},{10,2},{4,12},{12,4},{6,14},{14,6},{1,9},{9,1},... | collective-permute-start | bytes 2359304 | tf_op jit(solution)/shard_map/ppermute | solution.py:73
  34.4 48.7 %collective-permute-start.22 = (f32[4,3,128,128]{3,2,1,0:T(8,128)}, f32[4,3,128,128]{3,2,1,0:T(8,128)}, u32[]{:S(2)}, u32[]{:S(2)}) collective-permute-start(f32[4,3,128,128]{3,2,1,0:T(8,128)} %get-tuple-element.116), channel_id=1, source_target_pairs={{8,2},{2,8},{10,4},{4,10},{12,6},{6,12},{9,3},{3,9},{11,5},{5,11},... | collective-permute-start | bytes 2359304 | tf_op jit(solution)/shard_map/ppermute | solution.py:73
  41.5 15.3 %collective-permute-start = (f32[2,4,128,128]{3,2,1,0:T(8,128)S(1)}, f32[2,4,128,128]{3,2,1,0:T(8,128)S(1)}, u32[]{:S(2)}, u32[]{:S(2)}) collective-permute-start(f32[2,4,128,128]{3,2,1,0:T(8,128)S(1)} %slice_bitcast_fusion.3), channel_id=1, source_target_pairs={{0,0},{1,8},{2,2},{3,10},{4,4},{5,12},{6,6},{7,14},{8,1},{9,9},{10... | collective-permute-start | bytes 1572872 | tf_op jit(solution)/shard_map/ppermute | solution.py:73
  42.2 9.4 %collective-permute-start.8 = (f32[2,128,128]{2,1,0:T(8,128)S(1)}, f32[2,128,128]{2,1,0:T(8,128)S(1)}, u32[]{:S(2)}, u32[]{:S(2)}) collective-permute-start(f32[2,128,128]{2,1,0:T(8,128)S(1)} %get-tuple-element.122), channel_id=1, source_target_pairs={{8,2},{2,8},{10,4},{4,10},{12,6},{6,12},{9,3},{3,9},{11,5},{5,11},... | collective-permute-start | bytes 393224 | tf_op jit(solution)/shard_map/ppermute | solution.py:73
  51.7 25.9 %collective-permute-start.24 = (f32[4,2,128,128]{3,2,1,0:T(8,128)}, f32[4,2,128,128]{3,2,1,0:T(8,128)S(1)}, u32[]{:S(2)}, u32[]{:S(2)}) collective-permute-start(f32[4,2,128,128]{3,2,1,0:T(8,128)} %get-tuple-element.115), channel_id=1, source_target_pairs={{0,8},{8,0},{2,10},{10,2},{4,12},{12,4},{6,14},{14,6},{1,9},{9,1},... | collective-permute-start | bytes 1572872 | tf_op jit(solution)/shard_map/ppermute | solution.py:73
  53.3 24.2 %collective-permute-start.25 = (f32[4,2,128,128]{3,2,1,0:T(8,128)}, f32[4,2,128,128]{3,2,1,0:T(8,128)S(1)}, u32[]{:S(2)}, u32[]{:S(2)}) collective-permute-start(f32[4,2,128,128]{3,2,1,0:T(8,128)} %get-tuple-element.114), channel_id=1, source_target_pairs={{8,2},{2,8},{10,4},{4,10},{12,6},{6,12},{9,3},{3,9},{11,5},{5,11},... | collective-permute-start | bytes 1572872 | tf_op jit(solution)/shard_map/ppermute | solution.py:73
  56.8 52.2 %collective-permute-start.4 = (f32[2,2,128,128]{3,2,1,0:T(8,128)}, f32[2,2,128,128]{3,2,1,0:T(8,128)}, u32[]{:S(2)}, u32[]{:S(2)}) collective-permute-start(f32[2,2,128,128]{3,2,1,0:T(8,128)} %get-tuple-element.119), channel_id=1, source_target_pairs={{0,8},{8,0},{2,10},{10,2},{4,12},{12,4},{6,14},{14,6},{1,9},{9,1},... | collective-permute-start | bytes 786440 | tf_op jit(solution)/shard_map/ppermute | solution.py:73
  62.0 8.6 %all-to-all-start = ((f32[8,2,32]{2,1,0:T(2,128)}), f32[8,2,32]{2,1,0:T(2,128)S(1)}, u32[]{:S(2)}, u32[]{:S(2)}) async-start(f32[8,2,32]{2,1,0:T(2,128)} %bitcast.73), calls=%async_computation | async-start | bytes 16384 | tf_op jit(solution)/shard_map/all_to_all | solution.py:388
  70.6 42.6 %all-to-all-start.1 = ((f32[8,2,32,128]{3,2,1,0:T(8,128)}), f32[8,2,32,128]{3,2,1,0:T(8,128)S(1)}, u32[]{:S(2)}, u32[]{:S(2)}) async-start(f32[8,2,32,128]{3,2,1,0:T(8,128)} %pack.1), calls=%async_computation.1 | async-start | bytes 524288 | tf_op jit(solution)/shard_map/all_to_all | solution.py:388
  103.1 46.2 %collective-permute-start.26 = (f32[4,3,128,128]{3,2,1,0:T(8,128)}, f32[4,3,128,128]{3,2,1,0:T(8,128)S(1)}, u32[]{:S(2)}, u32[]{:S(2)}) collective-permute-start(f32[4,3,128,128]{3,2,1,0:T(8,128)} %get-tuple-element.73), channel_id=1, source_target_pairs={{0,8},{8,0},{2,10},{10,2},{4,12},{12,4},{6,14},{14,6},{1,9},{9,1},... | collective-permute-start | bytes 2359304 | tf_op jit(solution)/shard_map/ppermute | solution.py:73
  103.3 46.1 %collective-permute-start.27 = (f32[4,3,128,128]{3,2,1,0:T(8,128)}, f32[4,3,128,128]{3,2,1,0:T(8,128)S(1)}, u32[]{:S(2)}, u32[]{:S(2)}) collective-permute-start(f32[4,3,128,128]{3,2,1,0:T(8,128)} %get-tuple-element.74), channel_id=1, source_target_pairs={{8,2},{2,8},{10,4},{4,10},{12,6},{6,12},{9,3},{3,9},{11,5},{5,11},... | collective-permute-start | bytes 2359304 | tf_op jit(solution)/shard_map/ppermute | solution.py:73
  105.4 22.7 %collective-permute-start.1 = (f32[2,3,128,128]{3,2,1,0:T(8,128)S(1)}, f32[2,3,128,128]{3,2,1,0:T(8,128)S(1)}, u32[]{:S(2)}, u32[]{:S(2)}) collective-permute-start(f32[2,3,128,128]{3,2,1,0:T(8,128)S(1)} %get-tuple-element.121), channel_id=1, source_target_pairs={{0,8},{8,0},{2,10},{10,2},{4,12},{12,4},{6,14},{14,6},{1,9},{9,1},... | collective-permute-start | bytes 1179656 | tf_op jit(solution)/shard_map/ppermute | solution.py:73
  106.9 21.1 %collective-permute-start.2 = (f32[2,3,128,128]{3,2,1,0:T(8,128)S(1)}, f32[2,3,128,128]{3,2,1,0:T(8,128)S(1)}, u32[]{:S(2)}, u32[]{:S(2)}) collective-permute-start(f32[2,3,128,128]{3,2,1,0:T(8,128)S(1)} %get-tuple-element.120), channel_id=1, source_target_pairs={{8,2},{2,8},{10,4},{4,10},{12,6},{6,12},{9,3},{3,9},{11,5},{5,11},... | collective-permute-start | bytes 1179656 | tf_op jit(solution)/shard_map/ppermute | solution.py:73
  109.0 14.9 %collective-permute-start.5 = (f32[2,2,128,128]{3,2,1,0:T(8,128)}, f32[2,2,128,128]{3,2,1,0:T(8,128)}, u32[]{:S(2)}, u32[]{:S(2)}) collective-permute-start(f32[2,2,128,128]{3,2,1,0:T(8,128)} %get-tuple-element.118), channel_id=1, source_target_pairs={{8,2},{2,8},{10,4},{4,10},{12,6},{6,12},{9,3},{3,9},{11,5},{5,11},... | collective-permute-start | bytes 786440 | tf_op jit(solution)/shard_map/ppermute | solution.py:73
  141.6 24.0 %all-to-all-start.2 = ((f32[8,2,32,128]{3,2,1,0:T(8,128)}), f32[8,2,32,128]{3,2,1,0:T(8,128)S(1)}, u32[]{:S(2)}, u32[]{:S(2)}) async-start(f32[8,2,32,128]{3,2,1,0:T(8,128)} %get-tuple-element.62), calls=%async_computation.2 | async-start | bytes 524288 | tf_op jit(solution)/shard_map/all_to_all | solution.py:388
  147.3 24.6 %collective-permute-start.11 = (f32[2,3,128,128]{3,2,1,0:T(8,128)}, f32[2,3,128,128]{3,2,1,0:T(8,128)S(1)}, u32[]{:S(2)}, u32[]{:S(2)}) collective-permute-start(f32[2,3,128,128]{3,2,1,0:T(8,128)} %get-tuple-element.60), channel_id=1, source_target_pairs={{0,8},{8,0},{2,10},{10,2},{4,12},{12,4},{6,14},{14,6},{1,9},{9,1},... | collective-permute-start | bytes 1179656 | tf_op jit(solution)/shard_map/ppermute | solution.py:73
  147.4 24.5 %collective-permute-start.12 = (f32[2,3,128,128]{3,2,1,0:T(8,128)}, f32[2,3,128,128]{3,2,1,0:T(8,128)S(1)}, u32[]{:S(2)}, u32[]{:S(2)}) collective-permute-start(f32[2,3,128,128]{3,2,1,0:T(8,128)} %get-tuple-element.61), channel_id=1, source_target_pairs={{8,2},{2,8},{10,4},{4,10},{12,6},{6,12},{9,3},{3,9},{11,5},{5,11},... | collective-permute-start | bytes 1179656 | tf_op jit(solution)/shard_map/ppermute | solution.py:73
  162.0 30.7 %collective-permute-start.28 = (f32[4,3,128,128]{3,2,1,0:T(8,128)}, f32[4,3,128,128]{3,2,1,0:T(8,128)S(1)}, u32[]{:S(2)}, u32[]{:S(2)}) collective-permute-start(f32[4,3,128,128]{3,2,1,0:T(8,128)} %get-tuple-element.76), channel_id=1, source_target_pairs={{0,8},{8,0},{2,10},{10,2},{4,12},{12,4},{6,14},{14,6},{1,9},{9,1},... | collective-permute-start | bytes 2359304 | tf_op jit(solution)/shard_map/ppermute | solution.py:73
  163.6 29.1 %collective-permute-start.29 = (f32[4,3,128,128]{3,2,1,0:T(8,128)}, f32[4,3,128,128]{3,2,1,0:T(8,128)S(1)}, u32[]{:S(2)}, u32[]{:S(2)}) collective-permute-start(f32[4,3,128,128]{3,2,1,0:T(8,128)} %get-tuple-element.77), channel_id=1, source_target_pairs={{8,2},{2,8},{10,4},{4,10},{12,6},{6,12},{9,3},{3,9},{11,5},{5,11},... | collective-permute-start | bytes 2359304 | tf_op jit(solution)/shard_map/ppermute | solution.py:73
  168.5 8.4 %collective-permute-start.13 = (f32[2,128,128]{2,1,0:T(8,128)}, f32[2,128,128]{2,1,0:T(8,128)S(1)}, u32[]{:S(2)}, u32[]{:S(2)}) collective-permute-start(f32[2,128,128]{2,1,0:T(8,128)} %unpack.5.refs_7_), channel_id=1, source_target_pairs={{8,0},{2,8},{10,2},{4,10},{12,4},{6,12},{14,6},{9,1},{3,9},{11,3},... | collective-permute-start | bytes 393224 | tf_op jit(solution)/shard_map/ppermute | solution.py:73
  185.2 23.8 %all-to-all-start.3 = ((f32[8,2,32,128]{3,2,1,0:T(8,128)}), f32[8,2,32,128]{3,2,1,0:T(8,128)S(1)}, u32[]{:S(2)}, u32[]{:S(2)}) async-start(f32[8,2,32,128]{3,2,1,0:T(8,128)} %get-tuple-element.66), calls=%async_computation.3 | async-start | bytes 524288 | tf_op jit(solution)/shard_map/all_to_all | solution.py:388
  190.6 24.6 %collective-permute-start.14 = (f32[2,3,128,128]{3,2,1,0:T(8,128)}, f32[2,3,128,128]{3,2,1,0:T(8,128)S(1)}, u32[]{:S(2)}, u32[]{:S(2)}) collective-permute-start(f32[2,3,128,128]{3,2,1,0:T(8,128)} %get-tuple-element.64), channel_id=1, source_target_pairs={{0,8},{8,0},{2,10},{10,2},{4,12},{12,4},{6,14},{14,6},{1,9},{9,1},... | collective-permute-start | bytes 1179656 | tf_op jit(solution)/shard_map/ppermute | solution.py:73
  190.7 24.5 %collective-permute-start.15 = (f32[2,3,128,128]{3,2,1,0:T(8,128)}, f32[2,3,128,128]{3,2,1,0:T(8,128)S(1)}, u32[]{:S(2)}, u32[]{:S(2)}) collective-permute-start(f32[2,3,128,128]{3,2,1,0:T(8,128)} %get-tuple-element.65), channel_id=1, source_target_pairs={{8,2},{2,8},{10,4},{4,10},{12,6},{6,12},{9,3},{3,9},{11,5},{5,11},... | collective-permute-start | bytes 1179656 | tf_op jit(solution)/shard_map/ppermute | solution.py:73
  205.3 52.9 %collective-permute-start.30 = (f32[4,3,128,128]{3,2,1,0:T(8,128)}, f32[4,3,128,128]{3,2,1,0:T(8,128)S(1)}, u32[]{:S(2)}, u32[]{:S(2)}) collective-permute-start(f32[4,3,128,128]{3,2,1,0:T(8,128)} %get-tuple-element.79), channel_id=1, source_target_pairs={{0,8},{8,0},{2,10},{10,2},{4,12},{12,4},{6,14},{14,6},{1,9},{9,1},... | collective-permute-start | bytes 2359304 | tf_op jit(solution)/shard_map/ppermute | solution.py:73
  206.9 51.4 %collective-permute-start.31 = (f32[4,3,128,128]{3,2,1,0:T(8,128)}, f32[4,3,128,128]{3,2,1,0:T(8,128)S(1)}, u32[]{:S(2)}, u32[]{:S(2)}) collective-permute-start(f32[4,3,128,128]{3,2,1,0:T(8,128)} %get-tuple-element.80), channel_id=1, source_target_pairs={{8,2},{2,8},{10,4},{4,10},{12,6},{6,12},{9,3},{3,9},{11,5},{5,11},... | collective-permute-start | bytes 2359304 | tf_op jit(solution)/shard_map/ppermute | solution.py:73
  211.8 8.4 %collective-permute-start.16 = (f32[2,128,128]{2,1,0:T(8,128)}, f32[2,128,128]{2,1,0:T(8,128)S(1)}, u32[]{:S(2)}, u32[]{:S(2)}) collective-permute-start(f32[2,128,128]{2,1,0:T(8,128)} %unpack.6.refs_7_), channel_id=1, source_target_pairs={{8,0},{2,8},{10,2},{4,10},{12,4},{6,12},{14,6},{9,1},{3,9},{11,3},... | collective-permute-start | bytes 393224 | tf_op jit(solution)/shard_map/ppermute | solution.py:73
  228.5 13.2 %all-to-all-start.4 = ((f32[8,2,32,128]{3,2,1,0:T(8,128)}), f32[8,2,32,128]{3,2,1,0:T(8,128)S(1)}, u32[]{:S(2)}, u32[]{:S(2)}) async-start(f32[8,2,32,128]{3,2,1,0:T(8,128)} %get-tuple-element.70), calls=%async_computation.4 | async-start | bytes 524288 | tf_op jit(solution)/shard_map/all_to_all | solution.py:388
  234.0 13.7 %collective-permute-start.17 = (f32[2,3,128,128]{3,2,1,0:T(8,128)}, f32[2,3,128,128]{3,2,1,0:T(8,128)S(1)}, u32[]{:S(2)}, u32[]{:S(2)}) collective-permute-start(f32[2,3,128,128]{3,2,1,0:T(8,128)} %get-tuple-element.68), channel_id=1, source_target_pairs={{0,8},{8,0},{2,10},{10,2},{4,12},{12,4},{6,14},{14,6},{1,9},{9,1},... | collective-permute-start | bytes 1179656 | tf_op jit(solution)/shard_map/ppermute | solution.py:73
  234.1 13.6 %collective-permute-start.18 = (f32[2,3,128,128]{3,2,1,0:T(8,128)}, f32[2,3,128,128]{3,2,1,0:T(8,128)S(1)}, u32[]{:S(2)}, u32[]{:S(2)}) collective-permute-start(f32[2,3,128,128]{3,2,1,0:T(8,128)} %get-tuple-element.69), channel_id=1, source_target_pairs={{8,2},{2,8},{10,4},{4,10},{12,6},{6,12},{9,3},{3,9},{11,5},{5,11},... | collective-permute-start | bytes 1179656 | tf_op jit(solution)/shard_map/ppermute | solution.py:73
  273.5 27.0 %collective-permute-start.32 = (f32[2,4,128,128]{3,2,1,0:T(8,128)S(1)}, f32[2,4,128,128]{3,2,1,0:T(8,128)S(1)}, u32[]{:S(2)}, u32[]{:S(2)}) collective-permute-start(f32[2,4,128,128]{3,2,1,0:T(8,128)S(1)} %get-tuple-element.112), channel_id=1, source_target_pairs={{0,1},{8,9},{2,3},{10,11},{4,5},{12,13},{6,7},{14,15},{1,0},{9,8},... | collective-permute-start | bytes 1572872 | tf_op jit(solution)/shard_map/ppermute | solution.py:73
  274.8 25.7 %collective-permute-start.33 = (f32[2,4,128,128]{3,2,1,0:T(8,128)S(1)}, f32[2,4,128,128]{3,2,1,0:T(8,128)S(1)}, u32[]{:S(2)}, u32[]{:S(2)}) collective-permute-start(f32[2,4,128,128]{3,2,1,0:T(8,128)S(1)} %get-tuple-element.113), channel_id=1, source_target_pairs={{0,16},{8,24},{2,18},{10,26},{4,20},{12,28},{6,22},{14,30},{16,0},... | collective-permute-start | bytes 1572872 | tf_op jit(solution)/shard_map/ppermute | solution.py:73
  280.0 22.4 %collective-permute-start.34 = (f32[2,4,128,128]{3,2,1,0:T(8,128)S(1)}, f32[2,4,128,128]{3,2,1,0:T(8,128)S(1)}, u32[]{:S(2)}, u32[]{:S(2)}) collective-permute-start(f32[2,4,128,128]{3,2,1,0:T(8,128)S(1)} %get-tuple-element.110), channel_id=1, source_target_pairs={{1,16},{9,24},{3,18},{11,26},{5,20},{13,28},{7,22},{15,30},{16,1},... | collective-permute-start | bytes 1572872 | tf_op jit(solution)/shard_map/ppermute | solution.py:73
  307.7 7.3 %collective-permute-start.36 = (f32[3,128,128]{2,1,0:T(8,128)}, f32[3,128,128]{2,1,0:T(8,128)}, u32[]{:S(2)}, u32[]{:S(2)}) collective-permute-start(f32[3,128,128]{2,1,0:T(8,128)} %get-tuple-element.84), channel_id=1, source_target_pairs={{8,2},{2,8},{10,4},{4,10},{12,6},{6,12},{9,3},{3,9},{11,5},{5,11},... | collective-permute-start | bytes 589832 | tf_op jit(solution)/shard_map/ppermute | solution.py:73
  322.9 7.3 %collective-permute-start.38 = (f32[3,128,128]{2,1,0:T(8,128)}, f32[3,128,128]{2,1,0:T(8,128)}, u32[]{:S(2)}, u32[]{:S(2)}) collective-permute-start(f32[3,128,128]{2,1,0:T(8,128)} %get-tuple-element.87), channel_id=1, source_target_pairs={{8,2},{2,8},{10,4},{4,10},{12,6},{6,12},{9,3},{3,9},{11,5},{5,11},... | collective-permute-start | bytes 589832 | tf_op jit(solution)/shard_map/ppermute | solution.py:73
  337.7 7.3 %collective-permute-start.40 = (f32[3,128,128]{2,1,0:T(8,128)}, f32[3,128,128]{2,1,0:T(8,128)}, u32[]{:S(2)}, u32[]{:S(2)}) collective-permute-start(f32[3,128,128]{2,1,0:T(8,128)} %get-tuple-element.90), channel_id=1, source_target_pairs={{8,2},{2,8},{10,4},{4,10},{12,6},{6,12},{9,3},{3,9},{11,5},{5,11},... | collective-permute-start | bytes 589832 | tf_op jit(solution)/shard_map/ppermute | solution.py:73
  352.7 7.3 %collective-permute-start.42 = (f32[3,128,128]{2,1,0:T(8,128)}, f32[3,128,128]{2,1,0:T(8,128)}, u32[]{:S(2)}, u32[]{:S(2)}) collective-permute-start(f32[3,128,128]{2,1,0:T(8,128)} %get-tuple-element.93), channel_id=1, source_target_pairs={{8,2},{2,8},{10,4},{4,10},{12,6},{6,12},{9,3},{3,9},{11,5},{5,11},... | collective-permute-start | bytes 589832 | tf_op jit(solution)/shard_map/ppermute | solution.py:73
  367.5 7.3 %collective-permute-start.44 = (f32[3,128,128]{2,1,0:T(8,128)}, f32[3,128,128]{2,1,0:T(8,128)}, u32[]{:S(2)}, u32[]{:S(2)}) collective-permute-start(f32[3,128,128]{2,1,0:T(8,128)} %get-tuple-element.96), channel_id=1, source_target_pairs={{8,2},{2,8},{10,4},{4,10},{12,6},{6,12},{9,3},{3,9},{11,5},{5,11},... | collective-permute-start | bytes 589832 | tf_op jit(solution)/shard_map/ppermute | solution.py:73
  382.6 7.3 %collective-permute-start.46 = (f32[3,128,128]{2,1,0:T(8,128)}, f32[3,128,128]{2,1,0:T(8,128)}, u32[]{:S(2)}, u32[]{:S(2)}) collective-permute-start(f32[3,128,128]{2,1,0:T(8,128)} %get-tuple-element.99), channel_id=1, source_target_pairs={{8,2},{2,8},{10,4},{4,10},{12,6},{6,12},{9,3},{3,9},{11,5},{5,11},... | collective-permute-start | bytes 589832 | tf_op jit(solution)/shard_map/ppermute | solution.py:73
  397.3 7.3 %collective-permute-start.48 = (f32[3,128,128]{2,1,0:T(8,128)}, f32[3,128,128]{2,1,0:T(8,128)}, u32[]{:S(2)}, u32[]{:S(2)}) collective-permute-start(f32[3,128,128]{2,1,0:T(8,128)} %get-tuple-element.102), channel_id=1, source_target_pairs={{8,2},{2,8},{10,4},{4,10},{12,6},{6,12},{9,3},{3,9},{11,5},{5,11},... | collective-permute-start | bytes 589832 | tf_op jit(solution)/shard_map/ppermute | solution.py:73
  412.1 17.6 %collective-permute-start.52 = (f32[2,4,128,128]{3,2,1,0:T(8,128)}, f32[2,4,128,128]{3,2,1,0:T(8,128)S(1)}, u32[]{:S(2)}, u32[]{:S(2)}) collective-permute-start(f32[2,4,128,128]{3,2,1,0:T(8,128)} %get-tuple-element.107), channel_id=1, source_target_pairs={{0,24},{8,25},{2,26},{10,27},{4,28},{12,29},{6,30},{14,31},{1,16},... | collective-permute-start | bytes 1572872 | tf_op jit(solution)/shard_map/ppermute | solution.py:73
  416.2 23.9 %collective-permute-start.51 = (f32[2,4,128,128]{3,2,1,0:T(8,128)}, f32[2,4,128,128]{3,2,1,0:T(8,128)S(1)}, u32[]{:S(2)}, u32[]{:S(2)}) collective-permute-start(f32[2,4,128,128]{3,2,1,0:T(8,128)} %get-tuple-element.108), channel_id=1, source_target_pairs={{0,16},{8,17},{2,18},{10,19},{4,20},{12,21},{6,22},{14,23},{1,24},... | collective-permute-start | bytes 1572872 | tf_op jit(solution)/shard_map/ppermute | solution.py:73
  418.1 22.0 %collective-permute-start.50 = (f32[2,4,128,128]{3,2,1,0:T(8,128)S(1)}, f32[2,4,128,128]{3,2,1,0:T(8,128)S(1)}, u32[]{:S(2)}, u32[]{:S(2)}) collective-permute-start(f32[2,4,128,128]{3,2,1,0:T(8,128)S(1)} %get-tuple-element.109), channel_id=1, source_target_pairs={{0,8},{8,9},{2,10},{10,11},{4,12},{12,13},{6,14},{14,15},{1,0},{9,... | collective-permute-start | bytes 1572872 | tf_op jit(solution)/shard_map/ppermute | solution.py:73
  421.3 18.8 %collective-permute-start.49 = (f32[2,4,128,128]{3,2,1,0:T(8,128)S(1)}, f32[2,4,128,128]{3,2,1,0:T(8,128)S(1)}, u32[]{:S(2)}, u32[]{:S(2)}) collective-permute-start(f32[2,4,128,128]{3,2,1,0:T(8,128)S(1)} %get-tuple-element.106), channel_id=1, source_target_pairs={{0,0},{8,1},{2,2},{10,3},{4,4},{12,5},{6,6},{14,7},{1,8},{9,9},{3,... | collective-permute-start | bytes 1572872 | tf_op jit(solution)/shard_map/ppermute | solution.py:73
  (49 other events, 279.6 us)

commit v2 on v1

v2 whole, which is shorter than its diff:
```python
import functools

import jax
import jax.numpy as jnp
from jax import lax
from jax.experimental import pallas as pl
from jax.experimental.pallas import tpu as pltpu
from jax.sharding import PartitionSpec as P

STEPS = 4
SWEEPS = 3

inverse_step = 2.0
gap_gain = 1.0

AXES = ("tm", "space")
HIGHEST = lax.Precision.HIGHEST
PAD = 8


class Layout:
    def __init__(self, times, tiles):
        self.times, self.tiles = times, tiles
        self.all = [(t // 2, t % 2, s // 2, s % 2) for t in range(times) for s in range(tiles)]

    def number(self, ht, c, hs, y):
        return (2 * ht + c) * self.tiles + 2 * hs + y

    def at(self, block, tile):
        return self.number(block // 2, tile % 2, tile // 2, block % 2)

    def relabel(self):
        return [(self.number(h, c, z, y), self.number(h, y, z, c)) for h, c, z, y in self.all]

    def pairs(self, shift_of, blocks=None):
        found = []
        for block in range(self.times) if blocks is None else blocks:
            for tile in range(self.tiles):
                other = shift_of(tile)
                if 0 <= other < self.tiles:
                    found.append((self.at(block, tile), self.at(block, other)))
        return found

    def chip(self, blocks=None):
        return self.pairs(lambda tile: tile ^ 1, blocks)

    def hop(self, blocks=None):
        return self.pairs(lambda tile: tile + 1 if tile % 2 else tile - 1, blocks)

    def down(self):
        return self.pairs(lambda tile: tile - 1)

    def columns(self):
        return [[self.at(block, tile) for tile in range(self.tiles)] for block in range(self.times)]

    def spread(self, k, roles):
        return [
            (self.at(role ^ k, tile), self.at(role, tile))
            for role in roles
            for tile in range(self.tiles)
            if role ^ k < self.times
        ]

    def gather(self, block):
        return [(self.at(block, tile), self.at(0, tile)) for tile in range(self.tiles)]

    def home(self, k, roles):
        return [
            (self.at(role, tile), (role ^ k) * self.tiles + tile)
            for role in range(roles)
            for tile in range(self.tiles)
            if role ^ k < self.times - 1
        ]

    def home_last(self, role):
        return [
            (self.at(role, tile), (self.times - 1) * self.tiles + tile)
            for tile in range(self.tiles)
        ]


def send(value, pairs):
    return lax.ppermute(value, AXES, pairs)


def f32(*shape):
    return jax.ShapeDtypeStruct(shape, jnp.float32)


def whole(*shape):
    return pl.BlockSpec(shape, lambda i: (0,) * len(shape))


def each(*shape):
    return pl.BlockSpec((None,) + shape, lambda i: (i,) + (0,) * len(shape))


SCALARS = pl.BlockSpec(memory_space=pltpu.SMEM)


def run(kernel, name, grid, in_specs, out_specs, out_shape, scratch=()):
    return pl.pallas_call(
        kernel,
        grid=(grid,),
        in_specs=in_specs,
        out_specs=out_specs,
        out_shape=out_shape,
        scratch_shapes=list(scratch),
        name=name,
    )


def join(flags, own, chip, hop, put):
    wide, count = chip.shape[0], own.shape[0]
    put(wide, own)

    @pl.when(flags[0] == 0)
    def _():
        put(0, hop)
        put(wide + count, chip)

    @pl.when(flags[0] != 0)
    def _():
        put(0, chip)
        put(wide + count, hop)


def extend_kernel(flags, own, chip, hop, out):
    def put(start, ref):
        out[start : start + ref.shape[0]] = ref[...]

    join(flags, own, chip, hop, put)


def widen_kernel(flags, own, chip, hop, inv, out):
    def put(start, ref):
        stop = start + ref.shape[0]
        out[start:stop] = ref[...] * inv[start:stop]

    join(flags, own, chip, hop, put)


def conduct_kernel(flags, own, chip, hop, fine_rate, fine_inv, coarse_rate, coarse_inv):
    def put(start, ref):
        fine_rate[start : start + ref.shape[0]] = ref[...]

    join(flags, own, chip, hop, put)
    wide, count = chip.shape[0], own.shape[0]
    for plane in range(2 * wide + count):
        inside = 1
        if plane < wide:
            inside = flags[1]
        elif plane >= wide + count:
            inside = flags[2]
        mask = jnp.full(own.shape[1:], inside, jnp.int32) != 0
        rate = inverse_step * fine_rate[plane]
        inv = jnp.where(mask, 1.0 / (rate + 6.0), 0.0)
        fine_inv[plane] = inv
        fine_rate[plane] = rate * inv
        rate = rate / STEPS
        inv = jnp.where(mask, 1.0 / (rate + 6.0), 0.0)
        coarse_inv[plane] = inv
        coarse_rate[plane] = rate * inv


def sweep(src, base, inv, low, high, emit):
    rows, lanes = inv.shape[1:]
    lane = lax.broadcasted_iota(jnp.int32, (rows, lanes), 1)
    left_edge, right_edge = lane == 0, lane == lanes - 1
    for p in range(low, high):
        mid = src[p, PAD : PAD + rows, :]
        total = src[p - 1, PAD : PAD + rows, :] + src[p + 1, PAD : PAD + rows, :]
        total = total + (src[p, PAD - 1 : PAD - 1 + rows, :] + src[p, PAD + 1 : PAD + 1 + rows, :])
        left = jnp.where(left_edge, 0.0, pltpu.roll(mid, 1, 1))
        right = jnp.where(right_edge, 0.0, pltpu.roll(mid, lanes - 1, 1))
        emit(p, base(p - 1, mid) + (total + (left + right)) * inv[p - 1])


def three(start, work, other, keep, first_base, inv, finish):
    planes, rows = start.shape[0], inv.shape[1]

    def make(p, mid):
        value = first_base(p, mid)
        if 1 <= p < inv.shape[0] - 1:
            keep[p] = value
        return value

    def to(buffer):
        def emit(p, value):
            buffer[p, PAD : PAD + rows, :] = value

        return emit

    sweep(start, make, inv, 1, planes - 1, to(work))
    sweep(work, lambda p, mid: keep[p], inv, 2, planes - 2, to(other))
    sweep(other, lambda p, mid: keep[p], inv, SWEEPS, planes - SWEEPS, lambda p, v: finish(p - SWEEPS, v))


def clear_edges(*buffers):
    for buffer in buffers:
        rows = buffer.shape[1] - 2 * PAD
        zero = jnp.zeros((buffer.shape[0], PAD, buffer.shape[2]), jnp.float32)
        buffer[:, 0:PAD, :] = zero
        buffer[:, PAD + rows :, :] = zero


def load_field(flags, own, chip, hop, buffer):
    rows = own.shape[1]

    def put(start, ref):
        buffer[start : start + ref.shape[0], PAD : PAD + rows, :] = ref[...]

    join(flags, own, chip, hop, put)


def emit_halos(flags, out, to_chip, to_hop):
    core = flags[0]
    to_chip[...] = out[pl.ds(1 - core, SWEEPS)]
    to_hop[...] = out[pl.ds(core, SWEEPS)]


def fine_kernel(first, last, coupled, per, *refs):
    refs = list(refs)
    flags, own, chip, hop, source, rate, inv = refs[:7]
    refs = refs[7:]
    if coupled:
        got, arrived, refs = refs[0], refs[1], refs[2:]
    if coupled and not last:
        select, refs = refs[0], refs[1:]
    if first:
        coarse_rate, coarse_inv, refs = refs[0], refs[1], refs[2:]
    if last:
        old, refs = refs[0], refs[1:]
    out, refs = refs[0], refs[1:]
    if not last:
        to_chip, to_hop, refs = refs[0], refs[1], refs[2:]
    if coupled and not last:
        packed, refs = refs[0], refs[1:]
    if first:
        old_out, refs = refs[0], refs[1:]
    one, two, other, keep = refs[:4]
    wide = (inv.shape[0] - own.shape[0]) // 2

    @pl.when(pl.program_id(0) == 0)
    def _():
        clear_edges(one, two, other)

    load_field(flags, own, chip, hop, one)
    if first:

        def put_old(p, value):
            old_out[p] = value

        three(one, two, other, keep, lambda p, mid: coarse_rate[p] * mid, coarse_inv, put_old)

    gaps = {}
    if coupled:
        for which in range(2):
            gap = unpacked(got, arrived, which, own.shape[1])
            gaps[wide + which * own.shape[0]] = gap_gain * gap

    def base(p, mid):
        value = rate[p] * mid + source[p]
        if p in gaps:
            value = value + gaps[p] * inv[p]
        return value

    factor = jnp.where(pl.program_id(0) // per == flags[4], 0.0, 1.0)

    def put(p, value):
        if last:
            value = value - factor * old[p]
        out[p] = value

    three(one, two, other, keep, base, inv, put)
    if not last:
        emit_halos(flags, out, to_chip, to_hop)
    if coupled and not last:
        pack_into(select, out, packed)


def unpacked(got, arrived, which, rows):
    slots = got.shape[1]
    want = (lax.broadcasted_iota(jnp.int32, (rows, slots), 0) + 1).astype(jnp.float32)
    receive = (want == got[which : which + 1]).astype(jnp.float32)
    values = arrived[:, which].reshape(slots, arrived.shape[-1])
    return jnp.dot(receive, values, precision=HIGHEST, preferred_element_type=jnp.float32)


def pack_into(select, field, packed):
    rows = jnp.dot(select[...], field[0], precision=HIGHEST, preferred_element_type=jnp.float32)
    tiles, _, capacity, lanes = packed.shape
    rows = rows.reshape(tiles, capacity, lanes)
    packed[:, 0] = rows
    packed[: tiles - 1, 1] = rows[1:]
    packed[tiles - 1, 1] = jnp.zeros((capacity, lanes), jnp.float32)


def pack_kernel(select, field, packed):
    pack_into(select, field, packed)


def index_kernel(tiles_count, capacity, tile, row, select, dest):
    rows = tile.shape[-1]
    slots = tiles_count * capacity
    lower = lax.broadcasted_iota(jnp.int32, (rows, rows), 0)
    upper = lax.broadcasted_iota(jnp.int32, (rows, rows), 1)
    earlier = (lower < upper).astype(jnp.float32)
    hot = lax.broadcasted_iota(jnp.int32, (tiles_count, rows), 0) == tile[...]
    hot = hot.astype(jnp.float32)
    before = jnp.dot(hot, earlier, precision=HIGHEST, preferred_element_type=jnp.float32)
    position = jnp.sum(before * hot, axis=0, keepdims=True).astype(jnp.int32)
    slot = tile[...] * capacity + position
    chosen = (lax.broadcasted_iota(jnp.int32, (slots, rows), 0) == slot).astype(jnp.float32)
    select[...] = chosen
    wanted = jnp.broadcast_to((row[...] + 1).astype(jnp.float32), (8, rows))
    found = lax.dot_general(
        wanted,
        chosen,
        (((1,), (1,)), ((), ())),
        precision=HIGHEST,
        preferred_element_type=jnp.float32,
    )
    dest[...] = found[0:1]


def start_fetch(flags, choices, buffer, sem):
    count = len(choices)
    for role, (part, index) in enumerate(choices):
        mine = flags[3] == role if role < count - 1 else flags[3] >= role

        @pl.when(mine)
        def _():
            pltpu.make_async_copy(part.at[index], buffer, sem).start()

    part, index = choices[0]
    return pltpu.make_async_copy(part.at[index], buffer, sem)


def begin_kernel(indices, *refs):
    count = len(indices)
    flags, parts = refs[0], refs[1 : 1 + count]
    out, to_chip, to_hop, sem = refs[1 + count :]
    start_fetch(flags, list(zip(parts, indices)), out, sem).wait()
    emit_halos(flags, out, to_chip, to_hop)


def chain_kernel(indices, last, *refs):
    count = len(indices)
    flags, own, chip, hop, rate, inv = refs[:6]
    parts, refs = refs[6 : 6 + count], list(refs[6 + count :])
    out, refs = refs[0], refs[1:]
    if not last:
        to_chip, to_hop, refs = refs[0], refs[1], refs[2:]
    one, two, other, keep, jump, sem = refs
    copy = start_fetch(flags, list(zip(parts, indices)), jump, sem)
    clear_edges(one, two, other)
    load_field(flags, own, chip, hop, one)

    def put(p, value):
        if p == 0:
            copy.wait()
        out[p] = value + jump[p]

    three(one, two, other, keep, lambda p, mid: rate[p] * mid, inv, put)
    if not last:
        emit_halos(flags, out, to_chip, to_hop)


def shards(states, sources, conductivity, gap_tile, gap_row):
    times, tiles = lax.axis_size("tm"), lax.axis_size("space")
    slices, comps, planes, rows, lanes = states.shape
    lay = Layout(times, tiles)
    capacity = max(2, 2 * rows // tiles)
    time_index, tile_index = lax.axis_index("tm"), lax.axis_index("space")
    core = time_index % 2
    block = 2 * (time_index // 2) + tile_index % 2
    tile = 2 * (tile_index // 2) + core
    last_slot = jnp.where(block == times - 1, slices - 1, -1)
    flags = jnp.stack(
        [
            core,
            (tile > 0).astype(jnp.int32),
            (tile < tiles - 1).astype(jnp.int32),
            block,
            last_slot,
            jnp.full((), slices, jnp.int32),
        ]
    ).astype(jnp.int32)
    relabel = lay.relabel()
    edge = SWEEPS - 1
    ext_planes = planes + 2 * edge
    buf_planes = planes + 2 * SWEEPS
    plane = (rows, lanes)

    def cut(value, start, width, axis):
        return lax.dynamic_slice_in_dim(value, start, width, axis)

    def exchange(value, width, axis):
        top = planes - width
        return (
            send(cut(value, top * (1 - core), width, axis), lay.chip()),
            send(cut(value, top * core, width, axis), lay.hop()),
        )

    tables = send(jnp.stack([gap_tile[:, :, 0], gap_row]), relabel)
    state_0 = send(states[:, 0], relabel)
    conduct = send(conductivity, relabel)
    source_0 = send(sources[:, 0], relabel)
    state_1 = send(states[:, 1:].reshape(-1, planes, *plane), relabel)
    source_1 = send(sources[:, 1:].reshape(-1, planes, *plane), relabel)

    slots = tiles * capacity
    select, dest = run(
        functools.partial(index_kernel, tiles, capacity),
        "gap_index",
        slices,
        [each(1, rows), each(1, rows)],
        [each(slots, rows), each(1, slots)],
        [f32(slices, slots, rows), f32(slices, 1, slots)],
    )(tables[0][:, None], tables[1][:, None])
    groups = lay.columns()

    def trade(value):
        return lax.all_to_all(value, AXES, 0, 0, axis_index_groups=groups, tiled=True)

    dest = jnp.swapaxes(dest.reshape(slices, tiles, capacity), 0, 1)
    above = jnp.concatenate([dest[1:], jnp.zeros_like(dest[:1])], 0)
    got = trade(jnp.stack([dest, above], 2))
    got = got.transpose(1, 2, 0, 3).reshape(slices, 2, slots)

    cond_chip, cond_hop = exchange(conduct, edge, 0)
    fine_rate, fine_inv, coarse_rate, coarse_inv = run(
        conduct_kernel,
        "conduct",
        1,
        [SCALARS, whole(planes, *plane), whole(edge, *plane), whole(edge, *plane)],
        [whole(ext_planes, *plane)] * 4,
        [f32(ext_planes, *plane)] * 4,
    )(flags, conduct, cond_chip, cond_hop)

    def widen(value):
        chip, hop = exchange(value, edge, 1)
        return run(
            widen_kernel,
            "widen",
            value.shape[0],
            [SCALARS, each(planes, *plane)]
            + [each(edge, *plane)] * 2
            + [whole(ext_planes, *plane)],
            each(ext_planes, *plane),
            f32(value.shape[0], ext_planes, *plane),
        )(flags, value, chip, hop, fine_inv)

    buffers = [pltpu.VMEM((buf_planes, rows + 2 * PAD, lanes), jnp.float32)] * 3 + [
        pltpu.VMEM((ext_planes, *plane), jnp.float32)
    ]
    packed_shape = (tiles, slices, 2, capacity, lanes)
    packed_spec = pl.BlockSpec((tiles, None, 2, capacity, lanes), lambda i: (0, i, 0, 0, 0))

    def fine(step, field, chip, hop, source, arrived=None, old=None):
        first, last = step == 0, step == STEPS - 1
        count = field.shape[0]
        coupled = arrived is not None
        args = [flags, field, chip, hop, source, fine_rate, fine_inv]
        ins = [
            SCALARS,
            each(planes, *plane),
            each(SWEEPS, *plane),
            each(SWEEPS, *plane),
            each(ext_planes, *plane),
            whole(ext_planes, *plane),
            whole(ext_planes, *plane),
        ]
        outs, shapes = [each(planes, *plane)], [f32(count, planes, *plane)]
        if coupled:
            args += [got, arrived]
            ins += [each(2, slots), packed_spec]
            if not last:
                args.append(select)
                ins.append(each(slots, rows))
        if first:
            args += [coarse_rate, coarse_inv]
            ins += [whole(ext_planes, *plane)] * 2
        if last:
            args.append(old)
            ins.append(each(planes, *plane))
        if not last:
            outs += [each(SWEEPS, *plane)] * 2
            shapes += [f32(count, SWEEPS, *plane)] * 2
            if coupled:
                outs.append(packed_spec)
                shapes.append(f32(*packed_shape))
        if first:
            outs.append(each(planes, *plane))
            shapes.append(f32(count, planes, *plane))
        return run(
            functools.partial(fine_kernel, first, last, coupled, count // slices),
            f"fine_{step}_{int(coupled)}",
            count,
            ins,
            outs,
            shapes,
            buffers,
        )(*args)

    packed = run(
        pack_kernel,
        "pack",
        slices,
        [each(slots, rows), each(planes, *plane)],
        packed_spec,
        f32(*packed_shape),
    )(select, state_0)
    field_0, (chip_0, hop_0), wide_0 = state_0, exchange(state_0, SWEEPS, 1), widen(source_0)
    field_1, (chip_1, hop_1), wide_1 = state_1, exchange(state_1, SWEEPS, 1), widen(source_1)
    old_0 = old_1 = None
    for step in range(STEPS):
        arrived = trade(packed)
        result_1 = fine(step, field_1, chip_1, hop_1, wide_1, None, old_1)
        result_0 = fine(step, field_0, chip_0, hop_0, wide_0, arrived, old_0)
        field_0, field_1 = result_0[0], result_1[0]
        if step == 0:
            old_0, old_1 = result_0[4], result_1[3]
        if step < STEPS - 1:
            packed = result_0[3]
            chip_0, hop_0 = send(result_0[1], lay.chip()), send(result_0[2], lay.hop())
            chip_1, hop_1 = send(result_1[1], lay.chip()), send(result_1[2], lay.hop())

    others = comps - 1
    by_comp = field_1.reshape(slices, others, planes, *plane)

    def component(role):
        index = jnp.clip(role - 1, 0, others - 1)
        return lax.dynamic_index_in_dim(by_comp, index, 1, keepdims=False)

    spread = {k: send(component(block ^ k), lay.spread(k, range(1, comps))) for k in range(1, times)}
    end = times - 1
    gathered = {}
    for slot in reversed(range(slices)):
        gathered[end, slot] = (send(field_0[slot : slot + 1], lay.gather(end)), 0)
    for source in range(end):
        whole_block = field_0 if source == 0 else send(field_0, lay.gather(source))
        for slot in range(slices):
            gathered[source, slot] = (whole_block, slot)

    def choices(source, slot):
        found = [gathered[source, slot]]
        for role in range(1, comps):
            if role == source:
                found.append((field_1, slot * others + role - 1))
            else:
                found.append((spread[role ^ source], slot))
        return [part for part, _ in found], [index for _, index in found]

    anywhere = [pl.BlockSpec(memory_space=pl.ANY)] * comps
    halo_specs = [whole(SWEEPS, *plane)] * 2
    halo_shapes = [f32(SWEEPS, *plane)] * 2
    dma = pltpu.SemaphoreType.DMA(())
    roles = range(comps)
    total = times * slices
    parts, indices = choices(end, slices - 1)
    new, chip, hop = run(
        functools.partial(begin_kernel, indices),
        "begin",
        1,
        [SCALARS] + anywhere,
        [whole(planes, *plane)] + halo_specs,
        [f32(planes, *plane)] + halo_shapes,
        [dma],
    )(flags, *parts)
    news = [new]
    for j in range(total - 1):
        chip, hop = send(chip, lay.chip(roles)), send(hop, lay.hop(roles))
        last = j == total - 2
        parts, indices = choices(j // slices, j % slices)
        result = run(
            functools.partial(chain_kernel, indices, last),
            f"chain_{j}",
            1,
            [SCALARS, whole(planes, *plane)]
            + halo_specs
            + [whole(ext_planes, *plane)] * 2
            + anywhere,
            [whole(planes, *plane)] + ([] if last else halo_specs),
            [f32(planes, *plane)] + ([] if last else halo_shapes),
            buffers + [pltpu.VMEM((planes, *plane), jnp.float32), dma],
        )(flags, new, chip, hop, coarse_rate, coarse_inv, *parts)
        new = result[0]
        if not last:
            chip, hop = result[1:]
        news.append(new)

    early = total - slices
    ready = jnp.stack(news[:early]).reshape(end, slices, planes, *plane)
    back = []
    for k in range(times):
        value = lax.dynamic_index_in_dim(ready, jnp.minimum(block ^ k, end - 1), 0, keepdims=False)
        back.append(send(value, lay.home(k, comps)))
    back = jnp.stack(back)
    result = []
    for comp in range(comps):
        pairs = lay.home_last(comp)
        late = jnp.stack([send(news[early + slot], pairs) for slot in range(slices)])
        soon = lax.dynamic_index_in_dim(back, time_index ^ comp, 0, keepdims=False)
        result.append(jnp.where(time_index == end, late, soon))
    return jnp.stack(result, axis=1)


def solution(mesh):
    placed = (
        P("tm", None, "space", None, None),
        P("tm", None, "space", None, None),
        P("space", None, None),
        P("tm", "space", None),
        P("tm", "space"),
    )
    return jax.shard_map(
        shards,
        mesh=mesh,
        in_specs=placed,
        out_specs=P("tm", None, "space", None, None),
        check_vma=False,
    )
```

time: 448 us -> 358 us (0.80)
  the two profiles are of different devices: /device:TPU:10 before, /device:TPU:11 now
where the time goes in v2:
time: 358 us; the launch traced here: 355 us
  starting transfers between devices  148 us (41%)
  Pallas kernels  87.6 us (24%)
  waiting for transfers between devices  76.3 us (21%)
  local copies, waits for them, and re-layouts  37.2 us (10%)
  other arithmetic  4.16 us (1%)
    ppermute x59, starting transfers between devices, send(): return lax.ppermute(value, AXES, pairs)  127 us
    ppermute x59, waiting for transfers between devices, send(): return lax.ppermute(value, AXES, pairs)  76.3 us
    pallas_call x8, Pallas kernels, fine(): run(functools.partial(fine_kernel, first, last, coupled, count // slices)...  47.7 us
    pallas_call x7, Pallas kernels, shards(): run(functools.partial(chain_kernel, indices, last), f'chain_{j}', 1, [SCA...  23.8 us
    all_to_all x5, starting transfers between devices, trade(): lax.all_to_all(value, AXES, 0, 0, axis_index_groups=groups, tiled=True)  21.4 us
    unnamed x95, local copies, waits for them, and re-layouts  18.5 us
  transfers between devices with their start and end apart: 64, of which 16 were waited for; matrix products, arithmetic and copies ran while one was open for 7% of the time, Pallas kernels for 25%

profile of v2, /device:TPU:11, one launch (start us, length us, event | category | flops | bytes accessed | tf_op | source)
XLA Modules:
  0.0 354.5 jit_solution(16312108346655286241)
XLA Ops:
  2.4 3.7 %collective-permute-start.20 = (f32[4,4,128,128]{3,2,1,0:T(8,128)}, f32[4,4,128,128]{3,2,1,0:T(8,128)S(1)}, u32[]{:S(2)}, u32[]{:S(2)}) collective-permute-start(f32[4,4,128,128]{3,2,1,0:T(8,128)} %bitcast.18), channel_id=1, source_target_pairs={{0,0},{1,8},{2,2},{3,10},{4,4},{5,12},{6,6},{7,14},{8,1},{9,9},{10... | collective-permute-start | bytes 3145736 | tf_op jit(solution)/shard_map/ppermute | solution.py:83
  11.1 3.6 %collective-permute-start.3 = (f32[2,4,128,128]{3,2,1,0:T(8,128)}, f32[2,4,128,128]{3,2,1,0:T(8,128)}, u32[]{:S(2)}, u32[]{:S(2)}) collective-permute-start(f32[2,4,128,128]{3,2,1,0:T(8,128)} %slice_bitcast_fusion), channel_id=1, source_target_pairs={{0,0},{1,8},{2,2},{3,10},{4,4},{5,12},{6,6},{7,14},{8,1},{9,9},{10... | collective-permute-start | bytes 1572872 | tf_op jit(solution)/shard_map/ppermute | solution.py:83
  16.8 3.6 %collective-permute-start.9 = (s32[2,2,128]{2,1,0:T(2,128)S(1)}, s32[2,2,128]{2,1,0:T(2,128)S(1)}, u32[]{:S(2)}, u32[]{:S(2)}) collective-permute-start(s32[2,2,128]{2,1,0:T(2,128)S(1)} %pad_add_fusion), channel_id=1, source_target_pairs={{0,0},{1,8},{2,2},{3,10},{4,4},{5,12},{6,6},{7,14},{8,1},{9,9},{10... | collective-permute-start | bytes 6152 | tf_op jit(solution)/shard_map/ppermute | solution.py:83
  20.5 20.8 %collective-permute-done.9 = s32[2,2,128]{2,1,0:T(2,128)S(1)} collective-permute-done((s32[2,2,128]{2,1,0:T(2,128)S(1)}, s32[2,2,128]{2,1,0:T(2,128)S(1)}, u32[]{:S(2)}, u32[]{:S(2)}) %collective-permute-start.9) | collective-permute-done | bytes 2080 | tf_op jit(solution)/shard_map/ppermute | solution.py:83
  41.3 3.6 %collective-permute-start.6 = (f32[4,128,128]{2,1,0:T(8,128)}, f32[4,128,128]{2,1,0:T(8,128)S(1)}, u32[]{:S(2)}, u32[]{:S(2)}) collective-permute-start(f32[4,128,128]{2,1,0:T(8,128)} %param.7), channel_id=1, source_target_pairs={{0,0},{1,8},{2,2},{3,10},{4,4},{5,12},{6,6},{7,14},{8,1},{9,9},{10... | collective-permute-start | bytes 786440 | tf_op jit(solution)/shard_map/ppermute | solution.py:83
  49.3 5.0 %all-to-all-start = ((f32[8,1,128]{2,1,0:T(1,128)}), f32[8,1,128]{2,1,0:T(1,128)S(1)}, u32[]{:S(2)}, u32[]{:S(2)}) async-start(f32[8,1,128]{2,1,0:T(1,128)} %reshape.141), calls=%async_computation | async-start | bytes 8192 | tf_op jit(solution)/shard_map/all_to_all | solution.py:425
  55.6 3.1 collective-permute-start.8
  61.0 4.3 %all-to-all-start.1 = ((f32[8,2,2,32,128]{4,3,2,1,0:T(8,128)}), f32[8,2,2,32,128]{4,3,2,1,0:T(8,128)S(1)}, u32[]{:S(2)}, u32[]{:S(2)}) async-start(f32[8,2,2,32,128]{4,3,2,1,0:T(8,128)} %pack.1), calls=%async_computation.1 | async-start | bytes 1048576 | tf_op jit(solution)/shard_map/all_to_all | solution.py:425
  67.7 3.1 collective-permute-start.5
  72.5 3.1 collective-permute-start.19
  95.6 6.2 %fine_0_1.1 = (f32[2,4,128,128]{3,2,1,0:T(8,128)}, f32[2,3,128,128]{3,2,1,0:T(8,128)}, f32[2,3,128,128]{3,2,1,0:T(8,128)}, f32[8,2,2,32,128]{4,3,2,1,0:T(8,128)}, f32[2,4,128,128]{3,2,1,0:T(8,128)}) custom-call(s32[6]{0:T(128)} %stack.115.flags.refs_0_, f32[2,4,128,128]{3,2,1,0:T(8,128)} %copy-done.4, f32[2,3,128,128]{3,2,1,0:T(8,128)} %collective-permute-done.1.refs_2_, ...), custom_call_target="tpu_custom_call" | custom-call | tf_op jit(solution)/shard_map/fine_0_1/pallas_call | solution.py:497
  101.8 3.5 all-to-all-start.2
  105.3 4.1 %widen.3.refs_4_ = f32[4,8,128,128]{3,2,1,0:T(8,128)} custom-call(s32[6]{0:T(128)} %stack.115.flags.refs_0_, f32[4,4,128,128]{3,2,1,0:T(8,128)} %copy-done.6, f32[4,2,128,128]{3,2,1,0:T(8,128)} %collective-permute-done.21.chip, f32[4,2,128,128]{3,2,1,0:T(8,128)} %collective-permute-done.22.hop, f32[8,128,128]{2,1,0:T(8,128)} %get-tuple-element.55.inv.refs_6_), custom_call_target="tpu_custom_call" | custom-call | tf_op jit(solution)/shard_map/widen/pallas_call | solution.py:444
  110.4 8.6 %fine_0_0.1 = (f32[4,4,128,128]{3,2,1,0:T(8,128)}, f32[4,3,128,128]{3,2,1,0:T(8,128)}, f32[4,3,128,128]{3,2,1,0:T(8,128)}, f32[4,4,128,128]{3,2,1,0:T(8,128)}) custom-call(s32[6]{0:T(128)} %stack.115.flags.refs_0_, f32[4,4,128,128]{3,2,1,0:T(8,128)} %copy-done.3, f32[4,3,128,128]{3,2,1,0:T(8,128)} %copy-done.15, ...), custom_call_target="tpu_custom_call" | custom-call | tf_op jit(solution)/shard_map/fine_0_0/pallas_call | solution.py:497
  122.2 3.5 collective-permute-start.11
  125.7 11.1 %collective-permute-done.11.refs_3_ = f32[2,3,128,128]{3,2,1,0:T(8,128)S(1)} collective-permute-done((f32[2,3,128,128]{3,2,1,0:T(8,128)}, f32[2,3,128,128]{3,2,1,0:T(8,128)S(1)}, u32[]{:S(2)}, u32[]{:S(2)}) %collective-permute-start.11) | collective-permute-done | bytes 393248 | tf_op jit(solution)/shard_map/ppermute | solution.py:83
  137.8 4.7 %fine_1_1.1 = (f32[2,4,128,128]{3,2,1,0:T(8,128)}, f32[2,3,128,128]{3,2,1,0:T(8,128)}, f32[2,3,128,128]{3,2,1,0:T(8,128)}, f32[8,2,2,32,128]{4,3,2,1,0:T(8,128)}) custom-call(s32[6]{0:T(128)} %stack.115.flags.refs_0_, f32[2,4,128,128]{3,2,1,0:T(8,128)} %get-tuple-element.61.refs_1_, f32[2,3,128,128]{3,2,1,0:T(8,128)} %copy-done.26, ...), custom_call_target="tpu_custom_call" | custom-call | tf_op jit(solution)/shard_map/fine_1_1/pallas_call | solution.py:497
  142.5 4.8 %all-to-all-start.3 = ((f32[8,2,2,32,128]{4,3,2,1,0:T(8,128)}), f32[8,2,2,32,128]{4,3,2,1,0:T(8,128)S(1)}, u32[]{:S(2)}, u32[]{:S(2)}) async-start(f32[8,2,2,32,128]{4,3,2,1,0:T(8,128)} %get-tuple-element.68), calls=%async_computation.3 | async-start | bytes 1048576 | tf_op jit(solution)/shard_map/all_to_all | solution.py:425
  148.4 6.5 %fine_1_0.1 = (f32[4,4,128,128]{3,2,1,0:T(8,128)}, f32[4,3,128,128]{3,2,1,0:T(8,128)}, f32[4,3,128,128]{3,2,1,0:T(8,128)}) custom-call(s32[6]{0:T(128)} %stack.115.flags.refs_0_, f32[4,4,128,128]{3,2,1,0:T(8,128)} %get-tuple-element.74.refs_1_, f32[4,3,128,128]{3,2,1,0:T(8,128)} %copy-done.16, f32[4,3,128,128]{3,2,1,0:T(8,128)} %copy-done.17, ...), custom_call_target="tpu_custom_call" | custom-call | tf_op jit(solution)/shard_map/fine_1_0/pallas_call | solution.py:497
  155.3 3.1 collective-permute-start.26
  158.5 3.5 collective-permute-start.13
  162.0 7.6 %collective-permute-done.26.refs_3_ = f32[4,3,128,128]{3,2,1,0:T(8,128)S(1)} collective-permute-done((f32[4,3,128,128]{3,2,1,0:T(8,128)}, f32[4,3,128,128]{3,2,1,0:T(8,128)S(1)}, u32[]{:S(2)}, u32[]{:S(2)}) %collective-permute-start.26) | collective-permute-done | bytes 786464 | tf_op jit(solution)/shard_map/ppermute | solution.py:83
  170.5 6.4 %fine_2_0.1 = (f32[4,4,128,128]{3,2,1,0:T(8,128)}, f32[4,3,128,128]{3,2,1,0:T(8,128)}, f32[4,3,128,128]{3,2,1,0:T(8,128)}) custom-call(s32[6]{0:T(128)} %stack.115.flags.refs_0_, f32[4,4,128,128]{3,2,1,0:T(8,128)} %get-tuple-element.77.refs_1_, f32[4,3,128,128]{3,2,1,0:T(8,128)} %copy-done.18, f32[4,3,128,128]{3,2,1,0:T(8,128)} %copy-done.19, ...), custom_call_target="tpu_custom_call" | custom-call | tf_op jit(solution)/shard_map/fine_2_0/pallas_call | solution.py:497
  176.9 3.2 collective-permute-start.28
  181.2 4.6 %fine_2_1.1 = (f32[2,4,128,128]{3,2,1,0:T(8,128)}, f32[2,3,128,128]{3,2,1,0:T(8,128)}, f32[2,3,128,128]{3,2,1,0:T(8,128)}, f32[8,2,2,32,128]{4,3,2,1,0:T(8,128)}) custom-call(s32[6]{0:T(128)} %stack.115.flags.refs_0_, f32[2,4,128,128]{3,2,1,0:T(8,128)} %get-tuple-element.65.refs_1_, f32[2,3,128,128]{3,2,1,0:T(8,128)} %copy-done.24, ...), custom_call_target="tpu_custom_call" | custom-call | tf_op jit(solution)/shard_map/fine_2_1/pallas_call | solution.py:497
  185.8 3.8 %all-to-all-start.4 = ((f32[8,2,2,32,128]{4,3,2,1,0:T(8,128)}), f32[8,2,2,32,128]{4,3,2,1,0:T(8,128)S(1)}, u32[]{:S(2)}, u32[]{:S(2)}) async-start(f32[8,2,2,32,128]{4,3,2,1,0:T(8,128)} %get-tuple-element.72), calls=%async_computation.4 | async-start | bytes 1048576 | tf_op jit(solution)/shard_map/all_to_all | solution.py:425
  190.1 3.1 collective-permute-start.15
  194.4 6.4 %fine_3_0.1.refs_7_.refs_8_ = f32[4,4,128,128]{3,2,1,0:T(8,128)} custom-call(s32[6]{0:T(128)} %stack.115.flags.refs_0_, f32[4,4,128,128]{3,2,1,0:T(8,128)} %get-tuple-element.80.refs_1_, f32[4,3,128,128]{3,2,1,0:T(8,128)} %copy-done.20, f32[4,3,128,128]{3,2,1,0:T(8,128)} %copy-done.21, f32[4,8,128,128]{3,2,1,0:T(8,128)} %widen.3.refs_4_, ...), custom_call_target="tpu_custom_call" | custom-call | tf_op jit(solution)/shard_map/fine_3_0/pallas_call | solution.py:497
  208.5 4.3 %fine_3_1.1.refs_6_ = f32[2,4,128,128]{3,2,1,0:T(8,128)} custom-call(s32[6]{0:T(128)} %stack.115.flags.refs_0_, f32[2,4,128,128]{3,2,1,0:T(8,128)} %get-tuple-element.69.refs_1_, f32[2,3,128,128]{3,2,1,0:T(8,128)} %copy-done.22, f32[2,3,128,128]{3,2,1,0:T(8,128)} %copy-done.23, f32[2,8,128,128]{3,2,1,0:T(8,128)} %widen.2.refs_4_, ...), custom_call_target="tpu_custom_call" | custom-call | tf_op jit(solution)/shard_map/fine_3_1/pallas_call | solution.py:497
  215.3 3.8 %collective-permute-start.43 = (f32[2,4,128,128]{3,2,1,0:T(8,128)}, f32[2,4,128,128]{3,2,1,0:T(8,128)S(1)}, u32[]{:S(2)}, u32[]{:S(2)}) collective-permute-start(f32[2,4,128,128]{3,2,1,0:T(8,128)} %fine_3_1.1.refs_6_), channel_id=1, source_target_pairs={{16,0},{24,8},{18,2},{26,10},{20,4},{28,12},{22,6},{30,14}} | collective-permute-start | bytes 1572872 | tf_op jit(solution)/shard_map/ppermute | solution.py:83
  227.8 3.3 collective-permute-start.32
  232.1 3.2 collective-permute-done.32.refs_3_
  235.2 3.4 chain_0.1
  240.8 3.5 collective-permute-start.34
  248.1 3.4 chain_1.1
  253.8 3.3 collective-permute-start.36
  261.1 3.4 chain_2.1
  266.6 3.5 collective-permute-start.40
  274.5 3.4 chain_3.1
  280.2 3.3 collective-permute-start.42
  288.0 3.4 chain_4.1
  293.6 3.5 collective-permute-start.45
  301.5 3.4 chain_5.1
  310.4 10.1 %collective-permute-start.53 = (f32[2,4,128,128]{3,2,1,0:T(8,128)S(1)}, f32[2,4,128,128]{3,2,1,0:T(8,128)S(1)}, u32[]{:S(2)}, u32[]{:S(2)}) collective-permute-start(f32[2,4,128,128]{3,2,1,0:T(8,128)S(1)} %get-tuple-element.110), channel_id=1, source_target_pairs={{0,16},{8,17},{2,18},{10,19},{4,20},{12,21},{6,22},{14,23},{16,0},... | collective-permute-start | bytes 1572872 | tf_op jit(solution)/shard_map/ppermute | solution.py:83
  324.7 4.4 %collective-permute-done.48.refs_3_ = f32[3,128,128]{2,1,0:T(8,128)S(1)} collective-permute-done((f32[3,128,128]{2,1,0:T(8,128)S(1)}, f32[3,128,128]{2,1,0:T(8,128)S(1)}, u32[]{:S(2)}, u32[]{:S(2)}) %collective-permute-start.48) | collective-permute-done | bytes 196640 | tf_op jit(solution)/shard_map/ppermute | solution.py:83
  331.1 3.3 chain_6.1
  334.4 3.3 collective-permute-done.46
  345.7 3.5 collective-permute-done.55
  (225 shorter events, 127.6 us)
Async XLA Ops:
  2.4 73.2 %collective-permute-start.20 = (f32[4,4,128,128]{3,2,1,0:T(8,128)}, f32[4,4,128,128]{3,2,1,0:T(8,128)S(1)}, u32[]{:S(2)}, u32[]{:S(2)}) collective-permute-start(f32[4,4,128,128]{3,2,1,0:T(8,128)} %bitcast.18), channel_id=1, source_target_pairs={{0,0},{1,8},{2,2},{3,10},{4,4},{5,12},{6,6},{7,14},{8,1},{9,9},{10... | collective-permute-start | bytes 3145736 | tf_op jit(solution)/shard_map/ppermute | solution.py:83
  7.2 63.6 %collective-permute-start.17 = (f32[4,4,128,128]{3,2,1,0:T(8,128)}, f32[4,4,128,128]{3,2,1,0:T(8,128)S(1)}, u32[]{:S(2)}, u32[]{:S(2)}) collective-permute-start(f32[4,4,128,128]{3,2,1,0:T(8,128)} %bitcast.17), channel_id=1, source_target_pairs={{0,0},{1,8},{2,2},{3,10},{4,4},{5,12},{6,6},{7,14},{8,1},{9,9},{10... | collective-permute-start | bytes 3145736 | tf_op jit(solution)/shard_map/ppermute | solution.py:83
  11.1 54.2 %collective-permute-start.3 = (f32[2,4,128,128]{3,2,1,0:T(8,128)}, f32[2,4,128,128]{3,2,1,0:T(8,128)}, u32[]{:S(2)}, u32[]{:S(2)}) collective-permute-start(f32[2,4,128,128]{3,2,1,0:T(8,128)} %slice_bitcast_fusion), channel_id=1, source_target_pairs={{0,0},{1,8},{2,2},{3,10},{4,4},{5,12},{6,6},{7,14},{8,1},{9,9},{10... | collective-permute-start | bytes 1572872 | tf_op jit(solution)/shard_map/ppermute | solution.py:83
  14.8 40.7 %collective-permute-start = (f32[2,4,128,128]{3,2,1,0:T(8,128)S(1)}, f32[2,4,128,128]{3,2,1,0:T(8,128)S(1)}, u32[]{:S(2)}, u32[]{:S(2)}) collective-permute-start(f32[2,4,128,128]{3,2,1,0:T(8,128)S(1)} %slice_bitcast_fusion.1), channel_id=1, source_target_pairs={{0,0},{1,8},{2,2},{3,10},{4,4},{5,12},{6,6},{7,14},{8,1},{9,9},{10... | collective-permute-start | bytes 1572872 | tf_op jit(solution)/shard_map/ppermute | solution.py:83
  16.8 24.5 %collective-permute-start.9 = (s32[2,2,128]{2,1,0:T(2,128)S(1)}, s32[2,2,128]{2,1,0:T(2,128)S(1)}, u32[]{:S(2)}, u32[]{:S(2)}) collective-permute-start(s32[2,2,128]{2,1,0:T(2,128)S(1)} %pad_add_fusion), channel_id=1, source_target_pairs={{0,0},{1,8},{2,2},{3,10},{4,4},{5,12},{6,6},{7,14},{8,1},{9,9},{10... | collective-permute-start | bytes 6152 | tf_op jit(solution)/shard_map/ppermute | solution.py:83
  41.3 13.1 %collective-permute-start.6 = (f32[4,128,128]{2,1,0:T(8,128)}, f32[4,128,128]{2,1,0:T(8,128)S(1)}, u32[]{:S(2)}, u32[]{:S(2)}) collective-permute-start(f32[4,128,128]{2,1,0:T(8,128)} %param.7), channel_id=1, source_target_pairs={{0,0},{1,8},{2,2},{3,10},{4,4},{5,12},{6,6},{7,14},{8,1},{9,9},{10... | collective-permute-start | bytes 786440 | tf_op jit(solution)/shard_map/ppermute | solution.py:83
  49.3 11.6 %all-to-all-start = ((f32[8,1,128]{2,1,0:T(1,128)}), f32[8,1,128]{2,1,0:T(1,128)S(1)}, u32[]{:S(2)}, u32[]{:S(2)}) async-start(f32[8,1,128]{2,1,0:T(1,128)} %reshape.141), calls=%async_computation | async-start | bytes 8192 | tf_op jit(solution)/shard_map/all_to_all | solution.py:425
  55.2 12.5 %collective-permute-start.7 = (f32[2,128,128]{2,1,0:T(8,128)}, f32[2,128,128]{2,1,0:T(8,128)S(1)}, u32[]{:S(2)}, u32[]{:S(2)}) collective-permute-start(f32[2,128,128]{2,1,0:T(8,128)} %get-tuple-element.126), channel_id=1, source_target_pairs={{0,8},{8,0},{2,10},{10,2},{4,12},{12,4},{6,14},{14,6},{1,9},{9,1},... | collective-permute-start | bytes 393224 | tf_op jit(solution)/shard_map/ppermute | solution.py:83
  55.6 16.5 %collective-permute-start.8 = (f32[2,128,128]{2,1,0:T(8,128)}, f32[2,128,128]{2,1,0:T(8,128)}, u32[]{:S(2)}, u32[]{:S(2)}) collective-permute-start(f32[2,128,128]{2,1,0:T(8,128)} %get-tuple-element.125), channel_id=1, source_target_pairs={{8,2},{2,8},{10,4},{4,10},{12,6},{6,12},{9,3},{3,9},{11,5},{5,11},... | collective-permute-start | bytes 393224 | tf_op jit(solution)/shard_map/ppermute | solution.py:83
  61.0 33.8 %all-to-all-start.1 = ((f32[8,2,2,32,128]{4,3,2,1,0:T(8,128)}), f32[8,2,2,32,128]{4,3,2,1,0:T(8,128)S(1)}, u32[]{:S(2)}, u32[]{:S(2)}) async-start(f32[8,2,2,32,128]{4,3,2,1,0:T(8,128)} %pack.1), calls=%async_computation.1 | async-start | bytes 1048576 | tf_op jit(solution)/shard_map/all_to_all | solution.py:425
  67.7 14.5 %collective-permute-start.5 = (f32[2,2,128,128]{3,2,1,0:T(8,128)S(1)}, f32[2,2,128,128]{3,2,1,0:T(8,128)S(1)}, u32[]{:S(2)}, u32[]{:S(2)}) collective-permute-start(f32[2,2,128,128]{3,2,1,0:T(8,128)S(1)} %get-tuple-element.121), channel_id=1, source_target_pairs={{8,2},{2,8},{10,4},{4,10},{12,6},{6,12},{9,3},{3,9},{11,5},{5,11},... | collective-permute-start | bytes 786440 | tf_op jit(solution)/shard_map/ppermute | solution.py:83
  70.8 11.4 %collective-permute-start.1 = (f32[2,3,128,128]{3,2,1,0:T(8,128)S(1)}, f32[2,3,128,128]{3,2,1,0:T(8,128)}, u32[]{:S(2)}, u32[]{:S(2)}) collective-permute-start(f32[2,3,128,128]{3,2,1,0:T(8,128)S(1)} %get-tuple-element.124), channel_id=1, source_target_pairs={{0,8},{8,0},{2,10},{10,2},{4,12},{12,4},{6,14},{14,6},{1,9},{9,1},... | collective-permute-start | bytes 1179656 | tf_op jit(solution)/shard_map/ppermute | solution.py:83
  72.1 37.3 %collective-permute-start.18 = (f32[4,3,128,128]{3,2,1,0:T(8,128)}, f32[4,3,128,128]{3,2,1,0:T(8,128)S(1)}, u32[]{:S(2)}, u32[]{:S(2)}) collective-permute-start(f32[4,3,128,128]{3,2,1,0:T(8,128)} %get-tuple-element.118), channel_id=1, source_target_pairs={{0,8},{8,0},{2,10},{10,2},{4,12},{12,4},{6,14},{14,6},{1,9},{9,1},... | collective-permute-start | bytes 2359304 | tf_op jit(solution)/shard_map/ppermute | solution.py:83
  72.5 36.9 %collective-permute-start.19 = (f32[4,3,128,128]{3,2,1,0:T(8,128)S(1)}, f32[4,3,128,128]{3,2,1,0:T(8,128)}, u32[]{:S(2)}, u32[]{:S(2)}) collective-permute-start(f32[4,3,128,128]{3,2,1,0:T(8,128)S(1)} %get-tuple-element.117), channel_id=1, source_target_pairs={{8,2},{2,8},{10,4},{4,10},{12,6},{6,12},{9,3},{3,9},{11,5},{5,11},... | collective-permute-start | bytes 2359304 | tf_op jit(solution)/shard_map/ppermute | solution.py:83
  75.7 19.1 %collective-permute-start.2 = (f32[2,3,128,128]{3,2,1,0:T(8,128)}, f32[2,3,128,128]{3,2,1,0:T(8,128)}, u32[]{:S(2)}, u32[]{:S(2)}) collective-permute-start(f32[2,3,128,128]{3,2,1,0:T(8,128)} %get-tuple-element.123), channel_id=1, source_target_pairs={{8,2},{2,8},{10,4},{4,10},{12,6},{6,12},{9,3},{3,9},{11,5},{5,11},... | collective-permute-start | bytes 1179656 | tf_op jit(solution)/shard_map/ppermute | solution.py:83
  82.2 23.1 %collective-permute-start.21 = (f32[4,2,128,128]{3,2,1,0:T(8,128)}, f32[4,2,128,128]{3,2,1,0:T(8,128)}, u32[]{:S(2)}, u32[]{:S(2)}) collective-permute-start(f32[4,2,128,128]{3,2,1,0:T(8,128)} %get-tuple-element.116), channel_id=1, source_target_pairs={{0,8},{8,0},{2,10},{10,2},{4,12},{12,4},{6,14},{14,6},{1,9},{9,1},... | collective-permute-start | bytes 1572872 | tf_op jit(solution)/shard_map/ppermute | solution.py:83
  82.9 22.4 %collective-permute-start.22 = (f32[4,2,128,128]{3,2,1,0:T(8,128)}, f32[4,2,128,128]{3,2,1,0:T(8,128)}, u32[]{:S(2)}, u32[]{:S(2)}) collective-permute-start(f32[4,2,128,128]{3,2,1,0:T(8,128)} %get-tuple-element.115), channel_id=1, source_target_pairs={{8,2},{2,8},{10,4},{4,10},{12,6},{6,12},{9,3},{3,9},{11,5},{5,11},... | collective-permute-start | bytes 1572872 | tf_op jit(solution)/shard_map/ppermute | solution.py:83
  101.8 35.0 %all-to-all-start.2 = ((f32[8,2,2,32,128]{4,3,2,1,0:T(8,128)}), f32[8,2,2,32,128]{4,3,2,1,0:T(8,128)S(1)}, u32[]{:S(2)}, u32[]{:S(2)}) async-start(f32[8,2,2,32,128]{4,3,2,1,0:T(8,128)} %get-tuple-element.64), calls=%async_computation.2 | async-start | bytes 1048576 | tf_op jit(solution)/shard_map/all_to_all | solution.py:425
  118.9 28.3 %collective-permute-start.23 = (f32[4,3,128,128]{3,2,1,0:T(8,128)}, f32[4,3,128,128]{3,2,1,0:T(8,128)S(1)}, u32[]{:S(2)}, u32[]{:S(2)}) collective-permute-start(f32[4,3,128,128]{3,2,1,0:T(8,128)} %get-tuple-element.75), channel_id=1, source_target_pairs={{0,8},{8,0},{2,10},{10,2},{4,12},{12,4},{6,14},{14,6},{1,9},{9,1},... | collective-permute-start | bytes 2359304 | tf_op jit(solution)/shard_map/ppermute | solution.py:83
  119.1 28.2 %collective-permute-start.24 = (f32[4,3,128,128]{3,2,1,0:T(8,128)}, f32[4,3,128,128]{3,2,1,0:T(8,128)S(1)}, u32[]{:S(2)}, u32[]{:S(2)}) collective-permute-start(f32[4,3,128,128]{3,2,1,0:T(8,128)} %get-tuple-element.76), channel_id=1, source_target_pairs={{8,2},{2,8},{10,4},{4,10},{12,6},{6,12},{9,3},{3,9},{11,5},{5,11},... | collective-permute-start | bytes 2359304 | tf_op jit(solution)/shard_map/ppermute | solution.py:83
  122.2 14.6 %collective-permute-start.11 = (f32[2,3,128,128]{3,2,1,0:T(8,128)}, f32[2,3,128,128]{3,2,1,0:T(8,128)S(1)}, u32[]{:S(2)}, u32[]{:S(2)}) collective-permute-start(f32[2,3,128,128]{3,2,1,0:T(8,128)} %get-tuple-element.63), channel_id=1, source_target_pairs={{8,2},{2,8},{10,4},{4,10},{12,6},{6,12},{9,3},{3,9},{11,5},{5,11},... | collective-permute-start | bytes 1179656 | tf_op jit(solution)/shard_map/ppermute | solution.py:83
  142.5 37.7 %all-to-all-start.3 = ((f32[8,2,2,32,128]{4,3,2,1,0:T(8,128)}), f32[8,2,2,32,128]{4,3,2,1,0:T(8,128)S(1)}, u32[]{:S(2)}, u32[]{:S(2)}) async-start(f32[8,2,2,32,128]{4,3,2,1,0:T(8,128)} %get-tuple-element.68), calls=%async_computation.3 | async-start | bytes 1048576 | tf_op jit(solution)/shard_map/all_to_all | solution.py:425
  155.3 14.3 %collective-permute-start.26 = (f32[4,3,128,128]{3,2,1,0:T(8,128)}, f32[4,3,128,128]{3,2,1,0:T(8,128)S(1)}, u32[]{:S(2)}, u32[]{:S(2)}) collective-permute-start(f32[4,3,128,128]{3,2,1,0:T(8,128)} %get-tuple-element.79), channel_id=1, source_target_pairs={{8,2},{2,8},{10,4},{4,10},{12,6},{6,12},{9,3},{3,9},{11,5},{5,11},... | collective-permute-start | bytes 2359304 | tf_op jit(solution)/shard_map/ppermute | solution.py:83
  158.4 21.7 %collective-permute-start.12 = (f32[2,3,128,128]{3,2,1,0:T(8,128)}, f32[2,3,128,128]{3,2,1,0:T(8,128)S(1)}, u32[]{:S(2)}, u32[]{:S(2)}) collective-permute-start(f32[2,3,128,128]{3,2,1,0:T(8,128)} %get-tuple-element.66), channel_id=1, source_target_pairs={{0,8},{8,0},{2,10},{10,2},{4,12},{12,4},{6,14},{14,6},{1,9},{9,1},... | collective-permute-start | bytes 1179656 | tf_op jit(solution)/shard_map/ppermute | solution.py:83
  158.5 21.7 %collective-permute-start.13 = (f32[2,3,128,128]{3,2,1,0:T(8,128)S(1)}, f32[2,3,128,128]{3,2,1,0:T(8,128)S(1)}, u32[]{:S(2)}, u32[]{:S(2)}) collective-permute-start(f32[2,3,128,128]{3,2,1,0:T(8,128)S(1)} %copy-done.42), channel_id=1, source_target_pairs={{8,2},{2,8},{10,4},{4,10},{12,6},{6,12},{9,3},{3,9},{11,5},{5,11},... | collective-permute-start | bytes 1179656 | tf_op jit(solution)/shard_map/ppermute | solution.py:83
  176.9 16.2 %collective-permute-start.27 = (f32[4,3,128,128]{3,2,1,0:T(8,128)}, f32[4,3,128,128]{3,2,1,0:T(8,128)S(1)}, u32[]{:S(2)}, u32[]{:S(2)}) collective-permute-start(f32[4,3,128,128]{3,2,1,0:T(8,128)} %get-tuple-element.81), channel_id=1, source_target_pairs={{0,8},{8,0},{2,10},{10,2},{4,12},{12,4},{6,14},{14,6},{1,9},{9,1},... | collective-permute-start | bytes 2359304 | tf_op jit(solution)/shard_map/ppermute | solution.py:83
  176.9 16.3 %collective-permute-start.28 = (f32[4,3,128,128]{3,2,1,0:T(8,128)}, f32[4,3,128,128]{3,2,1,0:T(8,128)S(1)}, u32[]{:S(2)}, u32[]{:S(2)}) collective-permute-start(f32[4,3,128,128]{3,2,1,0:T(8,128)} %get-tuple-element.82), channel_id=1, source_target_pairs={{8,2},{2,8},{10,4},{4,10},{12,6},{6,12},{9,3},{3,9},{11,5},{5,11},... | collective-permute-start | bytes 2359304 | tf_op jit(solution)/shard_map/ppermute | solution.py:83
  185.8 21.7 %all-to-all-start.4 = ((f32[8,2,2,32,128]{4,3,2,1,0:T(8,128)}), f32[8,2,2,32,128]{4,3,2,1,0:T(8,128)S(1)}, u32[]{:S(2)}, u32[]{:S(2)}) async-start(f32[8,2,2,32,128]{4,3,2,1,0:T(8,128)} %get-tuple-element.72), calls=%async_computation.4 | async-start | bytes 1048576 | tf_op jit(solution)/shard_map/all_to_all | solution.py:425
  189.7 16.3 %collective-permute-start.14 = (f32[2,3,128,128]{3,2,1,0:T(8,128)}, f32[2,3,128,128]{3,2,1,0:T(8,128)S(1)}, u32[]{:S(2)}, u32[]{:S(2)}) collective-permute-start(f32[2,3,128,128]{3,2,1,0:T(8,128)} %get-tuple-element.70), channel_id=1, source_target_pairs={{0,8},{8,0},{2,10},{10,2},{4,12},{12,4},{6,14},{14,6},{1,9},{9,1},... | collective-permute-start | bytes 1179656 | tf_op jit(solution)/shard_map/ppermute | solution.py:83
  190.1 17.5 %collective-permute-start.15 = (f32[2,3,128,128]{3,2,1,0:T(8,128)}, f32[2,3,128,128]{3,2,1,0:T(8,128)S(1)}, u32[]{:S(2)}, u32[]{:S(2)}) collective-permute-start(f32[2,3,128,128]{3,2,1,0:T(8,128)} %get-tuple-element.71), channel_id=1, source_target_pairs={{8,2},{2,8},{10,4},{4,10},{12,6},{6,12},{9,3},{3,9},{11,5},{5,11},... | collective-permute-start | bytes 1179656 | tf_op jit(solution)/shard_map/ppermute | solution.py:83
  203.3 18.3 %collective-permute-start.29 = (f32[2,4,128,128]{3,2,1,0:T(8,128)}, f32[2,4,128,128]{3,2,1,0:T(8,128)S(1)}, u32[]{:S(2)}, u32[]{:S(2)}) collective-permute-start(f32[2,4,128,128]{3,2,1,0:T(8,128)} %get-tuple-element.114), channel_id=1, source_target_pairs={{17,1},{25,9},{19,3},{27,11},{21,5},{29,13},{23,7},{31,15},{0,16},... | collective-permute-start | bytes 1572872 | tf_op jit(solution)/shard_map/ppermute | solution.py:83
  204.6 17.0 %collective-permute-start.30 = (f32[2,4,128,128]{3,2,1,0:T(8,128)}, f32[2,4,128,128]{3,2,1,0:T(8,128)S(1)}, u32[]{:S(2)}, u32[]{:S(2)}) collective-permute-start(f32[2,4,128,128]{3,2,1,0:T(8,128)} %get-tuple-element.113), channel_id=1, source_target_pairs={{0,1},{8,9},{2,3},{10,11},{4,5},{12,13},{6,7},{14,15},{17,16},{25,... | collective-permute-start | bytes 1572872 | tf_op jit(solution)/shard_map/ppermute | solution.py:83
  214.6 44.9 %collective-permute-start.37 = (f32[2,4,128,128]{3,2,1,0:T(8,128)}, f32[2,4,128,128]{3,2,1,0:T(8,128)S(1)}, u32[]{:S(2)}, u32[]{:S(2)}) collective-permute-start(f32[2,4,128,128]{3,2,1,0:T(8,128)} %fine_3_1.1.refs_6_), channel_id=1, source_target_pairs={{1,0},{9,8},{3,2},{11,10},{5,4},{13,12},{7,6},{15,14}} | collective-permute-start | bytes 1572872 | tf_op jit(solution)/shard_map/ppermute | solution.py:83
  215.3 69.2 %collective-permute-start.43 = (f32[2,4,128,128]{3,2,1,0:T(8,128)}, f32[2,4,128,128]{3,2,1,0:T(8,128)S(1)}, u32[]{:S(2)}, u32[]{:S(2)}) collective-permute-start(f32[2,4,128,128]{3,2,1,0:T(8,128)} %fine_3_1.1.refs_6_), channel_id=1, source_target_pairs={{16,0},{24,8},{18,2},{26,10},{20,4},{28,12},{22,6},{30,14}} | collective-permute-start | bytes 1572872 | tf_op jit(solution)/shard_map/ppermute | solution.py:83
  219.1 38.9 %collective-permute-start.38 = (f32[2,4,128,128]{3,2,1,0:T(8,128)}, f32[2,4,128,128]{3,2,1,0:T(8,128)S(1)}, u32[]{:S(2)}, u32[]{:S(2)}) collective-permute-start(f32[2,4,128,128]{3,2,1,0:T(8,128)} %get-tuple-element.112), channel_id=1, source_target_pairs={{16,1},{24,9},{18,3},{26,11},{20,5},{28,13},{22,7},{30,15},{1,16},... | collective-permute-start | bytes 1572872 | tf_op jit(solution)/shard_map/ppermute | solution.py:83
  251.5 7.9 %collective-permute-start.35 = (f32[3,128,128]{2,1,0:T(8,128)}, f32[3,128,128]{2,1,0:T(8,128)}, u32[]{:S(2)}, u32[]{:S(2)}) collective-permute-start(f32[3,128,128]{2,1,0:T(8,128)} %get-tuple-element.91), channel_id=1, source_target_pairs={{0,8},{8,0},{2,10},{10,2},{4,12},{12,4},{6,14},{14,6},{1,9},{9,1},... | collective-permute-start | bytes 589832 | tf_op jit(solution)/shard_map/ppermute | solution.py:83
  258.1 62.4 %collective-permute-start.49 = (f32[1,4,128,128]{3,2,1,0:T(8,128)S(1)}, f32[1,4,128,128]{3,2,1,0:T(8,128)}, u32[]{:S(2)}, u32[]{:S(2)}) collective-permute-start(f32[1,4,128,128]{3,2,1,0:T(8,128)S(1)} %get-tuple-element.119), channel_id=1, source_target_pairs={{17,0},{25,8},{19,2},{27,10},{21,4},{29,12},{23,6},{31,14}} | collective-permute-start | bytes 786440 | tf_op jit(solution)/shard_map/ppermute | solution.py:83
  304.9 16.9 %collective-permute-start.47 = (f32[3,128,128]{2,1,0:T(8,128)}, f32[3,128,128]{2,1,0:T(8,128)S(1)}, u32[]{:S(2)}, u32[]{:S(2)}) collective-permute-start(f32[3,128,128]{2,1,0:T(8,128)} %get-tuple-element.103), channel_id=1, source_target_pairs={{0,8},{8,0},{2,10},{10,2},{4,12},{12,4},{6,14},{14,6},{1,9},{9,1},... | collective-permute-start | bytes 589832 | tf_op jit(solution)/shard_map/ppermute | solution.py:83
  308.4 30.6 %collective-permute-start.51 = (f32[2,4,128,128]{3,2,1,0:T(8,128)}, f32[2,4,128,128]{3,2,1,0:T(8,128)S(1)}, u32[]{:S(2)}, u32[]{:S(2)}) collective-permute-start(f32[2,4,128,128]{3,2,1,0:T(8,128)} %get-tuple-element.108), channel_id=1, source_target_pairs={{0,0},{8,1},{2,2},{10,3},{4,4},{12,5},{6,6},{14,7},{1,8},{9,9},{3,... | collective-permute-start | bytes 1572872 | tf_op jit(solution)/shard_map/ppermute | solution.py:83
  309.7 31.3 %collective-permute-start.52 = (f32[2,4,128,128]{3,2,1,0:T(8,128)}, f32[2,4,128,128]{3,2,1,0:T(8,128)S(1)}, u32[]{:S(2)}, u32[]{:S(2)}) collective-permute-start(f32[2,4,128,128]{3,2,1,0:T(8,128)} %get-tuple-element.111), channel_id=1, source_target_pairs={{0,8},{8,9},{2,10},{10,11},{4,12},{12,13},{6,14},{14,15},{1,0},{9,... | collective-permute-start | bytes 1572872 | tf_op jit(solution)/shard_map/ppermute | solution.py:83
  310.4 31.9 %collective-permute-start.53 = (f32[2,4,128,128]{3,2,1,0:T(8,128)S(1)}, f32[2,4,128,128]{3,2,1,0:T(8,128)S(1)}, u32[]{:S(2)}, u32[]{:S(2)}) collective-permute-start(f32[2,4,128,128]{3,2,1,0:T(8,128)S(1)} %get-tuple-element.110), channel_id=1, source_target_pairs={{0,16},{8,17},{2,18},{10,19},{4,20},{12,21},{6,22},{14,23},{16,0},... | collective-permute-start | bytes 1572872 | tf_op jit(solution)/shard_map/ppermute | solution.py:83
  320.5 23.1 %collective-permute-start.54 = (f32[2,4,128,128]{3,2,1,0:T(8,128)S(1)}, f32[2,4,128,128]{3,2,1,0:T(8,128)S(1)}, u32[]{:S(2)}, u32[]{:S(2)}) collective-permute-start(f32[2,4,128,128]{3,2,1,0:T(8,128)S(1)} %get-tuple-element.109), channel_id=1, source_target_pairs={{1,16},{9,17},{3,18},{11,19},{5,20},{13,21},{7,22},{15,23},{16,8},... | collective-permute-start | bytes 1572872 | tf_op jit(solution)/shard_map/ppermute | solution.py:83
  329.8 7.9 %collective-permute-start.46 = (f32[4,128,128]{2,1,0:T(8,128)}, f32[4,128,128]{2,1,0:T(8,128)S(1)}, u32[]{:S(2)}, u32[]{:S(2)}) collective-permute-start(f32[4,128,128]{2,1,0:T(8,128)} %get-tuple-element.102.refs_1_), channel_id=1, source_target_pairs={{0,24},{8,25},{2,26},{10,27},{4,28},{12,29},{6,30},{14,31}} | collective-permute-start | bytes 786440 | tf_op jit(solution)/shard_map/ppermute | solution.py:83
  337.7 11.5 %collective-permute-start.55 = (f32[4,128,128]{2,1,0:T(8,128)}, f32[4,128,128]{2,1,0:T(8,128)}, u32[]{:S(2)}, u32[]{:S(2)}) collective-permute-start(f32[4,128,128]{2,1,0:T(8,128)} %get-tuple-element.102.refs_1_), channel_id=1, source_target_pairs={{1,24},{9,25},{3,26},{11,27},{5,28},{13,29},{7,30},{15,31}} | collective-permute-start | bytes 786440 | tf_op jit(solution)/shard_map/ppermute | solution.py:83
  339.0 10.2 %collective-permute-start.57 = (f32[4,128,128]{2,1,0:T(8,128)}, f32[4,128,128]{2,1,0:T(8,128)}, u32[]{:S(2)}, u32[]{:S(2)}) collective-permute-start(f32[4,128,128]{2,1,0:T(8,128)} %get-tuple-element.102.refs_1_), channel_id=1, source_target_pairs={{16,24},{24,25},{18,26},{26,27},{20,28},{28,29},{22,30},{30,31}} | collective-permute-start | bytes 786440 | tf_op jit(solution)/shard_map/ppermute | solution.py:83
  340.9 8.3 %collective-permute-start.50 = (f32[4,128,128]{2,1,0:T(8,128)}, f32[4,128,128]{2,1,0:T(8,128)}, u32[]{:S(2)}, u32[]{:S(2)}) collective-permute-start(f32[4,128,128]{2,1,0:T(8,128)} %chain_6.1), channel_id=1, source_target_pairs={{0,24},{8,25},{2,26},{10,27},{4,28},{12,29},{6,30},{14,31}} | collective-permute-start | bytes 786440 | tf_op jit(solution)/shard_map/ppermute | solution.py:83
  342.2 9.7 %collective-permute-start.56 = (f32[4,128,128]{2,1,0:T(8,128)}, f32[4,128,128]{2,1,0:T(8,128)S(1)}, u32[]{:S(2)}, u32[]{:S(2)}) collective-permute-start(f32[4,128,128]{2,1,0:T(8,128)} %chain_6.1), channel_id=1, source_target_pairs={{1,24},{9,25},{3,26},{11,27},{5,28},{13,29},{7,30},{15,31}} | collective-permute-start | bytes 786440 | tf_op jit(solution)/shard_map/ppermute | solution.py:83
  343.6 8.4 %collective-permute-start.58 = (f32[4,128,128]{2,1,0:T(8,128)}, f32[4,128,128]{2,1,0:T(8,128)S(1)}, u32[]{:S(2)}, u32[]{:S(2)}) collective-permute-start(f32[4,128,128]{2,1,0:T(8,128)} %chain_6.1), channel_id=1, source_target_pairs={{16,24},{24,25},{18,26},{26,27},{20,28},{28,29},{22,30},{30,31}} | collective-permute-start | bytes 786440 | tf_op jit(solution)/shard_map/ppermute | solution.py:83
  (60 other events, 273.0 us)

commit v3 on v2

--- a/solution.py
+++ b/solution.py
@@ -6,6 +6,7 @@
 from jax.experimental import pallas as pl
 from jax.experimental.pallas import tpu as pltpu
 from jax.sharding import PartitionSpec as P
+
 
 STEPS = 4
 SWEEPS = 3
@@ -61,8 +62,8 @@
             if role ^ k < self.times
         ]
 
-    def gather(self, block):
-        return [(self.at(block, tile), self.at(0, tile)) for tile in range(self.tiles)]
+    def move(self, block, role):
+        return [(self.at(block, tile), self.at(role, tile)) for tile in range(self.tiles)]
 
     def home(self, k, roles):
         return [
@@ -91,14 +92,14 @@
     return pl.BlockSpec(shape, lambda i: (0,) * len(shape))
 
 
-def each(*shape):
-    return pl.BlockSpec((None,) + shape, lambda i: (i,) + (0,) * len(shape))
+def each(*shape, at=0):
+    return pl.BlockSpec((None,) + shape, lambda i: (i + at,) + (0,) * len(shape))
 
 
 SCALARS = pl.BlockSpec(memory_space=pltpu.SMEM)
 
 
-def run(kernel, name, grid, in_specs, out_specs, out_shape, scratch=()):
+def run(kernel, grid, in_specs, out_specs, out_shape, scratch=()):
     return pl.pallas_call(
         kernel,
         grid=(grid,),
@@ -106,46 +107,39 @@
         out_specs=out_specs,
         out_shape=out_shape,
         scratch_shapes=list(scratch),
-        name=name,
     )
 
 
-def join(flags, own, chip, hop, put):
-    wide, count = chip.shape[0], own.shape[0]
-    put(wide, own)
+def join(flags, own, chip, hop, wide, put):
+    count, held = own.shape[0], chip.shape[0]
+    put(wide, own[...])
 
     @pl.when(flags[0] == 0)
     def _():
-        put(0, hop)
-        put(wide + count, chip)
+        put(0, hop[held - wide :])
+        put(wide + count, chip[:wide])
 
     @pl.when(flags[0] != 0)
     def _():
-        put(0, chip)
-        put(wide + count, hop)
-
-
-def extend_kernel(flags, own, chip, hop, out):
-    def put(start, ref):
-        out[start : start + ref.shape[0]] = ref[...]
-
-    join(flags, own, chip, hop, put)
+        put(0, chip[held - wide :])
+        put(wide + count, hop[:wide])
 
 
 def widen_kernel(flags, own, chip, hop, inv, out):
-    def put(start, ref):
-        stop = start + ref.shape[0]
-        out[start:stop] = ref[...] * inv[start:stop]
-
-    join(flags, own, chip, hop, put)
+    def put(start, planes):
+        stop = start + planes.shape[0]
+        out[start:stop] = planes * inv[start:stop]
+
+    join(flags, own, chip, hop, (out.shape[0] - own.shape[0]) // 2, put)
 
 
 def conduct_kernel(flags, own, chip, hop, fine_rate, fine_inv, coarse_rate, coarse_inv):
-    def put(start, ref):
-        fine_rate[start : start + ref.shape[0]] = ref[...]
-
-    join(flags, own, chip, hop, put)
-    wide, count = chip.shape[0], own.shape[0]
+    def put(start, planes):
+        fine_rate[start : start + planes.shape[0]] = planes
+
+    count = own.shape[0]
+    wide = (fine_rate.shape[0] - count) // 2
+    join(flags, own, chip, hop, wide, put)
     for plane in range(2 * wide + count):
         inside = 1
         if plane < wide:
@@ -207,10 +201,10 @@
 def load_field(flags, own, chip, hop, buffer):
     rows = own.shape[1]
 
-    def put(start, ref):
-        buffer[start : start + ref.shape[0], PAD : PAD + rows, :] = ref[...]
-
-    join(flags, own, chip, hop, put)
+    def put(start, planes):
+        buffer[start : start + planes.shape[0], PAD : PAD + rows, :] = planes
+
+    join(flags, own, chip, hop, chip.shape[0], put)
 
 
 def emit_halos(flags, out, to_chip, to_hop):
@@ -388,8 +382,7 @@
         ]
     ).astype(jnp.int32)
     relabel = lay.relabel()
-    edge = SWEEPS - 1
-    ext_planes = planes + 2 * edge
+    ext_planes = planes + 2 * (SWEEPS - 1)
     buf_planes = planes + 2 * SWEEPS
     plane = (rows, lanes)
 
@@ -404,16 +397,15 @@
         )
 
     tables = send(jnp.stack([gap_tile[:, :, 0], gap_row]), relabel)
-    state_0 = send(states[:, 0], relabel)
-    conduct = send(conductivity, relabel)
-    source_0 = send(sources[:, 0], relabel)
-    state_1 = send(states[:, 1:].reshape(-1, planes, *plane), relabel)
-    source_1 = send(sources[:, 1:].reshape(-1, planes, *plane), relabel)
+    all_0 = jnp.concatenate([states[:, 0], sources[:, 0], conductivity[None]], 0)
+    all_0 = send(all_0, relabel)
+    flat = (slices * (comps - 1), planes) + plane
+    all_1 = jnp.concatenate([states[:, 1:].reshape(flat), sources[:, 1:].reshape(flat)], 0)
+    all_1 = send(all_1, relabel)
 
     slots = tiles * capacity
     select, dest = run(
         functools.partial(index_kernel, tiles, capacity),
-        "gap_index",
         slices,
         [each(1, rows), each(1, rows)],
         [each(slots, rows), each(1, slots)],
@@ -429,28 +421,29 @@
     got = trade(jnp.stack([dest, above], 2))
     got = got.transpose(1, 2, 0, 3).reshape(slices, 2, slots)
 
-    cond_chip, cond_hop = exchange(conduct, edge, 0)
+    chip_0, hop_0 = exchange(all_0, SWEEPS, 1)
+    chip_1, hop_1 = exchange(all_1, SWEEPS, 1)
+    count_0, count_1 = slices, slices * (comps - 1)
+
+    def parts_of(at):
+        return [each(planes, *plane, at=at)] + [each(SWEEPS, *plane, at=at)] * 2
+
     fine_rate, fine_inv, coarse_rate, coarse_inv = run(
         conduct_kernel,
-        "conduct",
         1,
-        [SCALARS, whole(planes, *plane), whole(edge, *plane), whole(edge, *plane)],
+        [SCALARS] + parts_of(2 * count_0),
         [whole(ext_planes, *plane)] * 4,
         [f32(ext_planes, *plane)] * 4,
-    )(flags, conduct, cond_chip, cond_hop)
-
-    def widen(value):
-        chip, hop = exchange(value, edge, 1)
+    )(flags, all_0, chip_0, hop_0)
+
+    def widen(fields, chip, hop, count):
         return run(
             widen_kernel,
-            "widen",
-            value.shape[0],
-            [SCALARS, each(planes, *plane)]
-            + [each(edge, *plane)] * 2
-            + [whole(ext_planes, *plane)],
+            count,
+            [SCALARS] + parts_of(count) + [whole(ext_planes, *plane)],
             each(ext_planes, *plane),
-            f32(value.shape[0], ext_planes, *plane),
-        )(flags, value, chip, hop, fine_inv)
+            f32(count, ext_planes, *plane),
+        )(flags, fields, chip, hop, fine_inv)
 
     buffers = [pltpu.VMEM((buf_planes, rows + 2 * PAD, lanes), jnp.float32)] * 3 + [
         pltpu.VMEM((ext_planes, *plane), jnp.float32)
@@ -458,9 +451,8 @@
     packed_shape = (tiles, slices, 2, capacity, lanes)
     packed_spec = pl.BlockSpec((tiles, None, 2, capacity, lanes), lambda i: (0, i, 0, 0, 0))
 
-    def fine(step, field, chip, hop, source, arrived=None, old=None):
+    def fine(step, count, field, chip, hop, source, arrived=None, old=None):
         first, last = step == 0, step == STEPS - 1
-        count = field.shape[0]
         coupled = arrived is not None
         args = [flags, field, chip, hop, source, fine_rate, fine_inv]
         ins = [
@@ -496,7 +488,6 @@
             shapes.append(f32(count, planes, *plane))
         return run(
             functools.partial(fine_kernel, first, last, coupled, count // slices),
-            f"fine_{step}_{int(coupled)}",
             count,
             ins,
             outs,
@@ -506,19 +497,18 @@
 
     packed = run(
         pack_kernel,
-        "pack",
         slices,
         [each(slots, rows), each(planes, *plane)],
         packed_spec,
         f32(*packed_shape),
-    )(select, state_0)
-    field_0, (chip_0, hop_0), wide_0 = state_0, exchange(state_0, SWEEPS, 1), widen(source_0)
-    field_1, (chip_1, hop_1), wide_1 = state_1, exchange(state_1, SWEEPS, 1), widen(source_1)
+    )(select, all_0)
+    field_0, wide_0 = all_0, widen(all_0, chip_0, hop_0, count_0)
+    field_1, wide_1 = all_1, widen(all_1, chip_1, hop_1, count_1)
     old_0 = old_1 = None
     for step in range(STEPS):
         arrived = trade(packed)
-        result_1 = fine(step, field_1, chip_1, hop_1, wide_1, None, old_1)
-        result_0 = fine(step, field_0, chip_0, hop_0, wide_0, arrived, old_0)
+        result_0 = fine(step, count_0, field_0, chip_0, hop_0, wide_0, arrived, old_0)
+        result_1 = fine(step, count_1, field_1, chip_1, hop_1, wide_1, None, old_1)
         field_0, field_1 = result_0[0], result_1[0]
         if step == 0:
             old_0, old_1 = result_0[4], result_1[3]
@@ -534,15 +524,25 @@
         index = jnp.clip(role - 1, 0, others - 1)
         return lax.dynamic_index_in_dim(by_comp, index, 1, keepdims=False)
 
-    spread = {k: send(component(block ^ k), lay.spread(k, range(1, comps))) for k in range(1, times)}
     end = times - 1
+    final = {}
+    for role in range(comps):
+        if role == 0:
+            value = field_0[slices - 1 : slices]
+        else:
+            at = (slices - 1) * others + role - 1
+            value = field_1[at : at + 1]
+        final[role] = send(value, lay.move(end, role))
     gathered = {}
-    for slot in reversed(range(slices)):
-        gathered[end, slot] = (send(field_0[slot : slot + 1], lay.gather(end)), 0)
     for source in range(end):
-        whole_block = field_0 if source == 0 else send(field_0, lay.gather(source))
+        whole_block = field_0 if source == 0 else send(field_0, lay.move(source, 0))
         for slot in range(slices):
             gathered[source, slot] = (whole_block, slot)
+    for slot in range(slices - 1):
+        gathered[end, slot] = (send(field_0[slot : slot + 1], lay.move(end, 0)), 0)
+    spread = {
+        k: send(component(block ^ k), lay.spread(k, range(1, comps))) for k in range(1, times)
+    }
 
     def choices(source, slot):
         found = [gathered[source, slot]]
@@ -559,10 +559,9 @@
     dma = pltpu.SemaphoreType.DMA(())
     roles = range(comps)
     total = times * slices
-    parts, indices = choices(end, slices - 1)
+    parts, indices = [final[role] for role in range(comps)], [0] * comps
     new, chip, hop = run(
         functools.partial(begin_kernel, indices),
-        "begin",
         1,
         [SCALARS] + anywhere,
         [whole(planes, *plane)] + halo_specs,
@@ -576,7 +575,6 @@
         parts, indices = choices(j // slices, j % slices)
         result = run(
             functools.partial(chain_kernel, indices, last),
-            f"chain_{j}",
             1,
             [SCALARS, whole(planes, *plane)]
             + halo_specs
@@ -615,6 +613,7 @@
         P("tm", "space", None),
         P("tm", "space"),
     )
+
     return jax.shard_map(
         shards,
         mesh=mesh,

time: 358 us -> 383 us (1.070)
  waiting for transfers between devices: 76.3 us -> 117 us
  starting transfers between devices: 148 us -> 130 us
    ppermute x59 -> x52, waiting for transfers between devices: 76.3 us -> 97 us  [send(): return lax.ppermute(value, AXES, pairs)]
    all_to_all x5, waiting for transfers between devices: 0.01 us -> 20.4 us  [trade(): lax.all_to_all(value, AXES, 0, 0, axis_index_groups=groups, tiled=True)]
    ppermute x59 -> x52, starting transfers between devices: 127 us -> 106 us  [send(): return lax.ppermute(value, AXES, pairs)]
    unnamed x95 -> x101, local copies, waits for them, and re-layouts: 18.5 us -> 21.6 us
  transfers between devices with their start and end apart: 64 -> 57, of which waited for: 16 -> 17; matrix products, arithmetic and copies ran while one was open for 7% -> 6% of each run, Pallas kernels for 25% -> 23%
where the time goes in v3:
time: 383 us; the launch traced here: 380 us
  starting transfers between devices  130 us (34%)
  waiting for transfers between devices  117 us (31%)
  Pallas kernels  88 us (23%)
  local copies, waits for them, and re-layouts  36.4 us (10%)
  other arithmetic  6.65 us (2%)
    ppermute x52, starting transfers between devices, send(): return lax.ppermute(value, AXES, pairs)  106 us
    ppermute x52, waiting for transfers between devices, send(): return lax.ppermute(value, AXES, pairs)  97 us
    pallas_call x8, Pallas kernels, fine(): run(functools.partial(fine_kernel, first, last, coupled, count // slices)...  47.8 us
    all_to_all x5, starting transfers between devices, trade(): lax.all_to_all(value, AXES, 0, 0, axis_index_groups=groups, tiled=True)  24.2 us
    pallas_call x7, Pallas kernels, shards(): run(functools.partial(chain_kernel, indices, last), 1, [SCALARS, whole(pl...  23.9 us
    unnamed x101, local copies, waits for them, and re-layouts  21.6 us
    all_to_all x5, waiting for transfers between devices, trade(): lax.all_to_all(value, AXES, 0, 0, axis_index_groups=groups, tiled=True)  20.4 us
  transfers between devices with their start and end apart: 57, of which 17 were waited for; matrix products, arithmetic and copies ran while one was open for 6% of the time, Pallas kernels for 23%

profile of v3, /device:TPU:11, one launch (start us, length us, event | category | flops | bytes accessed | tf_op | source)
XLA Modules:
  0.0 379.9 jit_solution(7386972425349031204)
XLA Ops:
  3.0 3.8 %collective-permute-start.11 = (f32[8,4,128,128]{3,2,1,0:T(8,128)}, f32[8,4,128,128]{3,2,1,0:T(8,128)S(1)}, u32[]{:S(2)}, u32[]{:S(2)}) collective-permute-start(f32[8,4,128,128]{3,2,1,0:T(8,128)} %pad_maximum_fusion), channel_id=1, source_target_pairs={{0,0},{1,8},{2,2},{3,10},{4,4},{5,12},{6,6},{7,14},{8,1},{9,9},{10... | collective-permute-start | bytes 6291464 | tf_op jit(solution)/shard_map/ppermute | solution.py:84
  10.1 3.6 collective-permute-start.3
  13.8 31.1 %collective-permute-done.3 = s32[2,2,128]{2,1,0:T(2,128)S(1)} collective-permute-done((s32[2,2,128]{2,1,0:T(2,128)S(1)}, s32[2,2,128]{2,1,0:T(2,128)S(1)}, u32[]{:S(2)}, u32[]{:S(2)}) %collective-permute-start.3) | collective-permute-done | bytes 2080 | tf_op jit(solution)/shard_map/ppermute | solution.py:84
  50.2 3.6 collective-permute-start.2
  56.2 3.6 collective-permute-start.13
  60.5 3.8 %all-to-all-start = ((f32[8,1,128]{2,1,0:T(1,128)}), f32[8,1,128]{2,1,0:T(1,128)S(1)}, u32[]{:S(2)}, u32[]{:S(2)}) async-start(f32[8,1,128]{2,1,0:T(1,128)} %reshape.141), calls=%async_computation | async-start | bytes 8192 | tf_op jit(solution)/shard_map/all_to_all | solution.py:417
  66.6 17.2 %all-to-all-done = f32[8,1,128]{2,1,0:T(1,128)S(1)} async-done(((f32[8,1,128]{2,1,0:T(1,128)}), f32[8,1,128]{2,1,0:T(1,128)S(1)}, u32[]{:S(2)}, u32[]{:S(2)}) %all-to-all-start) | async-done | bytes 4128 | tf_op jit(solution)/shard_map/all_to_all | solution.py:417
  83.8 5.2 %all-to-all-start.1 = ((f32[8,2,2,32,128]{4,3,2,1,0:T(8,128)}), f32[8,2,2,32,128]{4,3,2,1,0:T(8,128)S(1)}, u32[]{:S(2)}, u32[]{:S(2)}) async-start(f32[8,2,2,32,128]{4,3,2,1,0:T(8,128)} %shard_map.58), calls=%async_computation.1 | async-start | bytes 1048576 | tf_op jit(solution)/shard_map/all_to_all | solution.py:417
  97.5 3.2 all-to-all-done.1.refs_8_
  101.5 6.2 %shard_map.59 = (f32[2,4,128,128]{3,2,1,0:T(8,128)}, f32[2,3,128,128]{3,2,1,0:T(8,128)}, f32[2,3,128,128]{3,2,1,0:T(8,128)}, f32[8,2,2,32,128]{4,3,2,1,0:T(8,128)}, f32[2,4,128,128]{3,2,1,0:T(8,128)}) custom-call(s32[6]{0:T(128)} %stack.115.flags.refs_0_, f32[5,4,128,128]{3,2,1,0:T(8,128)} %copy-done.1, f32[5,3,128,128]{3,2,1,0:T(8,128)} %copy-done.3, ...), custom_call_target="tpu_custom_call" | custom-call | tf_op jit(solution)/shard_map/pallas_call | solution.py:489
  107.7 7.0 %all-to-all-start.2 = ((f32[8,2,2,32,128]{4,3,2,1,0:T(8,128)}), f32[8,2,2,32,128]{4,3,2,1,0:T(8,128)S(1)}, u32[]{:S(2)}, u32[]{:S(2)}) async-start(f32[8,2,2,32,128]{4,3,2,1,0:T(8,128)} %get-tuple-element.64), calls=%async_computation.2 | async-start | bytes 1048576 | tf_op jit(solution)/shard_map/all_to_all | solution.py:417
  115.0 3.1 collective-permute-start.5
  119.4 4.2 %shard_map.63.refs_4_ = f32[4,8,128,128]{3,2,1,0:T(8,128)} custom-call(s32[6]{0:T(128)} %stack.115.flags.refs_0_, f32[8,4,128,128]{3,2,1,0:T(8,128)} %copy-done.2, f32[8,3,128,128]{3,2,1,0:T(8,128)} %copy-done.6, f32[8,3,128,128]{3,2,1,0:T(8,128)} %collective-permute-done.13.hop.refs_3_, f32[8,128,128]{2,1,0:T(8,128)} %get-tuple-element.55.inv.refs_6_), custom_call_target="tpu_custom_call" | custom-call | tf_op jit(solution)/shard_map/pallas_call | solution.py:440
  123.6 8.5 %shard_map.64 = (f32[4,4,128,128]{3,2,1,0:T(8,128)}, f32[4,3,128,128]{3,2,1,0:T(8,128)}, f32[4,3,128,128]{3,2,1,0:T(8,128)}, f32[4,4,128,128]{3,2,1,0:T(8,128)}) custom-call(s32[6]{0:T(128)} %stack.115.flags.refs_0_, f32[8,4,128,128]{3,2,1,0:T(8,128)} %copy-done.2, f32[8,3,128,128]{3,2,1,0:T(8,128)} %copy-done.6, ...), custom_call_target="tpu_custom_call" | custom-call | tf_op jit(solution)/shard_map/pallas_call | solution.py:489
  132.2 3.5 collective-permute-start.15
  136.8 4.7 %shard_map.60 = (f32[2,4,128,128]{3,2,1,0:T(8,128)}, f32[2,3,128,128]{3,2,1,0:T(8,128)}, f32[2,3,128,128]{3,2,1,0:T(8,128)}, f32[8,2,2,32,128]{4,3,2,1,0:T(8,128)}) custom-call(s32[6]{0:T(128)} %stack.115.flags.refs_0_, f32[2,4,128,128]{3,2,1,0:T(8,128)} %get-tuple-element.61.refs_1_, f32[2,3,128,128]{3,2,1,0:T(8,128)} %copy-done.22, ...), custom_call_target="tpu_custom_call" | custom-call | tf_op jit(solution)/shard_map/pallas_call | solution.py:489
  141.5 3.8 %all-to-all-start.3 = ((f32[8,2,2,32,128]{4,3,2,1,0:T(8,128)}), f32[8,2,2,32,128]{4,3,2,1,0:T(8,128)S(1)}, u32[]{:S(2)}, u32[]{:S(2)}) async-start(f32[8,2,2,32,128]{4,3,2,1,0:T(8,128)} %get-tuple-element.68), calls=%async_computation.3 | async-start | bytes 1048576 | tf_op jit(solution)/shard_map/all_to_all | solution.py:417
  146.8 6.5 %shard_map.65 = (f32[4,4,128,128]{3,2,1,0:T(8,128)}, f32[4,3,128,128]{3,2,1,0:T(8,128)}, f32[4,3,128,128]{3,2,1,0:T(8,128)}) custom-call(s32[6]{0:T(128)} %stack.115.flags.refs_0_, f32[4,4,128,128]{3,2,1,0:T(8,128)} %get-tuple-element.74.refs_1_, f32[4,3,128,128]{3,2,1,0:T(8,128)} %copy-done.18, f32[4,3,128,128]{3,2,1,0:T(8,128)} %copy-done.19, ...), custom_call_target="tpu_custom_call" | custom-call | tf_op jit(solution)/shard_map/pallas_call | solution.py:489
  153.7 3.1 collective-permute-start.17
  156.9 3.1 collective-permute-start.7
  160.0 11.5 %collective-permute-done.7.refs_3_ = f32[2,3,128,128]{3,2,1,0:T(8,128)S(1)} collective-permute-done((f32[2,3,128,128]{3,2,1,0:T(8,128)S(1)}, f32[2,3,128,128]{3,2,1,0:T(8,128)S(1)}, u32[]{:S(2)}, u32[]{:S(2)}) %collective-permute-start.7) | collective-permute-done | bytes 393248 | tf_op jit(solution)/shard_map/ppermute | solution.py:84
  172.5 4.7 %shard_map.61 = (f32[2,4,128,128]{3,2,1,0:T(8,128)}, f32[2,3,128,128]{3,2,1,0:T(8,128)}, f32[2,3,128,128]{3,2,1,0:T(8,128)}, f32[8,2,2,32,128]{4,3,2,1,0:T(8,128)}) custom-call(s32[6]{0:T(128)} %stack.115.flags.refs_0_, f32[2,4,128,128]{3,2,1,0:T(8,128)} %get-tuple-element.65.refs_1_, f32[2,3,128,128]{3,2,1,0:T(8,128)} %copy-done.24, ...), custom_call_target="tpu_custom_call" | custom-call | tf_op jit(solution)/shard_map/pallas_call | solution.py:489
  177.1 4.4 %all-to-all-start.4 = ((f32[8,2,2,32,128]{4,3,2,1,0:T(8,128)}), f32[8,2,2,32,128]{4,3,2,1,0:T(8,128)S(1)}, u32[]{:S(2)}, u32[]{:S(2)}) async-start(f32[8,2,2,32,128]{4,3,2,1,0:T(8,128)} %get-tuple-element.72), calls=%async_computation.4 | async-start | bytes 1048576 | tf_op jit(solution)/shard_map/all_to_all | solution.py:417
  182.7 6.5 %shard_map.66 = (f32[4,4,128,128]{3,2,1,0:T(8,128)}, f32[4,3,128,128]{3,2,1,0:T(8,128)}, f32[4,3,128,128]{3,2,1,0:T(8,128)}) custom-call(s32[6]{0:T(128)} %stack.115.flags.refs_0_, f32[4,4,128,128]{3,2,1,0:T(8,128)} %get-tuple-element.77.refs_1_, f32[4,3,128,128]{3,2,1,0:T(8,128)} %copy-done.16, f32[4,3,128,128]{3,2,1,0:T(8,128)} %copy-done.17, ...), custom_call_target="tpu_custom_call" | custom-call | tf_op jit(solution)/shard_map/pallas_call | solution.py:489
  189.6 3.1 collective-permute-start.19
  192.8 3.5 collective-permute-start.9
  196.2 11.6 %collective-permute-done.9.refs_3_ = f32[2,3,128,128]{3,2,1,0:T(8,128)S(1)} collective-permute-done((f32[2,3,128,128]{3,2,1,0:T(8,128)S(1)}, f32[2,3,128,128]{3,2,1,0:T(8,128)S(1)}, u32[]{:S(2)}, u32[]{:S(2)}) %collective-permute-start.9) | collective-permute-done | bytes 393248 | tf_op jit(solution)/shard_map/ppermute | solution.py:84
  208.8 4.3 %shard_map.62.refs_6_ = f32[2,4,128,128]{3,2,1,0:T(8,128)} custom-call(s32[6]{0:T(128)} %stack.115.flags.refs_0_, f32[2,4,128,128]{3,2,1,0:T(8,128)} %get-tuple-element.69.refs_1_, f32[2,3,128,128]{3,2,1,0:T(8,128)} %copy-done.25, f32[2,3,128,128]{3,2,1,0:T(8,128)} %copy-done.27, f32[2,8,128,128]{3,2,1,0:T(8,128)} %shard_map.56.refs_4_, ...), custom_call_target="tpu_custom_call" | custom-call | tf_op jit(solution)/shard_map/pallas_call | solution.py:489
  217.4 6.4 %shard_map.67.refs_7_.refs_8_ = f32[4,4,128,128]{3,2,1,0:T(8,128)} custom-call(s32[6]{0:T(128)} %stack.115.flags.refs_0_, f32[4,4,128,128]{3,2,1,0:T(8,128)} %get-tuple-element.80.refs_1_, f32[4,3,128,128]{3,2,1,0:T(8,128)} %copy-done.20, f32[4,3,128,128]{3,2,1,0:T(8,128)} %copy-done.21, f32[4,8,128,128]{3,2,1,0:T(8,128)} %shard_map.63.refs_4_, ...), custom_call_target="tpu_custom_call" | custom-call | tf_op jit(solution)/shard_map/pallas_call | solution.py:489
  232.0 6.8 %collective-permute-done.21.refs_3_ = f32[1,4,128,128]{3,2,1,0:T(8,128)} collective-permute-done((f32[1,4,128,128]{3,2,1,0:T(8,128)}, f32[1,4,128,128]{3,2,1,0:T(8,128)}, u32[]{:S(2)}, u32[]{:S(2)}) %collective-permute-start.21) | collective-permute-done | bytes 262176 | tf_op jit(solution)/shard_map/ppermute | solution.py:84
  258.4 3.4 shard_map.69
  263.8 3.5 collective-permute-start.27
  271.8 3.4 shard_map.70
  277.6 3.1 collective-permute-start.29
  285.5 3.4 shard_map.71
  290.9 3.4 collective-permute-start.33
  298.8 3.4 shard_map.72
  304.6 3.1 collective-permute-start.35
  308.7 3.1 collective-permute-done.35.refs_3_
  312.5 3.4 shard_map.73
  317.9 3.4 collective-permute-start.38
  325.8 3.4 shard_map.74
  332.9 3.6 collective-permute-start.47
  343.5 5.4 %collective-permute-done.41.refs_3_ = f32[3,128,128]{2,1,0:T(8,128)S(1)} collective-permute-done((f32[3,128,128]{2,1,0:T(8,128)S(1)}, f32[3,128,128]{2,1,0:T(8,128)S(1)}, u32[]{:S(2)}, u32[]{:S(2)}) %collective-permute-start.41) | collective-permute-done | bytes 196640 | tf_op jit(solution)/shard_map/ppermute | solution.py:84
  350.1 3.3 shard_map.75
  353.4 6.0 %collective-permute-done.39 = f32[4,128,128]{2,1,0:T(8,128)S(1)} collective-permute-done((f32[4,128,128]{2,1,0:T(8,128)}, f32[4,128,128]{2,1,0:T(8,128)S(1)}, u32[]{:S(2)}, u32[]{:S(2)}) %collective-permute-start.39) | collective-permute-done | bytes 262176 | tf_op jit(solution)/shard_map/ppermute | solution.py:84
  368.6 4.8 %collective-permute-done.48 = f32[4,128,128]{2,1,0:T(8,128)S(1)} collective-permute-done((f32[4,128,128]{2,1,0:T(8,128)}, f32[4,128,128]{2,1,0:T(8,128)S(1)}, u32[]{:S(2)}, u32[]{:S(2)}) %collective-permute-start.48) | collective-permute-done | bytes 262176 | tf_op jit(solution)/shard_map/ppermute | solution.py:84
  373.4 4.0 %collective-permute-done.49 = f32[4,128,128]{2,1,0:T(8,128)} collective-permute-done((f32[4,128,128]{2,1,0:T(8,128)}, f32[4,128,128]{2,1,0:T(8,128)}, u32[]{:S(2)}, u32[]{:S(2)}) %collective-permute-start.49) | collective-permute-done | bytes 262176 | tf_op jit(solution)/shard_map/ppermute | solution.py:84
  (218 shorter events, 119.9 us)
Async XLA Ops:
  3.0 50.8 %collective-permute-start.11 = (f32[8,4,128,128]{3,2,1,0:T(8,128)}, f32[8,4,128,128]{3,2,1,0:T(8,128)S(1)}, u32[]{:S(2)}, u32[]{:S(2)}) collective-permute-start(f32[8,4,128,128]{3,2,1,0:T(8,128)} %pad_maximum_fusion), channel_id=1, source_target_pairs={{0,0},{1,8},{2,2},{3,10},{4,4},{5,12},{6,6},{7,14},{8,1},{9,9},{10... | collective-permute-start | bytes 6291464 | tf_op jit(solution)/shard_map/ppermute | solution.py:84
  8.1 40.4 %collective-permute-start = (f32[5,4,128,128]{3,2,1,0:T(8,128)}, f32[5,4,128,128]{3,2,1,0:T(8,128)S(1)}, u32[]{:S(2)}, u32[]{:S(2)}) collective-permute-start(f32[5,4,128,128]{3,2,1,0:T(8,128)} %pad_maximum_fusion.3), channel_id=1, source_target_pairs={{0,0},{1,8},{2,2},{3,10},{4,4},{5,12},{6,6},{7,14},{8,1},{9,9},{10... | collective-permute-start | bytes 3932168 | tf_op jit(solution)/shard_map/ppermute | solution.py:84
  10.1 34.7 %collective-permute-start.3 = (s32[2,2,128]{2,1,0:T(2,128)S(1)}, s32[2,2,128]{2,1,0:T(2,128)S(1)}, u32[]{:S(2)}, u32[]{:S(2)}) collective-permute-start(s32[2,2,128]{2,1,0:T(2,128)S(1)} %pad_add_fusion), channel_id=1, source_target_pairs={{0,0},{1,8},{2,2},{3,10},{4,4},{5,12},{6,6},{7,14},{8,1},{9,9},{10... | collective-permute-start | bytes 6152 | tf_op jit(solution)/shard_map/ppermute | solution.py:84
  50.2 41.3 %collective-permute-start.1 = (f32[5,3,128,128]{3,2,1,0:T(8,128)}, f32[5,3,128,128]{3,2,1,0:T(8,128)S(1)}, u32[]{:S(2)}, u32[]{:S(2)}) collective-permute-start(f32[5,3,128,128]{3,2,1,0:T(8,128)} %get-tuple-element.115), channel_id=1, source_target_pairs={{0,8},{8,0},{2,10},{10,2},{4,12},{12,4},{6,14},{14,6},{1,9},{9,1},... | collective-permute-start | bytes 2949128 | tf_op jit(solution)/shard_map/ppermute | solution.py:84
  50.2 41.3 %collective-permute-start.2 = (f32[5,3,128,128]{3,2,1,0:T(8,128)}, f32[5,3,128,128]{3,2,1,0:T(8,128)}, u32[]{:S(2)}, u32[]{:S(2)}) collective-permute-start(f32[5,3,128,128]{3,2,1,0:T(8,128)} %get-tuple-element.114), channel_id=1, source_target_pairs={{8,2},{2,8},{10,4},{4,10},{12,6},{6,12},{9,3},{3,9},{11,5},{5,11},... | collective-permute-start | bytes 2949128 | tf_op jit(solution)/shard_map/ppermute | solution.py:84
  56.2 62.0 %collective-permute-start.12 = (f32[8,3,128,128]{3,2,1,0:T(8,128)}, f32[8,3,128,128]{3,2,1,0:T(8,128)S(1)}, u32[]{:S(2)}, u32[]{:S(2)}) collective-permute-start(f32[8,3,128,128]{3,2,1,0:T(8,128)} %get-tuple-element.109), channel_id=1, source_target_pairs={{0,8},{8,0},{2,10},{10,2},{4,12},{12,4},{6,14},{14,6},{1,9},{9,1},... | collective-permute-start | bytes 4718600 | tf_op jit(solution)/shard_map/ppermute | solution.py:84
  56.2 62.0 %collective-permute-start.13 = (f32[8,3,128,128]{3,2,1,0:T(8,128)}, f32[8,3,128,128]{3,2,1,0:T(8,128)}, u32[]{:S(2)}, u32[]{:S(2)}) collective-permute-start(f32[8,3,128,128]{3,2,1,0:T(8,128)} %get-tuple-element.108), channel_id=1, source_target_pairs={{8,2},{2,8},{10,4},{4,10},{12,6},{6,12},{9,3},{3,9},{11,5},{5,11},... | collective-permute-start | bytes 4718600 | tf_op jit(solution)/shard_map/ppermute | solution.py:84
  60.5 23.3 %all-to-all-start = ((f32[8,1,128]{2,1,0:T(1,128)}), f32[8,1,128]{2,1,0:T(1,128)S(1)}, u32[]{:S(2)}, u32[]{:S(2)}) async-start(f32[8,1,128]{2,1,0:T(1,128)} %reshape.141), calls=%async_computation | async-start | bytes 8192 | tf_op jit(solution)/shard_map/all_to_all | solution.py:417
  83.8 17.0 %all-to-all-start.1 = ((f32[8,2,2,32,128]{4,3,2,1,0:T(8,128)}), f32[8,2,2,32,128]{4,3,2,1,0:T(8,128)S(1)}, u32[]{:S(2)}, u32[]{:S(2)}) async-start(f32[8,2,2,32,128]{4,3,2,1,0:T(8,128)} %shard_map.58), calls=%async_computation.1 | async-start | bytes 1048576 | tf_op jit(solution)/shard_map/all_to_all | solution.py:417
  107.7 28.1 %all-to-all-start.2 = ((f32[8,2,2,32,128]{4,3,2,1,0:T(8,128)}), f32[8,2,2,32,128]{4,3,2,1,0:T(8,128)S(1)}, u32[]{:S(2)}, u32[]{:S(2)}) async-start(f32[8,2,2,32,128]{4,3,2,1,0:T(8,128)} %get-tuple-element.64), calls=%async_computation.2 | async-start | bytes 1048576 | tf_op jit(solution)/shard_map/all_to_all | solution.py:417
  114.7 21.1 %collective-permute-start.4 = (f32[2,3,128,128]{3,2,1,0:T(8,128)}, f32[2,3,128,128]{3,2,1,0:T(8,128)S(1)}, u32[]{:S(2)}, u32[]{:S(2)}) collective-permute-start(f32[2,3,128,128]{3,2,1,0:T(8,128)} %get-tuple-element.62), channel_id=1, source_target_pairs={{0,8},{8,0},{2,10},{10,2},{4,12},{12,4},{6,14},{14,6},{1,9},{9,1},... | collective-permute-start | bytes 1179656 | tf_op jit(solution)/shard_map/ppermute | solution.py:84
  115.0 20.7 %collective-permute-start.5 = (f32[2,3,128,128]{3,2,1,0:T(8,128)}, f32[2,3,128,128]{3,2,1,0:T(8,128)S(1)}, u32[]{:S(2)}, u32[]{:S(2)}) collective-permute-start(f32[2,3,128,128]{3,2,1,0:T(8,128)} %get-tuple-element.63), channel_id=1, source_target_pairs={{8,2},{2,8},{10,4},{4,10},{12,6},{6,12},{9,3},{3,9},{11,5},{5,11},... | collective-permute-start | bytes 1179656 | tf_op jit(solution)/shard_map/ppermute | solution.py:84
  132.2 13.2 %collective-permute-start.14 = (f32[4,3,128,128]{3,2,1,0:T(8,128)}, f32[4,3,128,128]{3,2,1,0:T(8,128)S(1)}, u32[]{:S(2)}, u32[]{:S(2)}) collective-permute-start(f32[4,3,128,128]{3,2,1,0:T(8,128)} %get-tuple-element.75), channel_id=1, source_target_pairs={{0,8},{8,0},{2,10},{10,2},{4,12},{12,4},{6,14},{14,6},{1,9},{9,1},... | collective-permute-start | bytes 2359304 | tf_op jit(solution)/shard_map/ppermute | solution.py:84
  132.2 13.6 %collective-permute-start.15 = (f32[4,3,128,128]{3,2,1,0:T(8,128)}, f32[4,3,128,128]{3,2,1,0:T(8,128)S(1)}, u32[]{:S(2)}, u32[]{:S(2)}) collective-permute-start(f32[4,3,128,128]{3,2,1,0:T(8,128)} %get-tuple-element.76), channel_id=1, source_target_pairs={{8,2},{2,8},{10,4},{4,10},{12,6},{6,12},{9,3},{3,9},{11,5},{5,11},... | collective-permute-start | bytes 2359304 | tf_op jit(solution)/shard_map/ppermute | solution.py:84
  141.5 30.1 %all-to-all-start.3 = ((f32[8,2,2,32,128]{4,3,2,1,0:T(8,128)}), f32[8,2,2,32,128]{4,3,2,1,0:T(8,128)S(1)}, u32[]{:S(2)}, u32[]{:S(2)}) async-start(f32[8,2,2,32,128]{4,3,2,1,0:T(8,128)} %get-tuple-element.68), calls=%async_computation.3 | async-start | bytes 1048576 | tf_op jit(solution)/shard_map/all_to_all | solution.py:417
  153.3 28.3 %collective-permute-start.16 = (f32[4,3,128,128]{3,2,1,0:T(8,128)}, f32[4,3,128,128]{3,2,1,0:T(8,128)S(1)}, u32[]{:S(2)}, u32[]{:S(2)}) collective-permute-start(f32[4,3,128,128]{3,2,1,0:T(8,128)} %get-tuple-element.78), channel_id=1, source_target_pairs={{0,8},{8,0},{2,10},{10,2},{4,12},{12,4},{6,14},{14,6},{1,9},{9,1},... | collective-permute-start | bytes 2359304 | tf_op jit(solution)/shard_map/ppermute | solution.py:84
  153.7 27.9 %collective-permute-start.17 = (f32[4,3,128,128]{3,2,1,0:T(8,128)}, f32[4,3,128,128]{3,2,1,0:T(8,128)S(1)}, u32[]{:S(2)}, u32[]{:S(2)}) collective-permute-start(f32[4,3,128,128]{3,2,1,0:T(8,128)} %get-tuple-element.79), channel_id=1, source_target_pairs={{8,2},{2,8},{10,4},{4,10},{12,6},{6,12},{9,3},{3,9},{11,5},{5,11},... | collective-permute-start | bytes 2359304 | tf_op jit(solution)/shard_map/ppermute | solution.py:84
  156.9 14.7 %collective-permute-start.7 = (f32[2,3,128,128]{3,2,1,0:T(8,128)S(1)}, f32[2,3,128,128]{3,2,1,0:T(8,128)S(1)}, u32[]{:S(2)}, u32[]{:S(2)}) collective-permute-start(f32[2,3,128,128]{3,2,1,0:T(8,128)S(1)} %copy-done.45), channel_id=1, source_target_pairs={{8,2},{2,8},{10,4},{4,10},{12,6},{6,12},{9,3},{3,9},{11,5},{5,11},... | collective-permute-start | bytes 1179656 | tf_op jit(solution)/shard_map/ppermute | solution.py:84
  177.1 30.7 %all-to-all-start.4 = ((f32[8,2,2,32,128]{4,3,2,1,0:T(8,128)}), f32[8,2,2,32,128]{4,3,2,1,0:T(8,128)S(1)}, u32[]{:S(2)}, u32[]{:S(2)}) async-start(f32[8,2,2,32,128]{4,3,2,1,0:T(8,128)} %get-tuple-element.72), calls=%async_computation.4 | async-start | bytes 1048576 | tf_op jit(solution)/shard_map/all_to_all | solution.py:417
  189.2 27.0 %collective-permute-start.18 = (f32[4,3,128,128]{3,2,1,0:T(8,128)}, f32[4,3,128,128]{3,2,1,0:T(8,128)S(1)}, u32[]{:S(2)}, u32[]{:S(2)}) collective-permute-start(f32[4,3,128,128]{3,2,1,0:T(8,128)} %get-tuple-element.81), channel_id=1, source_target_pairs={{0,8},{8,0},{2,10},{10,2},{4,12},{12,4},{6,14},{14,6},{1,9},{9,1},... | collective-permute-start | bytes 2359304 | tf_op jit(solution)/shard_map/ppermute | solution.py:84
  189.6 26.6 %collective-permute-start.19 = (f32[4,3,128,128]{3,2,1,0:T(8,128)}, f32[4,3,128,128]{3,2,1,0:T(8,128)S(1)}, u32[]{:S(2)}, u32[]{:S(2)}) collective-permute-start(f32[4,3,128,128]{3,2,1,0:T(8,128)} %get-tuple-element.82), channel_id=1, source_target_pairs={{8,2},{2,8},{10,4},{4,10},{12,6},{6,12},{9,3},{3,9},{11,5},{5,11},... | collective-permute-start | bytes 2359304 | tf_op jit(solution)/shard_map/ppermute | solution.py:84
  192.8 15.0 %collective-permute-start.9 = (f32[2,3,128,128]{3,2,1,0:T(8,128)S(1)}, f32[2,3,128,128]{3,2,1,0:T(8,128)S(1)}, u32[]{:S(2)}, u32[]{:S(2)}) collective-permute-start(f32[2,3,128,128]{3,2,1,0:T(8,128)S(1)} %copy-done.44), channel_id=1, source_target_pairs={{8,2},{2,8},{10,4},{4,10},{12,6},{6,12},{9,3},{3,9},{11,5},{5,11},... | collective-permute-start | bytes 1179656 | tf_op jit(solution)/shard_map/ppermute | solution.py:84
  214.9 17.2 %collective-permute-start.10 = (f32[1,4,128,128]{3,2,1,0:T(8,128)}, f32[1,4,128,128]{3,2,1,0:T(8,128)}, u32[]{:S(2)}, u32[]{:S(2)}) collective-permute-start(f32[1,4,128,128]{3,2,1,0:T(8,128)} %get-tuple-element.122), channel_id=1, source_target_pairs={{17,0},{25,8},{19,2},{27,10},{21,4},{29,12},{23,6},{31,14}} | collective-permute-start | bytes 786440 | tf_op jit(solution)/shard_map/ppermute | solution.py:84
  227.2 11.7 %collective-permute-start.21 = (f32[1,4,128,128]{3,2,1,0:T(8,128)}, f32[1,4,128,128]{3,2,1,0:T(8,128)}, u32[]{:S(2)}, u32[]{:S(2)}) collective-permute-start(f32[1,4,128,128]{3,2,1,0:T(8,128)} %get-tuple-element.119), channel_id=1, source_target_pairs={{17,16},{25,24},{19,18},{27,26},{21,20},{29,28},{23,22},{31,30}} | collective-permute-start | bytes 786440 | tf_op jit(solution)/shard_map/ppermute | solution.py:84
  229.4 27.4 %collective-permute-start.24 = (f32[2,4,128,128]{3,2,1,0:T(8,128)S(1)}, f32[2,4,128,128]{3,2,1,0:T(8,128)S(1)}, u32[]{:S(2)}, u32[]{:S(2)}) collective-permute-start(f32[2,4,128,128]{3,2,1,0:T(8,128)S(1)} %get-tuple-element.118), channel_id=1, source_target_pairs={{0,1},{8,9},{2,3},{10,11},{4,5},{12,13},{6,7},{14,15},{17,16},{25,... | collective-permute-start | bytes 1572872 | tf_op jit(solution)/shard_map/ppermute | solution.py:84
  230.7 26.1 %collective-permute-start.25 = (f32[2,4,128,128]{3,2,1,0:T(8,128)S(1)}, f32[2,4,128,128]{3,2,1,0:T(8,128)S(1)}, u32[]{:S(2)}, u32[]{:S(2)}) collective-permute-start(f32[2,4,128,128]{3,2,1,0:T(8,128)S(1)} %get-tuple-element.117), channel_id=1, source_target_pairs={{17,1},{25,9},{19,3},{27,11},{21,5},{29,13},{23,7},{31,15},{0,16},... | collective-permute-start | bytes 1572872 | tf_op jit(solution)/shard_map/ppermute | solution.py:84
  243.9 37.8 %collective-permute-start.30 = (f32[2,4,128,128]{3,2,1,0:T(8,128)S(1)}, f32[2,4,128,128]{3,2,1,0:T(8,128)}, u32[]{:S(2)}, u32[]{:S(2)}) collective-permute-start(f32[2,4,128,128]{3,2,1,0:T(8,128)S(1)} %copy-done.4), channel_id=1, source_target_pairs={{1,0},{9,8},{3,2},{11,10},{5,4},{13,12},{7,6},{15,14}} | collective-permute-start | bytes 1572872 | tf_op jit(solution)/shard_map/ppermute | solution.py:84
  245.3 37.8 %collective-permute-start.31 = (f32[2,4,128,128]{3,2,1,0:T(8,128)}, f32[2,4,128,128]{3,2,1,0:T(8,128)S(1)}, u32[]{:S(2)}, u32[]{:S(2)}) collective-permute-start(f32[2,4,128,128]{3,2,1,0:T(8,128)} %get-tuple-element.116), channel_id=1, source_target_pairs={{16,1},{24,9},{18,3},{26,11},{20,5},{28,13},{22,7},{30,15},{1,16},... | collective-permute-start | bytes 1572872 | tf_op jit(solution)/shard_map/ppermute | solution.py:84
  247.2 7.5 %collective-permute-start.23 = (f32[3,128,128]{2,1,0:T(8,128)}, f32[3,128,128]{2,1,0:T(8,128)S(1)}, u32[]{:S(2)}, u32[]{:S(2)}) collective-permute-start(f32[3,128,128]{2,1,0:T(8,128)} %get-tuple-element.86), channel_id=1, source_target_pairs={{8,2},{2,8},{10,4},{4,10},{12,6},{6,12},{9,3},{3,9},{11,5},{5,11},... | collective-permute-start | bytes 589832 | tf_op jit(solution)/shard_map/ppermute | solution.py:84
  254.7 53.9 %collective-permute-start.36 = (f32[2,4,128,128]{3,2,1,0:T(8,128)S(1)}, f32[2,4,128,128]{3,2,1,0:T(8,128)}, u32[]{:S(2)}, u32[]{:S(2)}) collective-permute-start(f32[2,4,128,128]{3,2,1,0:T(8,128)S(1)} %copy-done.4), channel_id=1, source_target_pairs={{16,0},{24,8},{18,2},{26,10},{20,4},{28,12},{22,6},{30,14}} | collective-permute-start | bytes 1572872 | tf_op jit(solution)/shard_map/ppermute | solution.py:84
  263.8 7.3 %collective-permute-start.27 = (f32[3,128,128]{2,1,0:T(8,128)}, f32[3,128,128]{2,1,0:T(8,128)S(1)}, u32[]{:S(2)}, u32[]{:S(2)}) collective-permute-start(f32[3,128,128]{2,1,0:T(8,128)} %get-tuple-element.89), channel_id=1, source_target_pairs={{8,2},{2,8},{10,4},{4,10},{12,6},{6,12},{9,3},{3,9},{11,5},{5,11},... | collective-permute-start | bytes 589832 | tf_op jit(solution)/shard_map/ppermute | solution.py:84
  275.3 7.8 %collective-permute-start.28 = (f32[3,128,128]{2,1,0:T(8,128)}, f32[3,128,128]{2,1,0:T(8,128)S(1)}, u32[]{:S(2)}, u32[]{:S(2)}) collective-permute-start(f32[3,128,128]{2,1,0:T(8,128)} %get-tuple-element.91), channel_id=1, source_target_pairs={{0,8},{8,0},{2,10},{10,2},{4,12},{12,4},{6,14},{14,6},{1,9},{9,1},... | collective-permute-start | bytes 589832 | tf_op jit(solution)/shard_map/ppermute | solution.py:84
  277.6 7.2 %collective-permute-start.29 = (f32[3,128,128]{2,1,0:T(8,128)}, f32[3,128,128]{2,1,0:T(8,128)S(1)}, u32[]{:S(2)}, u32[]{:S(2)}) collective-permute-start(f32[3,128,128]{2,1,0:T(8,128)} %get-tuple-element.92), channel_id=1, source_target_pairs={{8,2},{2,8},{10,4},{4,10},{12,6},{6,12},{9,3},{3,9},{11,5},{5,11},... | collective-permute-start | bytes 589832 | tf_op jit(solution)/shard_map/ppermute | solution.py:84
  281.7 58.5 %collective-permute-start.42 = (f32[1,4,128,128]{3,2,1,0:T(8,128)S(1)}, f32[1,4,128,128]{3,2,1,0:T(8,128)}, u32[]{:S(2)}, u32[]{:S(2)}) collective-permute-start(f32[1,4,128,128]{3,2,1,0:T(8,128)S(1)} %get-tuple-element.121), channel_id=1, source_target_pairs={{17,0},{25,8},{19,2},{27,10},{21,4},{29,12},{23,6},{31,14}} | collective-permute-start | bytes 786440 | tf_op jit(solution)/shard_map/ppermute | solution.py:84
  290.9 7.2 %collective-permute-start.33 = (f32[3,128,128]{2,1,0:T(8,128)}, f32[3,128,128]{2,1,0:T(8,128)S(1)}, u32[]{:S(2)}, u32[]{:S(2)}) collective-permute-start(f32[3,128,128]{2,1,0:T(8,128)} %get-tuple-element.95), channel_id=1, source_target_pairs={{8,2},{2,8},{10,4},{4,10},{12,6},{6,12},{9,3},{3,9},{11,5},{5,11},... | collective-permute-start | bytes 589832 | tf_op jit(solution)/shard_map/ppermute | solution.py:84
  304.6 7.2 %collective-permute-start.35 = (f32[3,128,128]{2,1,0:T(8,128)}, f32[3,128,128]{2,1,0:T(8,128)S(1)}, u32[]{:S(2)}, u32[]{:S(2)}) collective-permute-start(f32[3,128,128]{2,1,0:T(8,128)} %get-tuple-element.98), channel_id=1, source_target_pairs={{8,2},{2,8},{10,4},{4,10},{12,6},{6,12},{9,3},{3,9},{11,5},{5,11},... | collective-permute-start | bytes 589832 | tf_op jit(solution)/shard_map/ppermute | solution.py:84
  329.3 12.3 %collective-permute-start.40 = (f32[3,128,128]{2,1,0:T(8,128)}, f32[3,128,128]{2,1,0:T(8,128)S(1)}, u32[]{:S(2)}, u32[]{:S(2)}) collective-permute-start(f32[3,128,128]{2,1,0:T(8,128)} %get-tuple-element.103), channel_id=1, source_target_pairs={{0,8},{8,0},{2,10},{10,2},{4,12},{12,4},{6,14},{14,6},{1,9},{9,1},... | collective-permute-start | bytes 589832 | tf_op jit(solution)/shard_map/ppermute | solution.py:84
  332.9 29.6 %collective-permute-start.47 = (f32[2,4,128,128]{3,2,1,0:T(8,128)}, f32[2,4,128,128]{3,2,1,0:T(8,128)S(1)}, u32[]{:S(2)}, u32[]{:S(2)}) collective-permute-start(f32[2,4,128,128]{3,2,1,0:T(8,128)} %get-tuple-element.111), channel_id=1, source_target_pairs={{1,16},{9,17},{3,18},{11,19},{5,20},{13,21},{7,22},{15,23},{16,8},... | collective-permute-start | bytes 1572872 | tf_op jit(solution)/shard_map/ppermute | solution.py:84
  336.6 27.2 %collective-permute-start.46 = (f32[2,4,128,128]{3,2,1,0:T(8,128)}, f32[2,4,128,128]{3,2,1,0:T(8,128)S(1)}, u32[]{:S(2)}, u32[]{:S(2)}) collective-permute-start(f32[2,4,128,128]{3,2,1,0:T(8,128)} %get-tuple-element.112), channel_id=1, source_target_pairs={{0,16},{8,17},{2,18},{10,19},{4,20},{12,21},{6,22},{14,23},{16,0},... | collective-permute-start | bytes 1572872 | tf_op jit(solution)/shard_map/ppermute | solution.py:84
  339.5 25.7 %collective-permute-start.45 = (f32[2,4,128,128]{3,2,1,0:T(8,128)}, f32[2,4,128,128]{3,2,1,0:T(8,128)S(1)}, u32[]{:S(2)}, u32[]{:S(2)}) collective-permute-start(f32[2,4,128,128]{3,2,1,0:T(8,128)} %get-tuple-element.113), channel_id=1, source_target_pairs={{0,8},{8,9},{2,10},{10,11},{4,12},{12,13},{6,14},{14,15},{1,0},{9,... | collective-permute-start | bytes 1572872 | tf_op jit(solution)/shard_map/ppermute | solution.py:84
  340.2 26.9 %collective-permute-start.44 = (f32[2,4,128,128]{3,2,1,0:T(8,128)}, f32[2,4,128,128]{3,2,1,0:T(8,128)S(1)}, u32[]{:S(2)}, u32[]{:S(2)}) collective-permute-start(f32[2,4,128,128]{3,2,1,0:T(8,128)} %get-tuple-element.110), channel_id=1, source_target_pairs={{0,0},{8,1},{2,2},{10,3},{4,4},{12,5},{6,6},{14,7},{1,8},{9,9},{3,... | collective-permute-start | bytes 1572872 | tf_op jit(solution)/shard_map/ppermute | solution.py:84
  341.5 7.3 %collective-permute-start.41 = (f32[3,128,128]{2,1,0:T(8,128)S(1)}, f32[3,128,128]{2,1,0:T(8,128)S(1)}, u32[]{:S(2)}, u32[]{:S(2)}) collective-permute-start(f32[3,128,128]{2,1,0:T(8,128)S(1)} %copy-done.46), channel_id=1, source_target_pairs={{8,2},{2,8},{10,4},{4,10},{12,6},{6,12},{9,3},{3,9},{11,5},{5,11},... | collective-permute-start | bytes 589832 | tf_op jit(solution)/shard_map/ppermute | solution.py:84
  348.8 10.6 %collective-permute-start.39 = (f32[4,128,128]{2,1,0:T(8,128)}, f32[4,128,128]{2,1,0:T(8,128)S(1)}, u32[]{:S(2)}, u32[]{:S(2)}) collective-permute-start(f32[4,128,128]{2,1,0:T(8,128)} %get-tuple-element.102.refs_1_), channel_id=1, source_target_pairs={{0,24},{8,25},{2,26},{10,27},{4,28},{12,29},{6,30},{14,31}} | collective-permute-start | bytes 786440 | tf_op jit(solution)/shard_map/ppermute | solution.py:84
  359.5 9.1 %collective-permute-start.50 = (f32[4,128,128]{2,1,0:T(8,128)}, f32[4,128,128]{2,1,0:T(8,128)S(1)}, u32[]{:S(2)}, u32[]{:S(2)}) collective-permute-start(f32[4,128,128]{2,1,0:T(8,128)} %get-tuple-element.102.refs_1_), channel_id=1, source_target_pairs={{16,24},{24,25},{18,26},{26,27},{20,28},{28,29},{22,30},{30,31}} | collective-permute-start | bytes 786440 | tf_op jit(solution)/shard_map/ppermute | solution.py:84
  362.5 10.9 %collective-permute-start.48 = (f32[4,128,128]{2,1,0:T(8,128)}, f32[4,128,128]{2,1,0:T(8,128)S(1)}, u32[]{:S(2)}, u32[]{:S(2)}) collective-permute-start(f32[4,128,128]{2,1,0:T(8,128)} %get-tuple-element.102.refs_1_), channel_id=1, source_target_pairs={{1,24},{9,25},{3,26},{11,27},{5,28},{13,29},{7,30},{15,31}} | collective-permute-start | bytes 786440 | tf_op jit(solution)/shard_map/ppermute | solution.py:84
  363.8 9.6 %collective-permute-start.43 = (f32[4,128,128]{2,1,0:T(8,128)}, f32[4,128,128]{2,1,0:T(8,128)S(1)}, u32[]{:S(2)}, u32[]{:S(2)}) collective-permute-start(f32[4,128,128]{2,1,0:T(8,128)} %shard_map.75), channel_id=1, source_target_pairs={{0,24},{8,25},{2,26},{10,27},{4,28},{12,29},{6,30},{14,31}} | collective-permute-start | bytes 786440 | tf_op jit(solution)/shard_map/ppermute | solution.py:84
  365.1 8.3 %collective-permute-start.51 = (f32[4,128,128]{2,1,0:T(8,128)}, f32[4,128,128]{2,1,0:T(8,128)S(1)}, u32[]{:S(2)}, u32[]{:S(2)}) collective-permute-start(f32[4,128,128]{2,1,0:T(8,128)} %shard_map.75), channel_id=1, source_target_pairs={{16,24},{24,25},{18,26},{26,27},{20,28},{28,29},{22,30},{30,31}} | collective-permute-start | bytes 786440 | tf_op jit(solution)/shard_map/ppermute | solution.py:84
  367.1 10.4 %collective-permute-start.49 = (f32[4,128,128]{2,1,0:T(8,128)}, f32[4,128,128]{2,1,0:T(8,128)}, u32[]{:S(2)}, u32[]{:S(2)}) collective-permute-start(f32[4,128,128]{2,1,0:T(8,128)} %shard_map.75), channel_id=1, source_target_pairs={{1,24},{9,25},{3,26},{11,27},{5,28},{13,29},{7,30},{15,31}} | collective-permute-start | bytes 786440 | tf_op jit(solution)/shard_map/ppermute | solution.py:84
  (58 other events, 209.8 us)

commit v4 on v3

--- a/solution.py
+++ b/solution.py
@@ -99,10 +99,15 @@
 SCALARS = pl.BlockSpec(memory_space=pltpu.SMEM)
 
 
+RESIDENT = pl.BlockSpec(memory_space=pltpu.VMEM)
+GRANT = 20 * 2**20
+
+
 def run(kernel, grid, in_specs, out_specs, out_shape, scratch=()):
     return pl.pallas_call(
         kernel,
-        grid=(grid,),
+        grid=(grid,) if grid else (),
+        compiler_params=pltpu.CompilerParams(vmem_limit_bytes=GRANT),
         in_specs=in_specs,
         out_specs=out_specs,
         out_shape=out_shape,
@@ -123,14 +128,6 @@
     def _():
         put(0, chip[held - wide :])
         put(wide + count, hop[:wide])
-
-
-def widen_kernel(flags, own, chip, hop, inv, out):
-    def put(start, planes):
-        stop = start + planes.shape[0]
-        out[start:stop] = planes * inv[start:stop]
-
-    join(flags, own, chip, hop, (out.shape[0] - own.shape[0]) // 2, put)
 
 
 def conduct_kernel(flags, own, chip, hop, fine_rate, fine_inv, coarse_rate, coarse_inv):
@@ -215,8 +212,11 @@
 
 def fine_kernel(first, last, coupled, per, *refs):
     refs = list(refs)
-    flags, own, chip, hop, source, rate, inv = refs[:7]
-    refs = refs[7:]
+    flags, own, chip, hop, source = refs[:5]
+    refs = refs[5:]
+    if first:
+        source_parts, refs = [source] + refs[:2], refs[2:]
+    rate, inv, refs = refs[0], refs[1], refs[2:]
     if coupled:
         got, arrived, refs = refs[0], refs[1], refs[2:]
     if coupled and not last:
@@ -231,7 +231,7 @@
     if coupled and not last:
         packed, refs = refs[0], refs[1:]
     if first:
-        old_out, refs = refs[0], refs[1:]
+        old_out, source, refs = refs[0], refs[1], refs[2:]
     one, two, other, keep = refs[:4]
     wide = (inv.shape[0] - own.shape[0]) // 2
 
@@ -241,6 +241,12 @@
 
     load_field(flags, own, chip, hop, one)
     if first:
+
+        def put_source(start, planes):
+            stop = start + planes.shape[0]
+            source[start:stop] = planes * inv[start:stop]
+
+        join(flags, *source_parts, wide, put_source)
 
         def put_old(p, value):
             old_out[p] = value
@@ -436,15 +442,6 @@
         [f32(ext_planes, *plane)] * 4,
     )(flags, all_0, chip_0, hop_0)
 
-    def widen(fields, chip, hop, count):
-        return run(
-            widen_kernel,
-            count,
-            [SCALARS] + parts_of(count) + [whole(ext_planes, *plane)],
-            each(ext_planes, *plane),
-            f32(count, ext_planes, *plane),
-        )(flags, fields, chip, hop, fine_inv)
-
     buffers = [pltpu.VMEM((buf_planes, rows + 2 * PAD, lanes), jnp.float32)] * 3 + [
         pltpu.VMEM((ext_planes, *plane), jnp.float32)
     ]
@@ -454,16 +451,15 @@
     def fine(step, count, field, chip, hop, source, arrived=None, old=None):
         first, last = step == 0, step == STEPS - 1
         coupled = arrived is not None
-        args = [flags, field, chip, hop, source, fine_rate, fine_inv]
-        ins = [
-            SCALARS,
-            each(planes, *plane),
-            each(SWEEPS, *plane),
-            each(SWEEPS, *plane),
-            each(ext_planes, *plane),
-            whole(ext_planes, *plane),
-            whole(ext_planes, *plane),
-        ]
+        args, ins = [flags, field, chip, hop], [SCALARS] + parts_of(0)
+        if first:
+            args += [field, chip, hop]
+            ins += parts_of(count)
+        else:
+            args.append(source)
+            ins.append(each(ext_planes, *plane))
+        args += [fine_rate, fine_inv]
+        ins += [whole(ext_planes, *plane)] * 2
         outs, shapes = [each(planes, *plane)], [f32(count, planes, *plane)]
         if coupled:
             args += [got, arrived]
@@ -484,8 +480,8 @@
                 outs.append(packed_spec)
                 shapes.append(f32(*packed_shape))
         if first:
-            outs.append(each(planes, *plane))
-            shapes.append(f32(count, planes, *plane))
+            outs += [each(planes, *plane), each(ext_planes, *plane)]
+            shapes += [f32(count, planes, *plane), f32(count, ext_planes, *plane)]
         return run(
             functools.partial(fine_kernel, first, last, coupled, count // slices),
             count,
@@ -502,8 +498,7 @@
         packed_spec,
         f32(*packed_shape),
     )(select, all_0)
-    field_0, wide_0 = all_0, widen(all_0, chip_0, hop_0, count_0)
-    field_1, wide_1 = all_1, widen(all_1, chip_1, hop_1, count_1)
+    field_0, field_1, wide_0, wide_1 = all_0, all_1, None, None
     old_0 = old_1 = None
     for step in range(STEPS):
         arrived = trade(packed)
@@ -511,7 +506,8 @@
         result_1 = fine(step, count_1, field_1, chip_1, hop_1, wide_1, None, old_1)
         field_0, field_1 = result_0[0], result_1[0]
         if step == 0:
-            old_0, old_1 = result_0[4], result_1[3]
+            old_0, wide_0 = result_0[4:]
+            old_1, wide_1 = result_1[3:]
         if step < STEPS - 1:
             packed = result_0[3]
             chip_0, hop_0 = send(result_0[1], lay.chip()), send(result_0[2], lay.hop())
@@ -554,7 +550,7 @@
         return [part for part, _ in found], [index for _, index in found]
 
     anywhere = [pl.BlockSpec(memory_space=pl.ANY)] * comps
-    halo_specs = [whole(SWEEPS, *plane)] * 2
+    halo_specs = [RESIDENT] * 2
     halo_shapes = [f32(SWEEPS, *plane)] * 2
     dma = pltpu.SemaphoreType.DMA(())
     roles = range(comps)
@@ -562,9 +558,9 @@
     parts, indices = [final[role] for role in range(comps)], [0] * comps
     new, chip, hop = run(
         functools.partial(begin_kernel, indices),
-        1,
+        0,
         [SCALARS] + anywhere,
-        [whole(planes, *plane)] + halo_specs,
+        [RESIDENT] + halo_specs,
         [f32(planes, *plane)] + halo_shapes,
         [dma],
     )(flags, *parts)
@@ -575,12 +571,9 @@
         parts, indices = choices(j // slices, j % slices)
         result = run(
             functools.partial(chain_kernel, indices, last),
-            1,
-            [SCALARS, whole(planes, *plane)]
-            + halo_specs
-            + [whole(ext_planes, *plane)] * 2
-            + anywhere,
-            [whole(planes, *plane)] + ([] if last else halo_specs),
+            0,
+            [SCALARS] + [RESIDENT] * 5 + anywhere,
+            [RESIDENT] + ([] if last else halo_specs),
             [f32(planes, *plane)] + ([] if last else halo_shapes),
             buffers + [pltpu.VMEM((planes, *plane), jnp.float32), dma],
         )(flags, new, chip, hop, coarse_rate, coarse_inv, *parts)
@@ -599,7 +592,10 @@
     result = []
     for comp in range(comps):
         pairs = lay.home_last(comp)
-        late = jnp.stack([send(news[early + slot], pairs) for slot in range(slices)])
+        late = []
+        for slot in range(slices):
+            late.append(send(news[early + slot], pairs))
+        late = jnp.stack(late)
         soon = lax.dynamic_index_in_dim(back, time_index ^ comp, 0, keepdims=False)
         result.append(jnp.where(time_index == end, late, soon))
     return jnp.stack(result, axis=1)

time: 383 us -> 375 us (0.979)
  Pallas kernels: 88 us -> 54.2 us
  local copies, waits for them, and re-layouts: 36.4 us -> 54.6 us
  waiting for transfers between devices: 117 us -> 125 us
    unnamed x101 -> x143, local copies, waits for them, and re-layouts: 21.6 us -> 45.5 us
    pallas_call x10 -> x8, Pallas kernels: 33 us -> 13.2 us  [the longest x7 11 us: shards(): run(functools.partial(chain_kernel, indices, last), 0, [SCALARS] + [RESID...]
    pallas_call x8, Pallas kernels: 47.8 us -> 37.5 us  [fine(): run(functools.partial(fine_kernel, first, last, coupled, count // slices)...]
    all_to_all x5, waiting for transfers between devices: 20.4 us -> 26.4 us  [trade(): lax.all_to_all(value, AXES, 0, 0, axis_index_groups=groups, tiled=True)]
  transfers between devices with their start and end apart: 57 -> 57, of which waited for: 17 -> 17; matrix products, arithmetic and copies ran while one was open for 6% -> 3% of each run, Pallas kernels for 23% -> 15%
where the time goes in v4:
time: 375 us; the launch traced here: 372 us
  starting transfers between devices  131 us (35%)
  waiting for transfers between devices  125 us (33%)
  local copies, waits for them, and re-layouts  54.6 us (15%)
  Pallas kernels  54.2 us (14%)
  other arithmetic  6.1 us (2%)
    ppermute x52, starting transfers between devices, send(): return lax.ppermute(value, AXES, pairs)  104 us
    ppermute x52, waiting for transfers between devices, send(): return lax.ppermute(value, AXES, pairs)  99.1 us
    unnamed x143, local copies, waits for them, and re-layouts  45.5 us
    pallas_call x8, Pallas kernels, fine(): run(functools.partial(fine_kernel, first, last, coupled, count // slices)...  37.5 us
    all_to_all x5, waiting for transfers between devices, trade(): lax.all_to_all(value, AXES, 0, 0, axis_index_groups=groups, tiled=True)  26.4 us
    all_to_all x5, starting transfers between devices, trade(): lax.all_to_all(value, AXES, 0, 0, axis_index_groups=groups, tiled=True)  26.2 us
    pallas_call x7, Pallas kernels, shards(): run(functools.partial(chain_kernel, indices, last), 0, [SCALARS] + [RESID...  11 us
  transfers between devices with their start and end apart: 57, of which 17 were waited for; matrix products, arithmetic and copies ran while one was open for 3% of the time, Pallas kernels for 15%

profile of v4, /device:TPU:11, one launch (start us, length us, event | category | flops | bytes accessed | tf_op | source)
XLA Modules:
  0.0 372.3 jit_solution(5594625545377679298)
XLA Ops:
  3.0 3.8 %collective-permute-start.11 = (f32[8,4,128,128]{3,2,1,0:T(8,128)}, f32[8,4,128,128]{3,2,1,0:T(8,128)S(1)}, u32[]{:S(2)}, u32[]{:S(2)}) collective-permute-start(f32[8,4,128,128]{3,2,1,0:T(8,128)} %pad_maximum_fusion), channel_id=1, source_target_pairs={{0,0},{1,8},{2,2},{3,10},{4,4},{5,12},{6,6},{7,14},{8,1},{9,9},{10... | collective-permute-start | bytes 6291464 | tf_op jit(solution)/shard_map/ppermute | solution.py:84
  10.1 3.6 collective-permute-start.3
  13.8 31.1 %collective-permute-done.3 = s32[2,2,128]{2,1,0:T(2,128)S(1)} collective-permute-done((s32[2,2,128]{2,1,0:T(2,128)S(1)}, s32[2,2,128]{2,1,0:T(2,128)S(1)}, u32[]{:S(2)}, u32[]{:S(2)}) %collective-permute-start.3) | collective-permute-done | bytes 2080 | tf_op jit(solution)/shard_map/ppermute | solution.py:84
  48.2 3.6 collective-permute-start.2
  54.2 3.6 collective-permute-start.13
  58.5 3.8 %all-to-all-start = ((f32[8,1,128]{2,1,0:T(1,128)}), f32[8,1,128]{2,1,0:T(1,128)S(1)}, u32[]{:S(2)}, u32[]{:S(2)}) async-start(f32[8,1,128]{2,1,0:T(1,128)} %reshape.141), calls=%async_computation | async-start | bytes 8192 | tf_op jit(solution)/shard_map/all_to_all | solution.py:423
  64.5 17.2 %all-to-all-done = f32[8,1,128]{2,1,0:T(1,128)S(1)} async-done(((f32[8,1,128]{2,1,0:T(1,128)}), f32[8,1,128]{2,1,0:T(1,128)S(1)}, u32[]{:S(2)}, u32[]{:S(2)}) %all-to-all-start) | async-done | bytes 4128 | tf_op jit(solution)/shard_map/all_to_all | solution.py:423
  81.7 5.8 %all-to-all-start.1 = ((f32[8,2,2,32,128]{4,3,2,1,0:T(8,128)}), f32[8,2,2,32,128]{4,3,2,1,0:T(8,128)}, u32[]{:S(2)}, u32[]{:S(2)}) async-start(f32[8,2,2,32,128]{4,3,2,1,0:T(8,128)} %shard_map.57), calls=%async_computation.1 | async-start | bytes 1048576 | tf_op jit(solution)/shard_map/all_to_all | solution.py:423
  90.2 9.1 %all-to-all-done.1.refs_10_ = f32[8,2,2,32,128]{4,3,2,1,0:T(8,128)} async-done(((f32[8,2,2,32,128]{4,3,2,1,0:T(8,128)}), f32[8,2,2,32,128]{4,3,2,1,0:T(8,128)}, u32[]{:S(2)}, u32[]{:S(2)}) %all-to-all-start.1) | async-done | bytes 524320 | tf_op jit(solution)/shard_map/all_to_all | solution.py:423
  100.3 4.7 %shard_map.58 = (f32[2,4,128,128]{3,2,1,0:T(8,128)S(1)}, f32[2,3,128,128]{3,2,1,0:T(8,128)S(1)}, f32[2,3,128,128]{3,2,1,0:T(8,128)S(1)}, f32[8,2,2,32,128]{4,3,2...) custom-call(s32[6]{0:T(128)S(1)} %stack.115.flags.refs_0_, ...), custom_call_target="tpu_custom_call" | custom-call | tf_op jit(solution)/shard_map/pallas_call | solution.py:485
  109.9 7.7 %all-to-all-start.2 = ((f32[8,2,2,32,128]{4,3,2,1,0:T(8,128)}), f32[8,2,2,32,128]{4,3,2,1,0:T(8,128)}, u32[]{:S(2)}, u32[]{:S(2)}) async-start(f32[8,2,2,32,128]{4,3,2,1,0:T(8,128)} %copy-done.34), calls=%async_computation.2 | async-start | bytes 1048576 | tf_op jit(solution)/shard_map/all_to_all | solution.py:423
  118.0 3.1 collective-permute-start.5
  122.7 8.1 %shard_map.62 = (f32[4,4,128,128]{3,2,1,0:T(8,128)S(1)}, f32[4,3,128,128]{3,2,1,0:T(8,128)}, f32[4,3,128,128]{3,2,1,0:T(8,128)}, f32[4,4,128,128]{3,2,1,0:T(8,128)S(1)}, f32[4,8,128,128]{3,2,1,0:T(8,128)S(1)}) custom-call(s32[6]{0:T(128)S(1)} %stack.115.flags.refs_0_, f32[8,4,128,128]{3,2,1,0:T(8,128)S(1)} %copy-done.5, ...), custom_call_target="tpu_custom_call" | custom-call | tf_op jit(solution)/shard_map/pallas_call | solution.py:485
  134.1 3.5 collective-permute-start.15
  142.2 3.0 shard_map.59
  148.3 4.1 %all-to-all-start.3 = ((f32[8,2,2,32,128]{4,3,2,1,0:T(8,128)}), f32[8,2,2,32,128]{4,3,2,1,0:T(8,128)}, u32[]{:S(2)}, u32[]{:S(2)}) async-start(f32[8,2,2,32,128]{4,3,2,1,0:T(8,128)} %copy-done.36), calls=%async_computation.3 | async-start | bytes 1048576 | tf_op jit(solution)/shard_map/all_to_all | solution.py:423
  155.3 5.5 %shard_map.63 = (f32[4,4,128,128]{3,2,1,0:T(8,128)S(1)}, f32[4,3,128,128]{3,2,1,0:T(8,128)}, f32[4,3,128,128]{3,2,1,0:T(8,128)}) custom-call(s32[6]{0:T(128)S(1)} %stack.115.flags.refs_0_, f32[4,4,128,128]{3,2,1,0:T(8,128)S(1)} %copy-done.25, f32[4,3,128,128]{3,2,1,0:T(8,128)} %collective-permute-done.14.refs_2_, ...), custom_call_target="tpu_custom_call" | custom-call | tf_op jit(solution)/shard_map/pallas_call | solution.py:485
  161.8 3.1 collective-permute-start.17
  165.0 3.5 collective-permute-start.7
  169.2 10.3 %collective-permute-done.7.refs_3_ = f32[2,3,128,128]{3,2,1,0:T(8,128)S(1)} collective-permute-done((f32[2,3,128,128]{3,2,1,0:T(8,128)S(1)}, f32[2,3,128,128]{3,2,1,0:T(8,128)S(1)}, u32[]{:S(2)}, u32[]{:S(2)}) %collective-permute-start.7) | collective-permute-done | bytes 393248 | tf_op jit(solution)/shard_map/ppermute | solution.py:84
  183.4 3.0 shard_map.60
  189.5 4.8 %all-to-all-start.4 = ((f32[8,2,2,32,128]{4,3,2,1,0:T(8,128)}), f32[8,2,2,32,128]{4,3,2,1,0:T(8,128)}, u32[]{:S(2)}, u32[]{:S(2)}) async-start(f32[8,2,2,32,128]{4,3,2,1,0:T(8,128)} %copy-done.35), calls=%async_computation.4 | async-start | bytes 1048576 | tf_op jit(solution)/shard_map/all_to_all | solution.py:423
  197.2 5.5 %shard_map.64 = (f32[4,4,128,128]{3,2,1,0:T(8,128)S(1)}, f32[4,3,128,128]{3,2,1,0:T(8,128)}, f32[4,3,128,128]{3,2,1,0:T(8,128)}) custom-call(s32[6]{0:T(128)S(1)} %stack.115.flags.refs_0_, f32[4,4,128,128]{3,2,1,0:T(8,128)S(1)} %copy-done.23, f32[4,3,128,128]{3,2,1,0:T(8,128)} %collective-permute-done.16.refs_2_, ...), custom_call_target="tpu_custom_call" | custom-call | tf_op jit(solution)/shard_map/pallas_call | solution.py:485
  204.0 3.1 collective-permute-start.19
  207.2 3.6 collective-permute-start.9
  210.9 10.9 %collective-permute-done.9.refs_3_ = f32[2,3,128,128]{3,2,1,0:T(8,128)S(1)} collective-permute-done((f32[2,3,128,128]{3,2,1,0:T(8,128)S(1)}, f32[2,3,128,128]{3,2,1,0:T(8,128)S(1)}, u32[]{:S(2)}, u32[]{:S(2)}) %collective-permute-start.9) | collective-permute-done | bytes 393248 | tf_op jit(solution)/shard_map/ppermute | solution.py:84
  225.6 3.0 shard_map.61.refs_6_
  232.3 4.7 %shard_map.65.refs_7_.refs_8_ = f32[4,4,128,128]{3,2,1,0:T(8,128)S(1)} custom-call(s32[6]{0:T(128)S(1)} %stack.115.flags.refs_0_, f32[4,4,128,128]{3,2,1,0:T(8,128)S(1)} %copy-done.21, f32[4,3,128,128]{3,2,1,0:T(8,128)} %collective-permute-done.18.refs_2_, f32[4,3,128,128]{3,2,1,0:T(8,128)} %collective-permute-done.19.refs_3_, ...), custom_call_target="tpu_custom_call" | custom-call | tf_op jit(solution)/shard_map/pallas_call | solution.py:485
  245.0 5.4 %collective-permute-done.21.refs_3_ = f32[1,4,128,128]{3,2,1,0:T(8,128)} collective-permute-done((f32[1,4,128,128]{3,2,1,0:T(8,128)}, f32[1,4,128,128]{3,2,1,0:T(8,128)}, u32[]{:S(2)}, u32[]{:S(2)}) %collective-permute-start.21) | collective-permute-done | bytes 262176 | tf_op jit(solution)/shard_map/ppermute | solution.py:84
  254.3 3.5 collective-permute-start.22
  260.4 3.0 collective-permute-start.23
  263.4 4.5 %collective-permute-done.23.refs_3_ = f32[3,128,128]{2,1,0:T(8,128)S(1)} collective-permute-done((f32[3,128,128]{2,1,0:T(8,128)}, f32[3,128,128]{2,1,0:T(8,128)S(1)}, u32[]{:S(2)}, u32[]{:S(2)}) %collective-permute-start.23) | collective-permute-done | bytes 196640 | tf_op jit(solution)/shard_map/ppermute | solution.py:84
  273.3 3.5 collective-permute-start.27
  276.8 3.6 collective-permute-done.27.refs_3_
  284.4 3.1 collective-permute-start.29
  288.3 3.1 collective-permute-done.29.refs_3_
  294.9 3.4 collective-permute-start.33
  298.3 3.6 collective-permute-done.33.refs_3_
  305.6 3.1 collective-permute-start.35
  308.8 3.8 %collective-permute-done.35.refs_3_ = f32[3,128,128]{2,1,0:T(8,128)S(1)} collective-permute-done((f32[3,128,128]{2,1,0:T(8,128)S(1)}, f32[3,128,128]{2,1,0:T(8,128)S(1)}, u32[]{:S(2)}, u32[]{:S(2)}) %collective-permute-start.35) | collective-permute-done | bytes 196640 | tf_op jit(solution)/shard_map/ppermute | solution.py:84
  316.1 3.4 collective-permute-start.38
  319.5 3.6 collective-permute-done.38.refs_3_
  327.1 3.1 collective-permute-start.47
  330.1 3.5 collective-permute-start.46
  337.6 5.1 %collective-permute-done.41.refs_3_ = f32[3,128,128]{2,1,0:T(8,128)S(1)} collective-permute-done((f32[3,128,128]{2,1,0:T(8,128)S(1)}, f32[3,128,128]{2,1,0:T(8,128)S(1)}, u32[]{:S(2)}, u32[]{:S(2)}) %collective-permute-start.41) | collective-permute-done | bytes 196640 | tf_op jit(solution)/shard_map/ppermute | solution.py:84
  345.3 7.5 %collective-permute-done.39 = f32[4,128,128]{2,1,0:T(8,128)S(1)} collective-permute-done((f32[4,128,128]{2,1,0:T(8,128)S(1)}, f32[4,128,128]{2,1,0:T(8,128)S(1)}, u32[]{:S(2)}, u32[]{:S(2)}) %collective-permute-start.39) | collective-permute-done | bytes 262176 | tf_op jit(solution)/shard_map/ppermute | solution.py:84
  352.9 3.3 collective-permute-start.50
  366.6 4.3 %collective-permute-done.49 = f32[4,128,128]{2,1,0:T(8,128)S(1)} collective-permute-done((f32[4,128,128]{2,1,0:T(8,128)S(1)}, f32[4,128,128]{2,1,0:T(8,128)S(1)}, u32[]{:S(2)}, u32[]{:S(2)}) %collective-permute-start.49) | collective-permute-done | bytes 262176 | tf_op jit(solution)/shard_map/ppermute | solution.py:84
  (258 shorter events, 117.1 us)
Async XLA Ops:
  3.0 48.8 %collective-permute-start.11 = (f32[8,4,128,128]{3,2,1,0:T(8,128)}, f32[8,4,128,128]{3,2,1,0:T(8,128)S(1)}, u32[]{:S(2)}, u32[]{:S(2)}) collective-permute-start(f32[8,4,128,128]{3,2,1,0:T(8,128)} %pad_maximum_fusion), channel_id=1, source_target_pairs={{0,0},{1,8},{2,2},{3,10},{4,4},{5,12},{6,6},{7,14},{8,1},{9,9},{10... | collective-permute-start | bytes 6291464 | tf_op jit(solution)/shard_map/ppermute | solution.py:84
  8.1 38.6 %collective-permute-start = (f32[5,4,128,128]{3,2,1,0:T(8,128)}, f32[5,4,128,128]{3,2,1,0:T(8,128)S(1)}, u32[]{:S(2)}, u32[]{:S(2)}) collective-permute-start(f32[5,4,128,128]{3,2,1,0:T(8,128)} %pad_maximum_fusion.3), channel_id=1, source_target_pairs={{0,0},{1,8},{2,2},{3,10},{4,4},{5,12},{6,6},{7,14},{8,1},{9,9},{10... | collective-permute-start | bytes 3932168 | tf_op jit(solution)/shard_map/ppermute | solution.py:84
  10.1 34.7 %collective-permute-start.3 = (s32[2,2,128]{2,1,0:T(2,128)S(1)}, s32[2,2,128]{2,1,0:T(2,128)S(1)}, u32[]{:S(2)}, u32[]{:S(2)}) collective-permute-start(s32[2,2,128]{2,1,0:T(2,128)S(1)} %pad_add_fusion), channel_id=1, source_target_pairs={{0,0},{1,8},{2,2},{3,10},{4,4},{5,12},{6,6},{7,14},{8,1},{9,9},{10... | collective-permute-start | bytes 6152 | tf_op jit(solution)/shard_map/ppermute | solution.py:84
  48.2 40.8 %collective-permute-start.1 = (f32[5,3,128,128]{3,2,1,0:T(8,128)}, f32[5,3,128,128]{3,2,1,0:T(8,128)}, u32[]{:S(2)}, u32[]{:S(2)}) collective-permute-start(f32[5,3,128,128]{3,2,1,0:T(8,128)} %get-tuple-element.119), channel_id=1, source_target_pairs={{0,8},{8,0},{2,10},{10,2},{4,12},{12,4},{6,14},{14,6},{1,9},{9,1},... | collective-permute-start | bytes 2949128 | tf_op jit(solution)/shard_map/ppermute | solution.py:84
  48.2 40.8 %collective-permute-start.2 = (f32[5,3,128,128]{3,2,1,0:T(8,128)}, f32[5,3,128,128]{3,2,1,0:T(8,128)}, u32[]{:S(2)}, u32[]{:S(2)}) collective-permute-start(f32[5,3,128,128]{3,2,1,0:T(8,128)} %get-tuple-element.118), channel_id=1, source_target_pairs={{8,2},{2,8},{10,4},{4,10},{12,6},{6,12},{9,3},{3,9},{11,5},{5,11},... | collective-permute-start | bytes 2949128 | tf_op jit(solution)/shard_map/ppermute | solution.py:84
  54.2 66.9 %collective-permute-start.12 = (f32[8,3,128,128]{3,2,1,0:T(8,128)}, f32[8,3,128,128]{3,2,1,0:T(8,128)}, u32[]{:S(2)}, u32[]{:S(2)}) collective-permute-start(f32[8,3,128,128]{3,2,1,0:T(8,128)} %get-tuple-element.113), channel_id=1, source_target_pairs={{0,8},{8,0},{2,10},{10,2},{4,12},{12,4},{6,14},{14,6},{1,9},{9,1},... | collective-permute-start | bytes 4718600 | tf_op jit(solution)/shard_map/ppermute | solution.py:84
  54.2 66.9 %collective-permute-start.13 = (f32[8,3,128,128]{3,2,1,0:T(8,128)}, f32[8,3,128,128]{3,2,1,0:T(8,128)}, u32[]{:S(2)}, u32[]{:S(2)}) collective-permute-start(f32[8,3,128,128]{3,2,1,0:T(8,128)} %get-tuple-element.112), channel_id=1, source_target_pairs={{8,2},{2,8},{10,4},{4,10},{12,6},{6,12},{9,3},{3,9},{11,5},{5,11},... | collective-permute-start | bytes 4718600 | tf_op jit(solution)/shard_map/ppermute | solution.py:84
  58.5 23.3 %all-to-all-start = ((f32[8,1,128]{2,1,0:T(1,128)}), f32[8,1,128]{2,1,0:T(1,128)S(1)}, u32[]{:S(2)}, u32[]{:S(2)}) async-start(f32[8,1,128]{2,1,0:T(1,128)} %reshape.141), calls=%async_computation | async-start | bytes 8192 | tf_op jit(solution)/shard_map/all_to_all | solution.py:423
  81.7 17.6 %all-to-all-start.1 = ((f32[8,2,2,32,128]{4,3,2,1,0:T(8,128)}), f32[8,2,2,32,128]{4,3,2,1,0:T(8,128)}, u32[]{:S(2)}, u32[]{:S(2)}) async-start(f32[8,2,2,32,128]{4,3,2,1,0:T(8,128)} %shard_map.57), calls=%async_computation.1 | async-start | bytes 1048576 | tf_op jit(solution)/shard_map/all_to_all | solution.py:423
  109.9 29.2 %all-to-all-start.2 = ((f32[8,2,2,32,128]{4,3,2,1,0:T(8,128)}), f32[8,2,2,32,128]{4,3,2,1,0:T(8,128)}, u32[]{:S(2)}, u32[]{:S(2)}) async-start(f32[8,2,2,32,128]{4,3,2,1,0:T(8,128)} %copy-done.34), calls=%async_computation.2 | async-start | bytes 1048576 | tf_op jit(solution)/shard_map/all_to_all | solution.py:423
  117.6 20.1 %collective-permute-start.4 = (f32[2,3,128,128]{3,2,1,0:T(8,128)}, f32[2,3,128,128]{3,2,1,0:T(8,128)S(1)}, u32[]{:S(2)}, u32[]{:S(2)}) collective-permute-start(f32[2,3,128,128]{3,2,1,0:T(8,128)} %copy-done.52), channel_id=1, source_target_pairs={{0,8},{8,0},{2,10},{10,2},{4,12},{12,4},{6,14},{14,6},{1,9},{9,1},... | collective-permute-start | bytes 1179656 | tf_op jit(solution)/shard_map/ppermute | solution.py:84
  118.0 20.4 %collective-permute-start.5 = (f32[2,3,128,128]{3,2,1,0:T(8,128)}, f32[2,3,128,128]{3,2,1,0:T(8,128)S(1)}, u32[]{:S(2)}, u32[]{:S(2)}) collective-permute-start(f32[2,3,128,128]{3,2,1,0:T(8,128)} %copy-done.49), channel_id=1, source_target_pairs={{8,2},{2,8},{10,4},{4,10},{12,6},{6,12},{9,3},{3,9},{11,5},{5,11},... | collective-permute-start | bytes 1179656 | tf_op jit(solution)/shard_map/ppermute | solution.py:84
  134.1 18.3 %collective-permute-start.14 = (f32[4,3,128,128]{3,2,1,0:T(8,128)}, f32[4,3,128,128]{3,2,1,0:T(8,128)}, u32[]{:S(2)}, u32[]{:S(2)}) collective-permute-start(f32[4,3,128,128]{3,2,1,0:T(8,128)} %get-tuple-element.78), channel_id=1, source_target_pairs={{0,8},{8,0},{2,10},{10,2},{4,12},{12,4},{6,14},{14,6},{1,9},{9,1},... | collective-permute-start | bytes 2359304 | tf_op jit(solution)/shard_map/ppermute | solution.py:84
  134.1 18.3 %collective-permute-start.15 = (f32[4,3,128,128]{3,2,1,0:T(8,128)}, f32[4,3,128,128]{3,2,1,0:T(8,128)}, u32[]{:S(2)}, u32[]{:S(2)}) collective-permute-start(f32[4,3,128,128]{3,2,1,0:T(8,128)} %get-tuple-element.79), channel_id=1, source_target_pairs={{8,2},{2,8},{10,4},{4,10},{12,6},{6,12},{9,3},{3,9},{11,5},{5,11},... | collective-permute-start | bytes 2359304 | tf_op jit(solution)/shard_map/ppermute | solution.py:84
  148.3 32.0 %all-to-all-start.3 = ((f32[8,2,2,32,128]{4,3,2,1,0:T(8,128)}), f32[8,2,2,32,128]{4,3,2,1,0:T(8,128)}, u32[]{:S(2)}, u32[]{:S(2)}) async-start(f32[8,2,2,32,128]{4,3,2,1,0:T(8,128)} %copy-done.36), calls=%async_computation.3 | async-start | bytes 1048576 | tf_op jit(solution)/shard_map/all_to_all | solution.py:423
  161.7 32.6 %collective-permute-start.16 = (f32[4,3,128,128]{3,2,1,0:T(8,128)}, f32[4,3,128,128]{3,2,1,0:T(8,128)}, u32[]{:S(2)}, u32[]{:S(2)}) collective-permute-start(f32[4,3,128,128]{3,2,1,0:T(8,128)} %get-tuple-element.82), channel_id=1, source_target_pairs={{0,8},{8,0},{2,10},{10,2},{4,12},{12,4},{6,14},{14,6},{1,9},{9,1},... | collective-permute-start | bytes 2359304 | tf_op jit(solution)/shard_map/ppermute | solution.py:84
  161.8 32.5 %collective-permute-start.17 = (f32[4,3,128,128]{3,2,1,0:T(8,128)}, f32[4,3,128,128]{3,2,1,0:T(8,128)}, u32[]{:S(2)}, u32[]{:S(2)}) collective-permute-start(f32[4,3,128,128]{3,2,1,0:T(8,128)} %get-tuple-element.83), channel_id=1, source_target_pairs={{8,2},{2,8},{10,4},{4,10},{12,6},{6,12},{9,3},{3,9},{11,5},{5,11},... | collective-permute-start | bytes 2359304 | tf_op jit(solution)/shard_map/ppermute | solution.py:84
  165.0 14.6 %collective-permute-start.7 = (f32[2,3,128,128]{3,2,1,0:T(8,128)S(1)}, f32[2,3,128,128]{3,2,1,0:T(8,128)S(1)}, u32[]{:S(2)}, u32[]{:S(2)}) collective-permute-start(f32[2,3,128,128]{3,2,1,0:T(8,128)S(1)} %copy-done.54), channel_id=1, source_target_pairs={{8,2},{2,8},{10,4},{4,10},{12,6},{6,12},{9,3},{3,9},{11,5},{5,11},... | collective-permute-start | bytes 1179656 | tf_op jit(solution)/shard_map/ppermute | solution.py:84
  189.5 33.0 %all-to-all-start.4 = ((f32[8,2,2,32,128]{4,3,2,1,0:T(8,128)}), f32[8,2,2,32,128]{4,3,2,1,0:T(8,128)}, u32[]{:S(2)}, u32[]{:S(2)}) async-start(f32[8,2,2,32,128]{4,3,2,1,0:T(8,128)} %copy-done.35), calls=%async_computation.4 | async-start | bytes 1048576 | tf_op jit(solution)/shard_map/all_to_all | solution.py:423
  203.6 26.5 %collective-permute-start.18 = (f32[4,3,128,128]{3,2,1,0:T(8,128)}, f32[4,3,128,128]{3,2,1,0:T(8,128)}, u32[]{:S(2)}, u32[]{:S(2)}) collective-permute-start(f32[4,3,128,128]{3,2,1,0:T(8,128)} %get-tuple-element.85), channel_id=1, source_target_pairs={{0,8},{8,0},{2,10},{10,2},{4,12},{12,4},{6,14},{14,6},{1,9},{9,1},... | collective-permute-start | bytes 2359304 | tf_op jit(solution)/shard_map/ppermute | solution.py:84
  204.0 26.1 %collective-permute-start.19 = (f32[4,3,128,128]{3,2,1,0:T(8,128)}, f32[4,3,128,128]{3,2,1,0:T(8,128)}, u32[]{:S(2)}, u32[]{:S(2)}) collective-permute-start(f32[4,3,128,128]{3,2,1,0:T(8,128)} %get-tuple-element.86), channel_id=1, source_target_pairs={{8,2},{2,8},{10,4},{4,10},{12,6},{6,12},{9,3},{3,9},{11,5},{5,11},... | collective-permute-start | bytes 2359304 | tf_op jit(solution)/shard_map/ppermute | solution.py:84
  207.2 14.5 %collective-permute-start.9 = (f32[2,3,128,128]{3,2,1,0:T(8,128)S(1)}, f32[2,3,128,128]{3,2,1,0:T(8,128)S(1)}, u32[]{:S(2)}, u32[]{:S(2)}) collective-permute-start(f32[2,3,128,128]{3,2,1,0:T(8,128)S(1)} %copy-done.51), channel_id=1, source_target_pairs={{8,2},{2,8},{10,4},{4,10},{12,6},{6,12},{9,3},{3,9},{11,5},{5,11},... | collective-permute-start | bytes 1179656 | tf_op jit(solution)/shard_map/ppermute | solution.py:84
  229.4 14.9 %collective-permute-start.10 = (f32[1,4,128,128]{3,2,1,0:T(8,128)}, f32[1,4,128,128]{3,2,1,0:T(8,128)S(1)}, u32[]{:S(2)}, u32[]{:S(2)}) collective-permute-start(f32[1,4,128,128]{3,2,1,0:T(8,128)} %get-tuple-element.126), channel_id=1, source_target_pairs={{17,0},{25,8},{19,2},{27,10},{21,4},{29,12},{23,6},{31,14}} | collective-permute-start | bytes 786440 | tf_op jit(solution)/shard_map/ppermute | solution.py:84
  237.8 7.2 %collective-permute-start.20 = (f32[1,4,128,128]{3,2,1,0:T(8,128)}, f32[1,4,128,128]{3,2,1,0:T(8,128)}, u32[]{:S(2)}, u32[]{:S(2)}) collective-permute-start(f32[1,4,128,128]{3,2,1,0:T(8,128)} %get-tuple-element.124), channel_id=1, source_target_pairs={{17,1},{25,9},{19,3},{27,11},{21,5},{29,13},{23,7},{31,15}} | collective-permute-start | bytes 786440 | tf_op jit(solution)/shard_map/ppermute | solution.py:84
  239.2 11.2 %collective-permute-start.21 = (f32[1,4,128,128]{3,2,1,0:T(8,128)}, f32[1,4,128,128]{3,2,1,0:T(8,128)}, u32[]{:S(2)}, u32[]{:S(2)}) collective-permute-start(f32[1,4,128,128]{3,2,1,0:T(8,128)} %get-tuple-element.123), channel_id=1, source_target_pairs={{17,16},{25,24},{19,18},{27,26},{21,20},{29,28},{23,22},{31,30}} | collective-permute-start | bytes 786440 | tf_op jit(solution)/shard_map/ppermute | solution.py:84
  241.7 27.5 %collective-permute-start.24 = (f32[2,4,128,128]{3,2,1,0:T(8,128)}, f32[2,4,128,128]{3,2,1,0:T(8,128)S(1)}, u32[]{:S(2)}, u32[]{:S(2)}) collective-permute-start(f32[2,4,128,128]{3,2,1,0:T(8,128)} %get-tuple-element.122), channel_id=1, source_target_pairs={{0,1},{8,9},{2,3},{10,11},{4,5},{12,13},{6,7},{14,15},{17,16},{25,... | collective-permute-start | bytes 1572872 | tf_op jit(solution)/shard_map/ppermute | solution.py:84
  243.0 26.3 %collective-permute-start.25 = (f32[2,4,128,128]{3,2,1,0:T(8,128)}, f32[2,4,128,128]{3,2,1,0:T(8,128)}, u32[]{:S(2)}, u32[]{:S(2)}) collective-permute-start(f32[2,4,128,128]{3,2,1,0:T(8,128)} %get-tuple-element.121), channel_id=1, source_target_pairs={{17,1},{25,9},{19,3},{27,11},{21,5},{29,13},{23,7},{31,15},{0,16},... | collective-permute-start | bytes 1572872 | tf_op jit(solution)/shard_map/ppermute | solution.py:84
  257.8 29.8 %collective-permute-start.30 = (f32[2,4,128,128]{3,2,1,0:T(8,128)S(1)}, f32[2,4,128,128]{3,2,1,0:T(8,128)S(1)}, u32[]{:S(2)}, u32[]{:S(2)}) collective-permute-start(f32[2,4,128,128]{3,2,1,0:T(8,128)S(1)} %copy-done.13), channel_id=1, source_target_pairs={{1,0},{9,8},{3,2},{11,10},{5,4},{13,12},{7,6},{15,14}} | collective-permute-start | bytes 1572872 | tf_op jit(solution)/shard_map/ppermute | solution.py:84
  258.5 29.8 %collective-permute-start.31 = (f32[2,4,128,128]{3,2,1,0:T(8,128)}, f32[2,4,128,128]{3,2,1,0:T(8,128)S(1)}, u32[]{:S(2)}, u32[]{:S(2)}) collective-permute-start(f32[2,4,128,128]{3,2,1,0:T(8,128)} %get-tuple-element.120), channel_id=1, source_target_pairs={{16,1},{24,9},{18,3},{26,11},{20,5},{28,13},{22,7},{30,15},{1,16},... | collective-permute-start | bytes 1572872 | tf_op jit(solution)/shard_map/ppermute | solution.py:84
  260.4 7.5 %collective-permute-start.23 = (f32[3,128,128]{2,1,0:T(8,128)}, f32[3,128,128]{2,1,0:T(8,128)S(1)}, u32[]{:S(2)}, u32[]{:S(2)}) collective-permute-start(f32[3,128,128]{2,1,0:T(8,128)} %copy-done.59), channel_id=1, source_target_pairs={{8,2},{2,8},{10,4},{4,10},{12,6},{6,12},{9,3},{3,9},{11,5},{5,11},... | collective-permute-start | bytes 589832 | tf_op jit(solution)/shard_map/ppermute | solution.py:84
  267.9 40.9 %collective-permute-start.36 = (f32[2,4,128,128]{3,2,1,0:T(8,128)S(1)}, f32[2,4,128,128]{3,2,1,0:T(8,128)S(1)}, u32[]{:S(2)}, u32[]{:S(2)}) collective-permute-start(f32[2,4,128,128]{3,2,1,0:T(8,128)S(1)} %copy-done.13), channel_id=1, source_target_pairs={{16,0},{24,8},{18,2},{26,10},{20,4},{28,12},{22,6},{30,14}} | collective-permute-start | bytes 1572872 | tf_op jit(solution)/shard_map/ppermute | solution.py:84
  273.3 7.1 %collective-permute-start.27 = (f32[3,128,128]{2,1,0:T(8,128)S(1)}, f32[3,128,128]{2,1,0:T(8,128)S(1)}, u32[]{:S(2)}, u32[]{:S(2)}) collective-permute-start(f32[3,128,128]{2,1,0:T(8,128)S(1)} %get-tuple-element.93), channel_id=1, source_target_pairs={{8,2},{2,8},{10,4},{4,10},{12,6},{6,12},{9,3},{3,9},{11,5},{5,11},... | collective-permute-start | bytes 589832 | tf_op jit(solution)/shard_map/ppermute | solution.py:84
  284.4 7.0 %collective-permute-start.29 = (f32[3,128,128]{2,1,0:T(8,128)S(1)}, f32[3,128,128]{2,1,0:T(8,128)S(1)}, u32[]{:S(2)}, u32[]{:S(2)}) collective-permute-start(f32[3,128,128]{2,1,0:T(8,128)S(1)} %get-tuple-element.96), channel_id=1, source_target_pairs={{8,2},{2,8},{10,4},{4,10},{12,6},{6,12},{9,3},{3,9},{11,5},{5,11},... | collective-permute-start | bytes 589832 | tf_op jit(solution)/shard_map/ppermute | solution.py:84
  287.6 46.7 %collective-permute-start.42 = (f32[1,4,128,128]{3,2,1,0:T(8,128)S(1)}, f32[1,4,128,128]{3,2,1,0:T(8,128)S(1)}, u32[]{:S(2)}, u32[]{:S(2)}) collective-permute-start(f32[1,4,128,128]{3,2,1,0:T(8,128)S(1)} %copy-done.65), channel_id=1, source_target_pairs={{17,0},{25,8},{19,2},{27,10},{21,4},{29,12},{23,6},{31,14}} | collective-permute-start | bytes 786440 | tf_op jit(solution)/shard_map/ppermute | solution.py:84
  294.9 7.0 %collective-permute-start.33 = (f32[3,128,128]{2,1,0:T(8,128)S(1)}, f32[3,128,128]{2,1,0:T(8,128)S(1)}, u32[]{:S(2)}, u32[]{:S(2)}) collective-permute-start(f32[3,128,128]{2,1,0:T(8,128)S(1)} %get-tuple-element.99), channel_id=1, source_target_pairs={{8,2},{2,8},{10,4},{4,10},{12,6},{6,12},{9,3},{3,9},{11,5},{5,11},... | collective-permute-start | bytes 589832 | tf_op jit(solution)/shard_map/ppermute | solution.py:84
  316.1 7.0 %collective-permute-start.38 = (f32[3,128,128]{2,1,0:T(8,128)S(1)}, f32[3,128,128]{2,1,0:T(8,128)S(1)}, u32[]{:S(2)}, u32[]{:S(2)}) collective-permute-start(f32[3,128,128]{2,1,0:T(8,128)S(1)} %get-tuple-element.105), channel_id=1, source_target_pairs={{8,2},{2,8},{10,4},{4,10},{12,6},{6,12},{9,3},{3,9},{11,5},{5,11},... | collective-permute-start | bytes 589832 | tf_op jit(solution)/shard_map/ppermute | solution.py:84
  324.5 11.1 %collective-permute-start.40 = (f32[3,128,128]{2,1,0:T(8,128)S(1)}, f32[3,128,128]{2,1,0:T(8,128)S(1)}, u32[]{:S(2)}, u32[]{:S(2)}) collective-permute-start(f32[3,128,128]{2,1,0:T(8,128)S(1)} %get-tuple-element.107), channel_id=1, source_target_pairs={{0,8},{8,0},{2,10},{10,2},{4,12},{12,4},{6,14},{14,6},{1,9},{9,1},... | collective-permute-start | bytes 589832 | tf_op jit(solution)/shard_map/ppermute | solution.py:84
  327.1 29.2 %collective-permute-start.47 = (f32[2,4,128,128]{3,2,1,0:T(8,128)S(1)}, f32[2,4,128,128]{3,2,1,0:T(8,128)S(1)}, u32[]{:S(2)}, u32[]{:S(2)}) collective-permute-start(f32[2,4,128,128]{3,2,1,0:T(8,128)S(1)} %get-tuple-element.115), channel_id=1, source_target_pairs={{1,16},{9,17},{3,18},{11,19},{5,20},{13,21},{7,22},{15,23},{16,8},... | collective-permute-start | bytes 1572872 | tf_op jit(solution)/shard_map/ppermute | solution.py:84
  330.1 27.4 %collective-permute-start.46 = (f32[2,4,128,128]{3,2,1,0:T(8,128)S(1)}, f32[2,4,128,128]{3,2,1,0:T(8,128)S(1)}, u32[]{:S(2)}, u32[]{:S(2)}) collective-permute-start(f32[2,4,128,128]{3,2,1,0:T(8,128)S(1)} %get-tuple-element.116), channel_id=1, source_target_pairs={{0,16},{8,17},{2,18},{10,19},{4,20},{12,21},{6,22},{14,23},{16,0},... | collective-permute-start | bytes 1572872 | tf_op jit(solution)/shard_map/ppermute | solution.py:84
  333.6 25.2 %collective-permute-start.45 = (f32[2,4,128,128]{3,2,1,0:T(8,128)S(1)}, f32[2,4,128,128]{3,2,1,0:T(8,128)S(1)}, u32[]{:S(2)}, u32[]{:S(2)}) collective-permute-start(f32[2,4,128,128]{3,2,1,0:T(8,128)S(1)} %get-tuple-element.117), channel_id=1, source_target_pairs={{0,8},{8,9},{2,10},{10,11},{4,12},{12,13},{6,14},{14,15},{1,0},{9,... | collective-permute-start | bytes 1572872 | tf_op jit(solution)/shard_map/ppermute | solution.py:84
  334.3 26.5 %collective-permute-start.44 = (f32[2,4,128,128]{3,2,1,0:T(8,128)S(1)}, f32[2,4,128,128]{3,2,1,0:T(8,128)S(1)}, u32[]{:S(2)}, u32[]{:S(2)}) collective-permute-start(f32[2,4,128,128]{3,2,1,0:T(8,128)S(1)} %get-tuple-element.114), channel_id=1, source_target_pairs={{0,0},{8,1},{2,2},{10,3},{4,4},{12,5},{6,6},{14,7},{1,8},{9,9},{3,... | collective-permute-start | bytes 1572872 | tf_op jit(solution)/shard_map/ppermute | solution.py:84
  335.6 7.0 %collective-permute-start.41 = (f32[3,128,128]{2,1,0:T(8,128)S(1)}, f32[3,128,128]{2,1,0:T(8,128)S(1)}, u32[]{:S(2)}, u32[]{:S(2)}) collective-permute-start(f32[3,128,128]{2,1,0:T(8,128)S(1)} %get-tuple-element.108), channel_id=1, source_target_pairs={{8,2},{2,8},{10,4},{4,10},{12,6},{6,12},{9,3},{3,9},{11,5},{5,11},... | collective-permute-start | bytes 589832 | tf_op jit(solution)/shard_map/ppermute | solution.py:84
  342.6 10.2 %collective-permute-start.39 = (f32[4,128,128]{2,1,0:T(8,128)S(1)}, f32[4,128,128]{2,1,0:T(8,128)S(1)}, u32[]{:S(2)}, u32[]{:S(2)}) collective-permute-start(f32[4,128,128]{2,1,0:T(8,128)S(1)} %get-tuple-element.106.refs_1_), channel_id=1, source_target_pairs={{0,24},{8,25},{2,26},{10,27},{4,28},{12,29},{6,30},{14,31}} | collective-permute-start | bytes 786440 | tf_op jit(solution)/shard_map/ppermute | solution.py:84
  352.9 11.4 %collective-permute-start.50 = (f32[4,128,128]{2,1,0:T(8,128)S(1)}, f32[4,128,128]{2,1,0:T(8,128)S(1)}, u32[]{:S(2)}, u32[]{:S(2)}) collective-permute-start(f32[4,128,128]{2,1,0:T(8,128)S(1)} %get-tuple-element.106.refs_1_), channel_id=1, source_target_pairs={{16,24},{24,25},{18,26},{26,27},{20,28},{28,29},{22,30},{30,31}} | collective-permute-start | bytes 786440 | tf_op jit(solution)/shard_map/ppermute | solution.py:84
  356.2 9.9 %collective-permute-start.48 = (f32[4,128,128]{2,1,0:T(8,128)S(1)}, f32[4,128,128]{2,1,0:T(8,128)S(1)}, u32[]{:S(2)}, u32[]{:S(2)}) collective-permute-start(f32[4,128,128]{2,1,0:T(8,128)S(1)} %get-tuple-element.106.refs_1_), channel_id=1, source_target_pairs={{1,24},{9,25},{3,26},{11,27},{5,28},{13,29},{7,30},{15,31}} | collective-permute-start | bytes 786440 | tf_op jit(solution)/shard_map/ppermute | solution.py:84
  357.5 9.0 %collective-permute-start.43 = (f32[4,128,128]{2,1,0:T(8,128)S(1)}, f32[4,128,128]{2,1,0:T(8,128)S(1)}, u32[]{:S(2)}, u32[]{:S(2)}) collective-permute-start(f32[4,128,128]{2,1,0:T(8,128)S(1)} %shard_map.73), channel_id=1, source_target_pairs={{0,24},{8,25},{2,26},{10,27},{4,28},{12,29},{6,30},{14,31}} | collective-permute-start | bytes 786440 | tf_op jit(solution)/shard_map/ppermute | solution.py:84
  358.9 7.7 %collective-permute-start.51 = (f32[4,128,128]{2,1,0:T(8,128)S(1)}, f32[4,128,128]{2,1,0:T(8,128)S(1)}, u32[]{:S(2)}, u32[]{:S(2)}) collective-permute-start(f32[4,128,128]{2,1,0:T(8,128)S(1)} %shard_map.73), channel_id=1, source_target_pairs={{16,24},{24,25},{18,26},{26,27},{20,28},{28,29},{22,30},{30,31}} | collective-permute-start | bytes 786440 | tf_op jit(solution)/shard_map/ppermute | solution.py:84
  361.6 9.3 %collective-permute-start.49 = (f32[4,128,128]{2,1,0:T(8,128)S(1)}, f32[4,128,128]{2,1,0:T(8,128)S(1)}, u32[]{:S(2)}, u32[]{:S(2)}) collective-permute-start(f32[4,128,128]{2,1,0:T(8,128)S(1)} %shard_map.73), channel_id=1, source_target_pairs={{1,24},{9,25},{3,26},{11,27},{5,28},{13,29},{7,30},{15,31}} | collective-permute-start | bytes 786440 | tf_op jit(solution)/shard_map/ppermute | solution.py:84
  (79 other events, 497.8 us)
